TPU v7x, 256 devices: a whole 4x4x8 slice. The times are simulated.
256 devices in a mesh: seq: 64 (over y, x, z_hi, core), fsdp: 4 (over z_lo).
Axes of the slice: x: 4, y: 4, z: 8 (z_hi: 2, z_lo: 4; z = z_hi * 4 + z_lo), core: 2. Of those that a mesh axis runs over, the one named last changes fastest.
Arguments:
- tokens: bfloat16 [40960, 5120], P('seq', 'fsdp'), may hold values from -24 to 24
- w_local: bfloat16 [5120, 3, 1536], P('seq', None, 'fsdp'), may hold values from -0.078125 to 0.078125
- w_strided: bfloat16 [5120, 3, 1024], P('seq', None, 'fsdp'), may hold values from -0.078125 to 0.078125
- valid: int32 [64, 640], P('seq'), may hold values 0 or 1
- band_reach: int32 [12], P('fsdp'), may hold values from 1 to 4, as said below
Outputs:
- out_local: bfloat16 [40960, 1536], P('seq', 'fsdp')
- out_strided: bfloat16 [40960, 1024], P('seq', 'fsdp')
Inputs may be any that keep to these rules, and one draw needn't show every extreme that they name: Query block b of local head h sees band blocks b - band_reach[h] to b.
All inputs are finite; a program needn't handle non-finite values. No bound on the sum of `valid` on one device may be relied on, other than what follows from the above.
Results may differ from a plain program's by a relative error of at most 0.012.
The roundings to bfloat16 on the way count: a program that leaves them out, or rounds other values in their place, can miss the bound.
Values may be sent and summed in bfloat16 or wider, within the bound.
No kernel may reach another device: no remote copies, remote signals or barrier semaphores. Data moves between devices by JAX's collectives and lax.ppermute only.
A program may use at most 128 MiB of HBM per device.

v0:
```python
import math

import jax
import jax.numpy as jnp
from jax import lax
from jax.sharding import PartitionSpec as P

HD = 128
BLK = 128


def local_attend(qkv_day, valid_day, reach, head_size):
    query = qkv_day[:, 0]
    keys = qkv_day[:, 1]
    values = qkv_day[:, 2]
    seconds = qkv_day.shape[0]
    scores = jnp.einsum(
        "qhc,khc->hqk", query, keys, preferred_element_type=jnp.float32
    ) / math.sqrt(head_size)
    position = jnp.arange(seconds)
    causal = position[None, :] <= position[:, None]
    block = position // BLK
    band = block[None, None, :] >= block[None, :, None] - reach[:, None, None]
    seen = (valid_day[None, :] > 0) | (position[None, :] == position[:, None])
    allowed = causal[None] & band & seen[None]
    scores = jnp.where(allowed, scores, -jnp.inf)
    row_max = jnp.max(scores, axis=-1, keepdims=True)
    expo = jnp.exp(scores - row_max)
    probs = (expo / jnp.sum(expo, axis=-1, keepdims=True)).astype(jnp.bfloat16)
    result = jnp.einsum("hqk,khc->qhc", probs, values, preferred_element_type=jnp.float32)
    return result.astype(jnp.bfloat16).reshape(seconds, -1)


def body(tokens, w_local, w_strided, valid, band_reach):
    gathered = lax.all_gather(tokens, "fsdp", axis=1, tiled=True)
    seconds = gathered.shape[0]
    local_cols = w_local.shape[2]
    strided_cols = w_strided.shape[2]
    head_size = HD
    peers = lax.axis_size("seq")
    per_peer = seconds // peers

    def add_rows(piece):
        rows = piece.shape[0]
        return jnp.dot(gathered, piece.reshape(rows, -1), preferred_element_type=jnp.float32)

    acc_local = add_rows(lax.all_gather(w_local, "seq", axis=0, tiled=True))
    acc_strided = add_rows(lax.all_gather(w_strided, "seq", axis=0, tiled=True))
    packed = acc_strided.astype(jnp.bfloat16).reshape(1, peers, per_peer, 3 * strided_cols)
    marks = valid.astype(jnp.bfloat16).reshape(1, peers, per_peer)
    strided_packed = lax.all_to_all(packed, "seq", split_axis=1, concat_axis=0, tiled=True)
    strided_marks = lax.all_to_all(marks, "seq", split_axis=1, concat_axis=0, tiled=True)
    days = strided_packed.shape[0]
    count = strided_packed.shape[2]
    heads = strided_cols // head_size
    split_up = strided_packed.reshape(days, count, 3, heads, head_size)
    query = split_up[:, :, 0]
    keys = split_up[:, :, 1]
    values = split_up[:, :, 2]
    scores = jnp.einsum(
        "dshc,eshc->shde", query, keys, preferred_element_type=jnp.float32
    ) / math.sqrt(head_size)
    day = jnp.arange(days)
    causal = day[None, :] <= day[:, None]
    same = day[None, :] == day[:, None]
    seen = jnp.transpose(strided_marks[:, 0, :]) > 0
    allowed = causal[None, None] & (seen[:, None, None, :] | same[None, None])
    scores = jnp.where(allowed, scores, -jnp.inf)
    row_max = jnp.max(scores, axis=-1, keepdims=True)
    expo = jnp.exp(scores - row_max)
    probs = (expo / jnp.sum(expo, axis=-1, keepdims=True)).astype(jnp.bfloat16)
    result = jnp.einsum("shde,eshc->dshc", probs, values, preferred_element_type=jnp.float32)
    result = result.astype(jnp.bfloat16).reshape(days, 1, count, strided_cols)
    result = lax.all_to_all(result, "seq", split_axis=0, concat_axis=1, tiled=True)
    out_strided = result.reshape(seconds, strided_cols)
    qkv_local = acc_local.astype(jnp.bfloat16).reshape(
        seconds, 3, local_cols // head_size, head_size
    )
    out_local = local_attend(qkv_local, valid[0], band_reach, head_size)
    return (out_local, out_strided)


def solution(mesh):
    in_specs = (
        P("seq", "fsdp"),
        P("seq", None, "fsdp"),
        P("seq", None, "fsdp"),
        P("seq", None),
        P("fsdp"),
    )
    out_specs = (P("seq", "fsdp"), P("seq", "fsdp"))
    return jax.shard_map(body, mesh=mesh, in_specs=in_specs, out_specs=out_specs, check_vma=False)
```

profile of v0, /device:TPU:1, one launch (start us, length us, event | category | flops | bytes accessed | tf_op | source)
XLA Modules:
  0.0 441.7 jit_solution(410772100073191428)
XLA Ops:
  7.2 0.0 all-gather.8.cloned.1.call-start
  7.2 0.7 all-gather.8.cloned.1.call-update
  7.9 0.0 all-gather.4.cloned.1.call-start
  7.9 0.7 all-gather.4.cloned.1.call-update
  8.6 0.0 all-gather.6.cloned.1.call-start
  8.7 0.7 all-gather.6.cloned.1.call-update
  9.4 0.7 convert_reduce_fusion
  10.1 0.8 reshape.195
  10.9 15.6 %all-to-all-start.1 = ((bf16[1,64,10]{2,0,1:T(2,128)(2,1)}), bf16[1,64,10]{2,0,1:T(2,128)(2,1)S(1)}, u32[]{:S(2)}, u32[]{:S(2)}) async-start(bf16[1,64,10]{2,0,1:T(2,128)(2,1)} %reshape.195), calls=%async_computation.1 | async-start | bytes 65536 | tf_op jit(solution)/shard_map/all_to_all | solution.py:52
  26.5 100.5 %all-gather.8.cloned.1.call-done = bf16[5120,3,256]{2,0,1:T(8,128)(2,1)} async-done(((bf16[80,3,256]{2,0,1:T(8,128)(2,1)}), bf16[5120,3,256]{2,0,1:T(8,128)(2,1)}) %all-gather.8.cloned.1.call-update) | async-done | bytes 7864336 | tf_op jit(solution)/shard_map/all_gather | solution.py:48
  127.0 11.0 %copy.51 = bf16[5120,3,256]{0,2,1:T(8,128)(2,1)} copy(bf16[5120,3,256]{2,0,1:T(8,128)(2,1)} %all-gather.8.cloned.1.call-done) | data formatting | bytes 15728640 | tf_op jit(solution)/shard_map/all_gather | solution.py:48
  138.0 107.3 %all-gather.4.cloned.1.call-done = bf16[640,5120]{1,0:T(8,128)(2,1)} async-done(((bf16[640,1280]{1,0:T(8,128)(2,1)}), bf16[640,5120]{1,0:T(8,128)(2,1)}) %all-gather.4.cloned.1.call-update) | async-done | bytes 6553616 | tf_op jit(solution)/shard_map/all_gather | solution.py:35
  245.3 9.7 %convolution_convert_fusion.1 = bf16[640,768]{1,0:T(8,128)(2,1)S(1)} fusion(bf16[640,5120]{1,0:T(8,128)(2,1)} %all-gather.4.cloned.1.call-done, bf16[5120,768]{0,1:T(8,128)(2,1)} %bitcast.60), kind=kOutput, calls=%fused_computation.17 | convolution fusion | flops 5033656320 | bytes 15400960 | tf_op jit(solution)/shard_map/dot_general | solution.py:45
  255.0 0.0 copy-start
  255.0 1.4 reshape.189
  256.4 0.0 all-to-all-done.1
  256.4 11.4 %all-to-all-start = ((bf16[1,64,10,768]{3,2,0,1:T(8,128)(2,1)}), bf16[1,64,10,768]{3,2,0,1:T(8,128)(2,1)S(1)}, u32[]{:S(2)}, u32[]{:S(2)}) async-start(bf16[1,64,10,768]{3,2,0,1:T(8,128)(2,1)} %bitcast.8), calls=%async_computation | async-start | bytes 3145728 | tf_op jit(solution)/shard_map/all_to_all | solution.py:51
  267.9 0.0 copy-done
  267.9 0.1 copy.56
  268.0 0.2 or_and_fusion
  268.2 37.1 %all-to-all-done = bf16[1,64,10,768]{3,2,0,1:T(8,128)(2,1)S(1)} async-done(((bf16[1,64,10,768]{3,2,0,1:T(8,128)(2,1)}), bf16[1,64,10,768]{3,2,0,1:T(8,128)(2,1)S(1)}, u32[]{:S(2)}, u32[]{:S(2)}) %all-to-all-start) | async-done | bytes 983072 | tf_op jit(solution)/shard_map/all_to_all | solution.py:51
  305.3 0.6 reshape.194
  305.9 0.0 copy-start.1
  305.9 0.7 fusion.30
  306.6 0.3 fusion.14
  306.9 0.2 fusion.32
  307.1 0.3 fusion.15
  307.4 0.3 copy.69
  307.8 1.0 reshape.196
  308.8 4.4 all-to-all-start.2
  313.2 0.1 iota_compare_fusion.1
  313.3 0.0 copy-done.1
  313.3 0.1 broadcast_subtract_fusion
  313.4 0.9 fusion.10
  314.3 14.2 %all-to-all-done.2 = bf16[64,1,10,256]{3,2,1,0:T(8,128)(2,1)S(1)} async-done(((bf16[64,1,10,256]{3,2,1,0:T(8,128)(2,1)}), bf16[64,1,10,256]{3,2,1,0:T(8,128)(2,1)S(1)}, u32[]{:S(2)}, u32[]{:S(2)}) %all-to-all-start.2) | async-done | bytes 327712 | tf_op jit(solution)/shard_map/all_to_all | solution.py:74
  328.5 0.8 reshape.193
  329.4 68.7 %all-gather.6.cloned.1.call-done = bf16[5120,3,384]{2,0,1:T(8,128)(2,1)} async-done(((bf16[80,3,384]{2,0,1:T(8,128)(2,1)}), bf16[5120,3,384]{2,0,1:T(8,128)(2,1)}) %all-gather.6.cloned.1.call-update) | async-done | bytes 11796496 | tf_op jit(solution)/shard_map/all_gather | solution.py:47
  398.1 15.0 %copy.46 = bf16[5120,3,384]{0,2,1:T(8,128)(2,1)} copy(bf16[5120,3,384]{2,0,1:T(8,128)(2,1)} %all-gather.6.cloned.1.call-done) | data formatting | bytes 23592960 | tf_op jit(solution)/shard_map/all_gather | solution.py:47
  413.1 12.7 %convolution_convert_fusion = bf16[640,1152]{1,0:T(8,128)(2,1)S(1)} fusion(bf16[640,5120]{1,0:T(8,128)(2,1)} %all-gather.4.cloned.1.call-done, bf16[5120,1152]{0,1:T(8,128)(2,1)} %bitcast.59), kind=kOutput, calls=%fused_computation.5 | convolution fusion | flops 7550484480 | bytes 19824640 | tf_op jit(solution)/shard_map/dot_general | solution.py:45
  425.8 0.9 copy.47
  426.7 3.5 fusion.31
  430.2 4.0 fusion.12
  434.2 1.0 copy.62
  (4 shorter events, 0.1 us)
Async XLA Ops:
  7.2 119.8 %all-gather.8.cloned.1.call-start = ((), (), s32[]{:S(2)}) async-start(), calls=%async_computation.5 | async-start | bytes 7987200 | tf_op jit(solution)/shard_map/all_gather | solution.py:48
  7.9 237.4 %all-gather.4.cloned.1.call-start = ((), (), s32[]{:S(2)}) async-start(), calls=%async_computation.3 | async-start | bytes 8192000 | tf_op jit(solution)/shard_map/all_gather | solution.py:35
  8.6 389.4 %all-gather.6.cloned.1.call-start = ((), (), s32[]{:S(2)}) async-start(), calls=%async_computation.4 | async-start | bytes 11980800 | tf_op jit(solution)/shard_map/all_gather | solution.py:47
  10.9 245.6 %all-to-all-start.1 = ((bf16[1,64,10]{2,0,1:T(2,128)(2,1)}), bf16[1,64,10]{2,0,1:T(2,128)(2,1)S(1)}, u32[]{:S(2)}, u32[]{:S(2)}) async-start(bf16[1,64,10]{2,0,1:T(2,128)(2,1)} %reshape.195), calls=%async_computation.1 | async-start | bytes 65536 | tf_op jit(solution)/shard_map/all_to_all | solution.py:52
  255.0 12.9 %copy-start = (s32[1,640]{1,0:T(1,128)S(1)}, s32[1,640]{1,0:T(1,128)}, u32[]{:S(2)}) copy-start(s32[1,640]{1,0:T(1,128)} %param.8) | copy-start | bytes 7684
  256.4 48.9 %all-to-all-start = ((bf16[1,64,10,768]{3,2,0,1:T(8,128)(2,1)}), bf16[1,64,10,768]{3,2,0,1:T(8,128)(2,1)S(1)}, u32[]{:S(2)}, u32[]{:S(2)}) async-start(bf16[1,64,10,768]{3,2,0,1:T(8,128)(2,1)} %bitcast.8), calls=%async_computation | async-start | bytes 3145728 | tf_op jit(solution)/shard_map/all_to_all | solution.py:51
  305.9 7.4 %copy-start.1 = (s32[3]{0:T(128)S(1)}, s32[3]{0:T(128)}, u32[]{:S(2)}) copy-start(s32[3]{0:T(128)} %param.9) | copy-start | bytes 40
  308.8 19.7 %all-to-all-start.2 = ((bf16[64,1,10,256]{3,2,1,0:T(8,128)(2,1)}), bf16[64,1,10,256]{3,2,1,0:T(8,128)(2,1)S(1)}, u32[]{:S(2)}, u32[]{:S(2)}) async-start(bf16[64,1,10,256]{3,2,1,0:T(8,128)(2,1)} %reshape.196), calls=%async_computation.2 | async-start | bytes 1048576 | tf_op jit(solution)/shard_map/all_to_all | solution.py:74
Sparse Core Ops, SparseCore 0:
  11.5 115.4 all-gather.7
  128.8 116.4 all-gather.3
  248.8 149.2 all-gather.5
where the time goes:
time: 443 us; the launch traced here: 442 us
  waiting for transfers between devices  330 us (74%)
  local copies, waits for them, and re-layouts  33.7 us (8%)
  starting transfers between devices  31.5 us (7%)
  matrix products  30.5 us (7%)
  between operations  13.9 us (3%)
    all_gather x1, waiting for transfers between devices, body(): gathered = lax.all_gather(tokens, 'fsdp', axis=1, tiled=True)  107 us
    all_gather x1, waiting for transfers between devices, body(): acc_strided = add_rows(lax.all_gather(w_strided, 'seq', axis=0, tiled=True))  101 us
    all_gather x1, waiting for transfers between devices, body(): acc_local = add_rows(lax.all_gather(w_local, 'seq', axis=0, tiled=True))  68.7 us
    all_to_all x1, waiting for transfers between devices, body(): lax.all_to_all(packed, 'seq', split_axis=1, concat_axis=0, tiled=True)  37.1 us
    dot_general x2, matrix products, add_rows(): jnp.dot(gathered, piece.reshape(rows, -1), preferred_element_type=jnp.flo...  22.4 us
    all_to_all x1, starting transfers between devices, body(): lax.all_to_all(marks, 'seq', split_axis=1, concat_axis=0, tiled=True)  15.6 us
    all_gather x1, local copies, waits for them, and re-layouts, body(): acc_local = add_rows(lax.all_gather(w_local, 'seq', axis=0, tiled=True))  15 us
    all_to_all x1, waiting for transfers between devices, body(): lax.all_to_all(result, 'seq', split_axis=0, concat_axis=1, tiled=True)  14.2 us
  transfers between devices with their start and end apart: 6, of which 5 were waited for; matrix products, arithmetic and copies ran while one was open for 7% of the time, Pallas kernels for 0%

commit v1 on v0

v1 whole, which is shorter than its diff:
```python
import functools
import math

import jax
import jax.numpy as jnp
from jax import lax
from jax.experimental import pallas as pl
from jax.experimental.pallas import tpu as pltpu
from jax.sharding import PartitionSpec as P

HD = 128
BLK = 128
NY, NX, NH, NC = 4, 4, 2, 2
CHUNKS = (320, 320)


def seq_pairs(move):
    pairs = []
    for y in range(NY):
        for x in range(NX):
            for h in range(NH):
                for c in range(NC):
                    ty, tx, th, tc = move(y, x, h, c)
                    pairs.append(
                        (((y * NX + x) * NH + h) * NC + c, ((ty * NX + tx) * NH + th) * NC + tc)
                    )
    return pairs


MOVES = {
    "x1": lambda y, x, h, c: (y, x ^ 1, h, c),
    "x3": lambda y, x, h, c: (y, x ^ 3, h, c),
    "y1": lambda y, x, h, c: (y ^ 1, x, h, c),
    "y3": lambda y, x, h, c: (y ^ 3, x, h, c),
    "h": lambda y, x, h, c: (y, x, 1 - h, c),
    "c": lambda y, x, h, c: (y, x, h, 1 - c),
}
FLIPS = {"x1": (0, 1), "x3": (0, 3), "y1": (1, 0), "y3": (3, 0)}
OWN_ORDERS = (("x1", "x3", "y1", "y3"), ("y1", "y3", "x1", "x3"))
OTHER_ORDERS = (("x3", "y1", "y3", "x1"), ("y3", "x1", "x3", "y1"))


def swap(value, kind):
    return lax.ppermute(value, "seq", seq_pairs(MOVES[kind]))


def double_up(value, order):
    value = value[None]
    for kind in order[:-1]:
        value = jnp.concatenate([value, swap(value, kind)], axis=0)
    received = swap(value, order[-1])
    return [value, received]


def place_kernel(orders, place, *refs):
    pieces = refs[:8]
    out, sem = refs[8:]
    y, x, h, c = (place[i] for i in range(4))
    count, _, part, _ = pieces[0].shape
    for group in range(2):
        half = h if group == 0 else 1 - h
        for last in range(2):
            for side in range(2):
                core = c if side == 0 else 1 - c
                ref = pieces[(group * 2 + last) * 2 + side]
                for k in range(count):
                    flip_y, flip_x = 0, 0
                    for bit, kind in enumerate(orders[group]):
                        if (k + last * count) >> bit & 1:
                            flip_y, flip_x = flip_y ^ FLIPS[kind][0], flip_x ^ FLIPS[kind][1]
                    block = (((y ^ flip_y) * NX + (x ^ flip_x)) * NH + half) * NC + core
                    rows = pl.ds(pl.multiple_of(block * part, 16), part)
                    pltpu.make_async_copy(ref.at[k], out.at[:, rows, :], sem).start()
    pltpu.make_async_copy(out, out, sem).wait()


def place_weights(place, own, other, which):
    pieces = []
    for value, order in ((own, OWN_ORDERS[which]), (other, OTHER_ORDERS[which])):
        for piece in double_up(value, order):
            pieces += [piece, swap(piece, "c")]
    part, cols = own.shape[1:]
    total = NY * NX * NH * NC * part
    return pl.pallas_call(
        functools.partial(place_kernel, (OWN_ORDERS[which], OTHER_ORDERS[which])),
        out_shape=jax.ShapeDtypeStruct((3, total, cols), jnp.bfloat16),
        in_specs=[pl.BlockSpec(memory_space=pltpu.SMEM)]
        + [pl.BlockSpec(memory_space=pltpu.HBM)] * 8,
        out_specs=pl.BlockSpec(memory_space=pltpu.VMEM),
        scratch_shapes=[pltpu.SemaphoreType.DMA],
        compiler_params=pltpu.CompilerParams(vmem_limit_bytes=16 * 1024 * 1024),
        cost_estimate=pl.CostEstimate(
            flops=0, bytes_accessed=4 * 3 * total * cols, transcendentals=0
        ),
    )(place, *pieces)


def project_kernel(tokens, weight, out):
    out[0] = jnp.dot(
        tokens[...], weight[0], preferred_element_type=jnp.float32
    ).astype(out.dtype)


def project(tokens, weight):
    rows, total = tokens.shape
    cols = weight.shape[2]
    return pl.pallas_call(
        project_kernel,
        grid=(3,),
        out_shape=jax.ShapeDtypeStruct((3, rows, cols), jnp.bfloat16),
        in_specs=[
            pl.BlockSpec((rows, total), lambda j: (0, 0)),
            pl.BlockSpec((1, total, cols), lambda j: (j, 0, 0)),
        ],
        out_specs=pl.BlockSpec((1, rows, cols), lambda j: (j, 0, 0)),
        compiler_params=pltpu.CompilerParams(vmem_limit_bytes=40 * 1024 * 1024),
        cost_estimate=pl.CostEstimate(
            flops=2 * rows * total * 3 * cols,
            bytes_accessed=2 * (rows * total + 3 * total * cols + 3 * rows * cols),
            transcendentals=0,
        ),
    )(tokens, weight)


def local_attend(qkv, valid_day, reach):
    query, keys, values = qkv[0], qkv[1], qkv[2]
    seconds = query.shape[0]
    query = query.reshape(seconds, -1, HD)
    keys = keys.reshape(seconds, -1, HD)
    values = values.reshape(seconds, -1, HD)
    scores = jnp.einsum(
        "qhc,khc->hqk", query, keys, preferred_element_type=jnp.float32
    ) / math.sqrt(HD)
    position = jnp.arange(seconds)
    causal = position[None, :] <= position[:, None]
    block = position // BLK
    band = block[None, None, :] >= block[None, :, None] - reach[:, None, None]
    seen = (valid_day[None, :] > 0) | (position[None, :] == position[:, None])
    allowed = causal[None] & band & seen[None]
    scores = jnp.where(allowed, scores, -jnp.inf)
    row_max = jnp.max(scores, axis=-1, keepdims=True)
    expo = jnp.exp(scores - row_max)
    probs = (expo / jnp.sum(expo, axis=-1, keepdims=True)).astype(jnp.bfloat16)
    result = jnp.einsum("hqk,khc->qhc", probs, values, preferred_element_type=jnp.float32)
    return result.astype(jnp.bfloat16).reshape(seconds, -1)


def strided_attend(qkv, marks):
    rows, cols = qkv.shape[1:]
    peers = NY * NX * NH * NC
    count = rows // peers
    heads = cols // HD
    packed = qkv.reshape(3, peers, count, heads, HD).transpose(1, 0, 3, 2, 4)
    packed = packed.reshape(peers, 3 * heads * count, HD)
    flags = marks.astype(jnp.bfloat16).reshape(peers, 1, count)
    flags = jnp.pad(flags, ((0, 0), (0, 0), (0, HD - count)))
    packed = jnp.concatenate([packed, flags], axis=1)
    packed = lax.all_to_all(packed, "seq", split_axis=0, concat_axis=0, tiled=True)
    days = packed.shape[0]
    split_up = packed[:, :-1].reshape(days, 3, heads, count, HD)
    query, keys, values = split_up[:, 0], split_up[:, 1], split_up[:, 2]
    scores = jnp.einsum(
        "dhsc,ehsc->hsde", query, keys, preferred_element_type=jnp.float32
    ) / math.sqrt(HD)
    day = jnp.arange(days)
    causal = day[None, :] <= day[:, None]
    same = day[None, :] == day[:, None]
    seen = jnp.transpose(packed[:, -1, :count]) > 0
    allowed = causal[None] & (seen[:, None, :] | same[None])
    scores = jnp.where(allowed[None], scores, -jnp.inf)
    row_max = jnp.max(scores, axis=-1, keepdims=True)
    expo = jnp.exp(scores - row_max)
    probs = (expo / jnp.sum(expo, axis=-1, keepdims=True)).astype(jnp.bfloat16)
    result = jnp.einsum("hsde,ehsc->dhsc", probs, values, preferred_element_type=jnp.float32)
    result = result.astype(jnp.bfloat16).reshape(days, heads * count, HD)
    result = lax.all_to_all(result, "seq", split_axis=0, concat_axis=0, tiled=True)
    result = result.reshape(peers, heads, count, HD).transpose(0, 2, 1, 3)
    return result.reshape(rows, cols)


def body(tokens, w_local, w_strided, valid, band_reach):
    seq = lax.axis_index("seq")
    place = jnp.stack(
        [
            seq // (NX * NH * NC),
            seq // (NH * NC) % NX,
            seq // NC % NH,
            seq % NC,
            lax.axis_index("fsdp"),
        ]
    ).astype(jnp.int32)
    own_strided = jnp.transpose(w_strided, (1, 0, 2))
    own_local = jnp.transpose(w_local, (1, 0, 2))
    other_strided = swap(own_strided, "h")
    other_local = swap(own_local, "h")
    tokens, other_strided, other_local = lax.optimization_barrier(
        (tokens, other_strided, other_local)
    )
    weight_strided = place_weights(place, own_strided, other_strided, 0)
    weight_local = place_weights(place, own_local, other_local, 1)
    out_strided, qkv_local = [], []
    start = 0
    for size in CHUNKS:
        rows = slice(start, start + size)
        gathered = lax.all_gather(tokens[rows], "fsdp", axis=1, tiled=True)
        qkv = project(gathered, weight_strided)
        out_strided.append(strided_attend(qkv, valid[0, rows]))
        qkv_local.append(project(gathered, weight_local))
        start += size
    out_strided = jnp.concatenate(out_strided, axis=0)
    qkv_local = jnp.concatenate(qkv_local, axis=1)
    out_local = local_attend(qkv_local, valid[0], band_reach)
    return (out_local, out_strided)


def solution(mesh):
    in_specs = (
        P("seq", "fsdp"),
        P("seq", None, "fsdp"),
        P("seq", None, "fsdp"),
        P("seq", None),
        P("fsdp"),
    )
    out_specs = (P("seq", "fsdp"), P("seq", "fsdp"))
    return jax.shard_map(body, mesh=mesh, in_specs=in_specs, out_specs=out_specs, check_vma=False)
```

time: 443 us -> 294 us (0.66)
  waiting for transfers between devices: 330 us -> 96.3 us
  starting transfers between devices: 31.5 us -> 96.9 us
  Pallas kernels: 0 us -> 31.4 us
  matrix products: 30.5 us -> 8.61 us
  local copies, waits for them, and re-layouts: 33.7 us -> 40.1 us
    all_gather x3 -> x2, waiting for transfers between devices: 277 us -> 47.3 us  [body(): gathered = lax.all_gather(tokens[rows], 'fsdp', axis=1, tiled=True)]
    ppermute x0 -> x26, starting transfers between devices: none -> 54 us  [swap(): return lax.ppermute(value, 'seq', seq_pairs(MOVES[kind]))]
    all_to_all x3 -> x4, waiting for transfers between devices: 51.3 us -> 15.6 us  [the longest x2 15.6 us: strided_attend(): lax.all_to_all(result, 'seq', split_axis=0, concat_axis=0, tiled=True)]
    ppermute x0 -> x26, waiting for transfers between devices: none -> 32.7 us  [swap(): return lax.ppermute(value, 'seq', seq_pairs(MOVES[kind]))]
    pallas_call x0 -> x6, Pallas kernels: none -> 31.4 us  [the longest x4 22.2 us: project(): pl.pallas_call(project_kernel, grid=(3,), out_shape=jax.ShapeDtypeStruct(...]
    all_gather x2 -> x0, local copies, waits for them, and re-layouts: 26 us -> none  [the longest x1 15 us: body(): acc_local = add_rows(lax.all_gather(w_local, 'seq', axis=0, tiled=True))]
    unnamed x5 -> x43, local copies, waits for them, and re-layouts: 1.01 us -> 23.3 us
    dot_general x4, matrix products: 23.1 us -> 2.17 us  [the longest x2 1.74 us: strided_attend(): jnp.einsum('hsde,ehsc->dhsc', probs, values, preferred_element_type=jnp.f...]
  transfers between devices with their start and end apart: 6 -> 32, of which waited for: 5 -> 13; matrix products, arithmetic and copies ran while one was open for 7% -> 8% of each run, Pallas kernels for 0% -> 11%
where the time goes in v1:
time: 294 us; the launch traced here: 292 us
  starting transfers between devices  96.9 us (33%)
  waiting for transfers between devices  96.3 us (33%)
  local copies, waits for them, and re-layouts  40.1 us (14%)
  Pallas kernels  31.4 us (11%)
  between operations  14.6 us (5%)
  matrix products  8.61 us (3%)
  other arithmetic  4.56 us (2%)
    ppermute x26, starting transfers between devices, swap(): return lax.ppermute(value, 'seq', seq_pairs(MOVES[kind]))  54 us
    all_gather x2, waiting for transfers between devices, body(): gathered = lax.all_gather(tokens[rows], 'fsdp', axis=1, tiled=True)  47.3 us
    ppermute x26, waiting for transfers between devices, swap(): return lax.ppermute(value, 'seq', seq_pairs(MOVES[kind]))  32.7 us
    all_to_all x2, starting transfers between devices, strided_attend(): lax.all_to_all(packed, 'seq', split_axis=0, concat_axis=0, tiled=True)  25.5 us
    unnamed x43, local copies, waits for them, and re-layouts  23.3 us
    pallas_call x4, Pallas kernels, project(): pl.pallas_call(project_kernel, grid=(3,), out_shape=jax.ShapeDtypeStruct(...  22.2 us
    all_to_all x2, starting transfers between devices, strided_attend(): lax.all_to_all(result, 'seq', split_axis=0, concat_axis=0, tiled=True)  17.3 us
    all_to_all x2, waiting for transfers between devices, strided_attend(): lax.all_to_all(result, 'seq', split_axis=0, concat_axis=0, tiled=True)  15.6 us
  transfers between devices with their start and end apart: 32, of which 13 were waited for; matrix products, arithmetic and copies ran while one was open for 8% of the time, Pallas kernels for 11%

profile of v1, /device:TPU:1, one launch (start us, length us, event | category | flops | bytes accessed | tf_op | source)
XLA Modules:
  0.0 292.4 jit_solution(10979358047001122989)
XLA Ops:
  7.2 7.8 %collective-permute-start.1 = (bf16[3,80,384]{2,1,0:T(8,128)(2,1)}, bf16[3,80,384]{2,1,0:T(8,128)(2,1)S(1)}, u32[]{:S(2)}, u32[]{:S(2)}) collective-permute-start(bf16[3,80,384]{2,1,0:T(8,128)(2,1)} %bitcast.88), channel_id=1, source_target_pairs={{0,8},{4,12},{8,0},{12,4},{16,24},{20,28},{24,16},{28,20},{32,40},... | collective-permute-start | bytes 552968 | tf_op jit(solution)/shard_map/ppermute | solution.py:44
  15.1 7.8 %collective-permute-done = bf16[3,80,256]{2,1,0:T(8,128)(2,1)S(1)} collective-permute-done((bf16[3,80,256]{2,1,0:T(8,128)(2,1)}, bf16[3,80,256]{2,1,0:T(8,128)(2,1)S(1)}, u32[]{:S(2)}, u32[]{:S(2)}) %collective-permute-start) | collective-permute-done | bytes 122912 | tf_op jit(solution)/shard_map/ppermute | solution.py:44
  23.0 2.7 fusion.40
  26.6 1.2 collective-permute-start.14
  27.8 1.3 collective-permute-start.2
  29.1 1.8 collective-permute-start.20
  31.0 2.0 collective-permute-start.15
  33.0 2.7 collective-permute-start.8
  36.0 2.9 collective-permute-done.8
  39.2 0.9 collective-permute-start.16
  40.1 1.2 collective-permute-done.21
  41.4 2.7 collective-permute-start.22
  44.1 2.5 collective-permute-done.3
  46.9 0.9 collective-permute-start.10
  47.8 3.3 %collective-permute-done.16 = bf16[4,3,80,256]{3,2,1,0:T(8,128)(2,1)S(1)} collective-permute-done((bf16[4,3,80,256]{3,2,1,0:T(8,128)(2,1)S(1)}, bf16[4,3,80,256]{3,2,1,0:T(8,128)(2,1)S(1)}, u32[]{:S(2)}, u32[]{:S(2)}) %collective-permute-start.16) | collective-permute-done | bytes 491552 | tf_op jit(solution)/shard_map/ppermute | solution.py:44
  51.2 6.4 %collective-permute-start.17 = (bf16[8,3,80,256]{3,2,1,0:T(8,128)(2,1)S(1)}, bf16[8,3,80,256]{3,2,1,0:T(8,128)(2,1)S(1)}, u32[]{:S(2)}, u32[]{:S(2)}) collective-permute-start(bf16[8,3,80,256]{3,2,1,0:T(8,128)(2,1)S(1)} %pad_maximum_fusion.2.refs_0_), channel_id=1, source_target_pairs={{0,4},{4,0},{8,12},{12,8},{16,20},{20,16},{24,28},{28,24},{32,36},... | collective-permute-start | bytes 2949128 | tf_op jit(solution)/shard_map/ppermute | solution.py:44
  57.6 2.8 collective-permute-start.18
  60.4 1.1 pad_maximum_fusion.3.refs_4_
  61.4 2.8 collective-permute-done.4
  64.4 0.9 collective-permute-start.6
  65.7 1.0 copy-done.10
  66.6 7.5 %collective-permute-start.23 = (bf16[8,3,80,256]{3,2,1,0:T(8,128)(2,1)}, bf16[8,3,80,256]{3,2,1,0:T(8,128)(2,1)}, u32[]{:S(2)}, u32[]{:S(2)}) collective-permute-start(bf16[8,3,80,256]{3,2,1,0:T(8,128)(2,1)} %pad_maximum_fusion.3.refs_4_), channel_id=1, source_target_pairs={{0,4},{4,0},{8,12},{12,8},{16,20},{20,16},{24,28},{28,24},{32,36},... | collective-permute-start | bytes 2949128 | tf_op jit(solution)/shard_map/ppermute | solution.py:44
  74.1 8.2 %collective-permute-done.18.refs_2_ = bf16[8,3,80,256]{3,2,1,0:T(8,128)(2,1)} collective-permute-done((bf16[8,3,80,256]{3,2,1,0:T(8,128)(2,1)S(1)}, bf16[8,3,80,256]{3,2,1,0:T(8,128)(2,1)}, u32[]{:S(2)}, u32[]{:S(2)}) %collective-permute-start.18) | collective-permute-done | bytes 983072 | tf_op jit(solution)/shard_map/ppermute | solution.py:44
  83.1 2.5 collective-permute-done.24.refs_6_
  85.6 4.1 %collective-permute-start.25 = (bf16[8,3,80,256]{3,2,1,0:T(8,128)(2,1)}, bf16[8,3,80,256]{3,2,1,0:T(8,128)(2,1)}, u32[]{:S(2)}, u32[]{:S(2)}) collective-permute-start(bf16[8,3,80,256]{3,2,1,0:T(8,128)(2,1)} %collective-permute-done.24.refs_6_), channel_id=1, source_target_pairs={{0,4},{4,0},{8,12},{12,8},{16,20},{20,16},{24,28},{28,24},{32,36},... | collective-permute-start | bytes 2949128 | tf_op jit(solution)/shard_map/ppermute | solution.py:44
  90.1 1.4 collective-permute-done.6.refs_2_
  91.5 9.0 %collective-permute-start.11 = (bf16[8,3,80,384]{3,2,1,0:T(8,128)(2,1)S(1)}, bf16[8,3,80,384]{3,2,1,0:T(8,128)(2,1)}, u32[]{:S(2)}, u32[]{:S(2)}) collective-permute-start(bf16[8,3,80,384]{3,2,1,0:T(8,128)(2,1)S(1)} %pad_maximum_fusion.1.refs_4_), channel_id=1, source_target_pairs={{0,4},{4,0},{8,12},{12,8},{16,20},{20,16},{24,28},{28,24},{32,36},... | collective-permute-start | bytes 4423688 | tf_op jit(solution)/shard_map/ppermute | solution.py:44
  101.0 1.2 copy-done.9
  102.2 1.2 copy-done.11
  103.4 4.2 %shard_map.71.weight = bf16[3,5120,256]{2,1,0:T(8,128)(2,1)S(1)} custom-call(s32[5]{0:T(128)S(1)} %stack.23.place, bf16[8,3,80,256]{3,2,1,0:T(8,128)(2,1)S(1)} %copy-done.9, bf16[8,3,80,256]{3,2,1,0:T(8,128)(2,1)S(1)} %copy-done.11, bf16[8,3,80,256]{3,2,1,0:T(8,128)(2,1)} %collective-permute-done.18.refs_2_, ...), custom_call_target="tpu_custom_call" | custom-call | bytes 15728640 | tf_op jit(solution)/shard_map/pallas_call | solution.py:84
  107.7 3.1 %copy-done.1 = bf16[3,5120,256]{2,1,0:T(8,128)(2,1)} copy-done((bf16[3,5120,256]{2,1,0:T(8,128)(2,1)}, bf16[3,5120,256]{2,1,0:T(8,128)(2,1)S(1)}, u32[]{:S(2)}) %copy-start.1) | copy-done | bytes 7864344
  110.8 3.2 %copy-done.2 = bf16[3,5120,256]{2,1,0:T(8,128)(2,1)S(1)} copy-done((bf16[3,5120,256]{2,1,0:T(8,128)(2,1)S(1)}, bf16[3,5120,256]{2,1,0:T(8,128)(2,1)}, u32[]{:S(2)}) %copy-start.2) | copy-done | bytes 7864344
  114.0 2.0 copy-done.4
  116.0 3.1 %shard_map.73 = bf16[3,320,256]{2,1,0:T(8,128)(2,1)S(1)} custom-call(bf16[320,5120]{1,0:T(8,128)(2,1)S(1)} %copy-done.4, bf16[3,5120,256]{2,1,0:T(8,128)(2,1)S(1)} %copy-done.2), custom_call_target="tpu_custom_call" | custom-call | flops 2516582400 | bytes 11632640 | tf_op jit(solution)/shard_map/pallas_call | solution.py:107
  119.1 0.9 reshape.216
  120.0 1.1 copy.89
  121.2 1.1 copy.90
  122.3 13.2 %all-to-all-start.2 = ((bf16[64,31,128]{2,1,0:T(8,128)(2,1)}), bf16[64,31,128]{2,1,0:T(8,128)(2,1)}, u32[]{:S(2)}, u32[]{:S(2)}) async-start(bf16[64,31,128]{2,1,0:T(8,128)(2,1)} %copy.90), calls=%async_computation.2 | async-start | bytes 1048576 | tf_op jit(solution)/shard_map/all_to_all | solution.py:158
  135.7 1.1 iota_compare_fusion.1
  136.8 47.3 %all-gather.3.cloned.1.call-done.tokens = bf16[320,5120]{1,0:T(8,128)(2,1)} async-done(((bf16[320,1280]{1,0:T(8,128)(2,1)}), bf16[320,5120]{1,0:T(8,128)(2,1)}) %all-gather.3.cloned.1.call-update) | async-done | bytes 3276816 | tf_op jit(solution)/shard_map/all_gather | solution.py:205
  184.1 3.2 %copy-done.3 = bf16[3,5120,256]{2,1,0:T(8,128)(2,1)S(1)} copy-done((bf16[3,5120,256]{2,1,0:T(8,128)(2,1)S(1)}, bf16[3,5120,256]{2,1,0:T(8,128)(2,1)}, u32[]{:S(2)}) %copy-start.3) | copy-done | bytes 7864344
  187.4 1.9 copy-done.6
  189.3 3.1 %shard_map.72 = bf16[3,320,256]{2,1,0:T(8,128)(2,1)S(1)} custom-call(bf16[320,5120]{1,0:T(8,128)(2,1)S(1)} %copy-done.6, bf16[3,5120,256]{2,1,0:T(8,128)(2,1)S(1)} %copy-done.3), custom_call_target="tpu_custom_call" | custom-call | flops 2516582400 | bytes 11632640 | tf_op jit(solution)/shard_map/pallas_call | solution.py:107
  192.3 0.9 reshape.210
  193.2 1.1 copy.81
  194.4 1.2 copy.82
  195.6 12.3 %all-to-all-start = ((bf16[64,31,128]{2,1,0:T(8,128)(2,1)}), bf16[64,31,128]{2,1,0:T(8,128)(2,1)}, u32[]{:S(2)}, u32[]{:S(2)}) async-start(bf16[64,31,128]{2,1,0:T(8,128)(2,1)} %copy.82), calls=%async_computation | async-start | bytes 1048576 | tf_op jit(solution)/shard_map/all_to_all | solution.py:158
  208.1 5.0 %shard_map.68.weight = bf16[3,5120,384]{2,1,0:T(8,128)(2,1)S(1)} custom-call(s32[5]{0:T(128)S(1)} %stack.23.place, bf16[8,3,80,384]{3,2,1,0:T(8,128)(2,1)S(1)} %pad_maximum_fusion.refs_0_, bf16[8,3,80,384]{3,2,1,0:T(8,128)(2,1)} %collective-permute-done.5.refs_1_, bf16[8,3,80,384]{3,2,1,0:T(8,128)(2,1)} %collective-permute-done.6.refs_2_, ...), custom_call_target="tpu_custom_call" | custom-call | bytes 23592960 | tf_op jit(solution)/shard_map/pallas_call | solution.py:84
  213.1 4.3 %copy-done = bf16[3,5120,384]{2,1,0:T(8,128)(2,1)} copy-done((bf16[3,5120,384]{2,1,0:T(8,128)(2,1)}, bf16[3,5120,384]{2,1,0:T(8,128)(2,1)S(1)}, u32[]{:S(2)}) %copy-start) | copy-done | bytes 11796504
  217.5 8.1 %shard_map.70 = bf16[3,320,384]{2,1,0:T(8,128)(2,1)S(1)} custom-call(bf16[320,5120]{1,0:T(8,128)(2,1)S(1)} %copy-done.5, bf16[3,5120,384]{2,1,0:T(8,128)(2,1)} %copy-done), custom_call_target="tpu_custom_call" | custom-call | flops 3774873600 | bytes 15810560 | tf_op jit(solution)/shard_map/pallas_call | solution.py:107
  225.6 8.0 %shard_map.69 = bf16[3,320,384]{2,1,0:T(8,128)(2,1)S(1)} custom-call(bf16[320,5120]{1,0:T(8,128)(2,1)S(1)} %copy-done.7, bf16[3,5120,384]{2,1,0:T(8,128)(2,1)} %copy-done), custom_call_target="tpu_custom_call" | custom-call | flops 3774873600 | bytes 15810560 | tf_op jit(solution)/shard_map/pallas_call | solution.py:107
  234.2 1.2 copy.91
  235.5 0.9 slice.83
  236.5 0.9 slice.77
  238.3 0.8 copy.94
  239.2 12.7 %all-to-all-start.3 = ((bf16[64,10,128]{2,1,0:T(8,128)(2,1)}), bf16[64,10,128]{2,1,0:T(8,128)(2,1)S(1)}, u32[]{:S(2)}, u32[]{:S(2)}) async-start(bf16[64,10,128]{2,1,0:T(8,128)(2,1)} %copy.94), calls=%async_computation.3 | async-start | bytes 524288 | tf_op jit(solution)/shard_map/all_to_all | solution.py:176
  251.9 1.2 copy.83
  254.2 1.5 convolution_convert_fusion.1
  256.5 9.4 %all-to-all-done.3 = bf16[64,10,128]{2,1,0:T(8,128)(2,1)S(1)} async-done(((bf16[64,10,128]{2,1,0:T(8,128)(2,1)}), bf16[64,10,128]{2,1,0:T(8,128)(2,1)S(1)}, u32[]{:S(2)}, u32[]{:S(2)}) %all-to-all-start.3) | async-done | bytes 163872 | tf_op jit(solution)/shard_map/all_to_all | solution.py:176
  265.9 4.5 %all-to-all-start.1 = ((bf16[64,10,128]{2,1,0:T(8,128)(2,1)}), bf16[64,10,128]{2,1,0:T(8,128)(2,1)S(1)}, u32[]{:S(2)}, u32[]{:S(2)}) async-start(bf16[64,10,128]{2,1,0:T(8,128)(2,1)} %copy.86), calls=%async_computation.1 | async-start | bytes 524288 | tf_op jit(solution)/shard_map/all_to_all | solution.py:176
  270.5 2.5 fusion.41
  273.2 3.9 %fusion.12 = bf16[3,128,640]{2,1,0:T(8,128)(2,1)S(1)} fusion(bf16[640,3,128]{0,2,1:T(8,128)(2,1)S(1)} %bitcast.118, f32[3,640]{1,0:T(4,128)S(1)} %fusion.41, s32[3,640]{1,0:T(4,128)S(1)} %broadcast_subtract_fusion, s32[640]{0:T(1024)S(1)} %add_select_fusion, pred[640,640]{0,1:T(8,128)(4,1)} %get-tuple-element.28, pred[640,640]{0,1:T(8,128)(4,1)S(1)} %copy-done.14, ...), kind=kOutput, calls=%fused_computation.23 | convolution fusion | flops 639224320 | bytes 2803200 | tf_op jit(solution)/shard_map/hqk,khc->qhc/dot_general | solution.py:144
  277.2 1.0 copy.97
  278.4 6.1 %all-to-all-done.1 = bf16[64,10,128]{2,1,0:T(8,128)(2,1)S(1)} async-done(((bf16[64,10,128]{2,1,0:T(8,128)(2,1)}), bf16[64,10,128]{2,1,0:T(8,128)(2,1)S(1)}, u32[]{:S(2)}, u32[]{:S(2)}) %all-to-all-start.1) | async-done | bytes 163872 | tf_op jit(solution)/shard_map/all_to_all | solution.py:176
  (107 shorter events, 9.5 us)
Async XLA Ops:
  7.2 103.6 %all-gather.5.cloned.1.call-start = ((), (), s32[]{:S(2)}) async-start(), calls=%async_computation.5 | async-start | bytes 4096000 | tf_op jit(solution)/shard_map/all_gather | solution.py:205
  7.2 15.8 %collective-permute-start.1 = (bf16[3,80,384]{2,1,0:T(8,128)(2,1)}, bf16[3,80,384]{2,1,0:T(8,128)(2,1)S(1)}, u32[]{:S(2)}, u32[]{:S(2)}) collective-permute-start(bf16[3,80,384]{2,1,0:T(8,128)(2,1)} %bitcast.88), channel_id=1, source_target_pairs={{0,8},{4,12},{8,0},{12,4},{16,24},{20,28},{24,16},{28,20},{32,40},... | collective-permute-start | bytes 552968 | tf_op jit(solution)/shard_map/ppermute | solution.py:44
  15.0 7.9 %collective-permute-start = (bf16[3,80,256]{2,1,0:T(8,128)(2,1)}, bf16[3,80,256]{2,1,0:T(8,128)(2,1)S(1)}, u32[]{:S(2)}, u32[]{:S(2)}) collective-permute-start(bf16[3,80,256]{2,1,0:T(8,128)(2,1)} %bitcast.97), channel_id=1, source_target_pairs={{0,8},{4,12},{8,0},{12,4},{16,24},{20,28},{24,16},{28,20},{32,40},... | collective-permute-start | bytes 368648 | tf_op jit(solution)/shard_map/ppermute | solution.py:44
  25.7 0.9 copy-start.13
  25.7 2.1 copy-start.12
  25.8 158.4 %all-gather.3.cloned.1.call-start = ((), (), s32[]{:S(2)}) async-start(), calls=%async_computation.4 | async-start | bytes 4096000 | tf_op jit(solution)/shard_map/all_gather | solution.py:205
  26.6 4.3 %collective-permute-start.14 = (bf16[1,3,80,256]{3,2,1,0:T(8,128)(2,1)S(1)}, bf16[1,3,80,256]{3,2,1,0:T(8,128)(2,1)S(1)}, u32[]{:S(2)}, u32[]{:S(2)}) collective-permute-start(bf16[1,3,80,256]{3,2,1,0:T(8,128)(2,1)S(1)} %bitcast.98), channel_id=1, source_target_pairs={{0,16},{4,20},{8,24},{12,28},{16,0},{20,4},{24,8},{28,12},{32,48},... | collective-permute-start | bytes 368648 | tf_op jit(solution)/shard_map/ppermute | solution.py:44
  27.8 7.8 %collective-permute-start.2 = (bf16[1,3,80,384]{3,2,1,0:T(8,128)(2,1)S(1)}, bf16[1,3,80,384]{3,2,1,0:T(8,128)(2,1)S(1)}, u32[]{:S(2)}, u32[]{:S(2)}) collective-permute-start(bf16[1,3,80,384]{3,2,1,0:T(8,128)(2,1)S(1)} %bitcast.89), channel_id=1, source_target_pairs={{0,64},{4,68},{8,72},{12,76},{16,80},{20,84},{24,88},{28,92},{32,9... | collective-permute-start | bytes 552968 | tf_op jit(solution)/shard_map/ppermute | solution.py:44
  29.1 6.7 %collective-permute-start.20 = (bf16[1,3,80,256]{3,2,1,0:T(8,128)(2,1)S(1)}, bf16[1,3,80,256]{3,2,1,0:T(8,128)(2,1)S(1)}, u32[]{:S(2)}, u32[]{:S(2)}) collective-permute-start(bf16[1,3,80,256]{3,2,1,0:T(8,128)(2,1)S(1)} %bitcast.102), channel_id=1, source_target_pairs={{0,48},{4,52},{8,56},{12,60},{16,32},{20,36},{24,40},{28,44},{32,1... | collective-permute-start | bytes 368648 | tf_op jit(solution)/shard_map/ppermute | solution.py:44
  31.0 8.2 %collective-permute-start.15 = (bf16[2,3,80,256]{3,2,1,0:T(8,128)(2,1)S(1)}, bf16[2,3,80,256]{3,2,1,0:T(8,128)(2,1)S(1)}, u32[]{:S(2)}, u32[]{:S(2)}) collective-permute-start(bf16[2,3,80,256]{3,2,1,0:T(8,128)(2,1)S(1)} %pad_maximum_fusion.12), channel_id=1, source_target_pairs={{0,48},{4,52},{8,56},{12,60},{16,32},{20,36},{24,40},{28,44},{32,1... | collective-permute-start | bytes 737288 | tf_op jit(solution)/shard_map/ppermute | solution.py:44
  33.0 6.0 %collective-permute-start.8 = (bf16[1,3,80,384]{3,2,1,0:T(8,128)(2,1)S(1)}, bf16[1,3,80,384]{3,2,1,0:T(8,128)(2,1)S(1)}, u32[]{:S(2)}, u32[]{:S(2)}) collective-permute-start(bf16[1,3,80,384]{3,2,1,0:T(8,128)(2,1)S(1)} %bitcast.93), channel_id=1, source_target_pairs={{0,192},{4,196},{8,200},{12,204},{16,208},{20,212},{24,216},{28,22... | collective-permute-start | bytes 552968 | tf_op jit(solution)/shard_map/ppermute | solution.py:44
  35.7 10.9 %collective-permute-start.3 = (bf16[2,3,80,384]{3,2,1,0:T(8,128)(2,1)S(1)}, bf16[2,3,80,384]{3,2,1,0:T(8,128)(2,1)S(1)}, u32[]{:S(2)}, u32[]{:S(2)}) collective-permute-start(bf16[2,3,80,384]{3,2,1,0:T(8,128)(2,1)S(1)} %pad_maximum_fusion.9), channel_id=1, source_target_pairs={{0,192},{4,196},{8,200},{12,204},{16,208},{20,212},{24,216},{28,22... | collective-permute-start | bytes 1105928 | tf_op jit(solution)/shard_map/ppermute | solution.py:44
  35.9 5.4 %collective-permute-start.21 = (bf16[2,3,80,256]{3,2,1,0:T(8,128)(2,1)S(1)}, bf16[2,3,80,256]{3,2,1,0:T(8,128)(2,1)S(1)}, u32[]{:S(2)}, u32[]{:S(2)}) collective-permute-start(bf16[2,3,80,256]{3,2,1,0:T(8,128)(2,1)S(1)} %pad_maximum_fusion.13), channel_id=1, source_target_pairs={{0,64},{4,68},{8,72},{12,76},{16,80},{20,84},{24,88},{28,92},{32,9... | collective-permute-start | bytes 737288 | tf_op jit(solution)/shard_map/ppermute | solution.py:44
  39.0 7.9 %collective-permute-start.9 = (bf16[2,3,80,384]{3,2,1,0:T(8,128)(2,1)S(1)}, bf16[2,3,80,384]{3,2,1,0:T(8,128)(2,1)S(1)}, u32[]{:S(2)}, u32[]{:S(2)}) collective-permute-start(bf16[2,3,80,384]{3,2,1,0:T(8,128)(2,1)S(1)} %pad_maximum_fusion.10), channel_id=1, source_target_pairs={{0,16},{4,20},{8,24},{12,28},{16,0},{20,4},{24,8},{28,12},{32,48},... | collective-permute-start | bytes 1105928 | tf_op jit(solution)/shard_map/ppermute | solution.py:44
  39.2 11.9 %collective-permute-start.16 = (bf16[4,3,80,256]{3,2,1,0:T(8,128)(2,1)S(1)}, bf16[4,3,80,256]{3,2,1,0:T(8,128)(2,1)S(1)}, u32[]{:S(2)}, u32[]{:S(2)}) collective-permute-start(bf16[4,3,80,256]{3,2,1,0:T(8,128)(2,1)S(1)} %pad_maximum_fusion.7), channel_id=1, source_target_pairs={{0,64},{4,68},{8,72},{12,76},{16,80},{20,84},{24,88},{28,92},{32,9... | collective-permute-start | bytes 1474568 | tf_op jit(solution)/shard_map/ppermute | solution.py:44
  41.4 19.0 %collective-permute-start.22 = (bf16[4,3,80,256]{3,2,1,0:T(8,128)(2,1)S(1)}, bf16[4,3,80,256]{3,2,1,0:T(8,128)(2,1)S(1)}, u32[]{:S(2)}, u32[]{:S(2)}) collective-permute-start(bf16[4,3,80,256]{3,2,1,0:T(8,128)(2,1)S(1)} %pad_maximum_fusion.8), channel_id=1, source_target_pairs={{0,192},{4,196},{8,200},{12,204},{16,208},{20,212},{24,216},{28,22... | collective-permute-start | bytes 1474568 | tf_op jit(solution)/shard_map/ppermute | solution.py:44
  46.7 17.5 %collective-permute-start.4 = (bf16[4,3,80,384]{3,2,1,0:T(8,128)(2,1)S(1)}, bf16[4,3,80,384]{3,2,1,0:T(8,128)(2,1)S(1)}, u32[]{:S(2)}, u32[]{:S(2)}) collective-permute-start(bf16[4,3,80,384]{3,2,1,0:T(8,128)(2,1)S(1)} %pad_maximum_fusion.4), channel_id=1, source_target_pairs={{0,16},{4,20},{8,24},{12,28},{16,0},{20,4},{24,8},{28,12},{32,48},... | collective-permute-start | bytes 2211848 | tf_op jit(solution)/shard_map/ppermute | solution.py:44
  46.9 18.4 %collective-permute-start.10 = (bf16[4,3,80,384]{3,2,1,0:T(8,128)(2,1)S(1)}, bf16[4,3,80,384]{3,2,1,0:T(8,128)(2,1)S(1)}, u32[]{:S(2)}, u32[]{:S(2)}) collective-permute-start(bf16[4,3,80,384]{3,2,1,0:T(8,128)(2,1)S(1)} %pad_maximum_fusion.5), channel_id=1, source_target_pairs={{0,48},{4,52},{8,56},{12,60},{16,32},{20,36},{24,40},{28,44},{32,1... | collective-permute-start | bytes 2211848 | tf_op jit(solution)/shard_map/ppermute | solution.py:44
  51.2 13.2 %copy-start.8 = (bf16[8,3,80,256]{3,2,1,0:T(8,128)(2,1)}, bf16[8,3,80,256]{3,2,1,0:T(8,128)(2,1)S(1)}, u32[]{:S(2)}) copy-start(bf16[8,3,80,256]{3,2,1,0:T(8,128)(2,1)S(1)} %pad_maximum_fusion.2.refs_0_) | copy-start | bytes 2949124
  51.2 14.5 %collective-permute-start.17 = (bf16[8,3,80,256]{3,2,1,0:T(8,128)(2,1)S(1)}, bf16[8,3,80,256]{3,2,1,0:T(8,128)(2,1)S(1)}, u32[]{:S(2)}, u32[]{:S(2)}) collective-permute-start(bf16[8,3,80,256]{3,2,1,0:T(8,128)(2,1)S(1)} %pad_maximum_fusion.2.refs_0_), channel_id=1, source_target_pairs={{0,4},{4,0},{8,12},{12,8},{16,20},{20,16},{24,28},{28,24},{32,36},... | collective-permute-start | bytes 2949128 | tf_op jit(solution)/shard_map/ppermute | solution.py:44
  57.6 24.8 %collective-permute-start.18 = (bf16[8,3,80,256]{3,2,1,0:T(8,128)(2,1)S(1)}, bf16[8,3,80,256]{3,2,1,0:T(8,128)(2,1)}, u32[]{:S(2)}, u32[]{:S(2)}) collective-permute-start(bf16[8,3,80,256]{3,2,1,0:T(8,128)(2,1)S(1)} %pad_maximum_fusion.2.refs_0_), channel_id=1, source_target_pairs={{0,192},{4,196},{8,200},{12,204},{16,208},{20,212},{24,216},{28,22... | collective-permute-start | bytes 2949128 | tf_op jit(solution)/shard_map/ppermute | solution.py:44
  61.4 24.2 %collective-permute-start.24 = (bf16[8,3,80,256]{3,2,1,0:T(8,128)(2,1)}, bf16[8,3,80,256]{3,2,1,0:T(8,128)(2,1)}, u32[]{:S(2)}, u32[]{:S(2)}) collective-permute-start(bf16[8,3,80,256]{3,2,1,0:T(8,128)(2,1)} %pad_maximum_fusion.3.refs_4_), channel_id=1, source_target_pairs={{0,16},{4,20},{8,24},{12,28},{16,0},{20,4},{24,8},{28,12},{32,48},... | collective-permute-start | bytes 2949128 | tf_op jit(solution)/shard_map/ppermute | solution.py:44
  64.4 25.3 %copy-start.16 = (s32[1,640]{1,0:T(1,128)S(1)}, s32[1,640]{1,0:T(1,128)}, u32[]{:S(2)}) copy-start(s32[1,640]{1,0:T(1,128)} %param.8) | copy-start | bytes 7684
  64.4 27.1 %collective-permute-start.6 = (bf16[8,3,80,384]{3,2,1,0:T(8,128)(2,1)S(1)}, bf16[8,3,80,384]{3,2,1,0:T(8,128)(2,1)}, u32[]{:S(2)}, u32[]{:S(2)}) collective-permute-start(bf16[8,3,80,384]{3,2,1,0:T(8,128)(2,1)S(1)} %pad_maximum_fusion.refs_0_), channel_id=1, source_target_pairs={{0,48},{4,52},{8,56},{12,60},{16,32},{20,36},{24,40},{28,44},{32,1... | collective-permute-start | bytes 4423688 | tf_op jit(solution)/shard_map/ppermute | solution.py:44
  65.5 35.0 %collective-permute-start.12 = (bf16[8,3,80,384]{3,2,1,0:T(8,128)(2,1)S(1)}, bf16[8,3,80,384]{3,2,1,0:T(8,128)(2,1)}, u32[]{:S(2)}, u32[]{:S(2)}) collective-permute-start(bf16[8,3,80,384]{3,2,1,0:T(8,128)(2,1)S(1)} %pad_maximum_fusion.1.refs_4_), channel_id=1, source_target_pairs={{0,64},{4,68},{8,72},{12,76},{16,80},{20,84},{24,88},{28,92},{32,9... | collective-permute-start | bytes 4423688 | tf_op jit(solution)/shard_map/ppermute | solution.py:44
  65.7 1.0 copy-start.10
  66.6 23.5 %collective-permute-start.23 = (bf16[8,3,80,256]{3,2,1,0:T(8,128)(2,1)}, bf16[8,3,80,256]{3,2,1,0:T(8,128)(2,1)}, u32[]{:S(2)}, u32[]{:S(2)}) collective-permute-start(bf16[8,3,80,256]{3,2,1,0:T(8,128)(2,1)} %pad_maximum_fusion.3.refs_4_), channel_id=1, source_target_pairs={{0,4},{4,0},{8,12},{12,8},{16,20},{20,16},{24,28},{28,24},{32,36},... | collective-permute-start | bytes 2949128 | tf_op jit(solution)/shard_map/ppermute | solution.py:44
  82.4 18.2 %collective-permute-start.19 = (bf16[8,3,80,256]{3,2,1,0:T(8,128)(2,1)}, bf16[8,3,80,256]{3,2,1,0:T(8,128)(2,1)}, u32[]{:S(2)}, u32[]{:S(2)}) collective-permute-start(bf16[8,3,80,256]{3,2,1,0:T(8,128)(2,1)} %collective-permute-done.18.refs_2_), channel_id=1, source_target_pairs={{0,4},{4,0},{8,12},{12,8},{16,20},{20,16},{24,28},{28,24},{32,36},... | collective-permute-start | bytes 2949128 | tf_op jit(solution)/shard_map/ppermute | solution.py:44
  85.6 15.4 %collective-permute-start.25 = (bf16[8,3,80,256]{3,2,1,0:T(8,128)(2,1)}, bf16[8,3,80,256]{3,2,1,0:T(8,128)(2,1)}, u32[]{:S(2)}, u32[]{:S(2)}) collective-permute-start(bf16[8,3,80,256]{3,2,1,0:T(8,128)(2,1)} %collective-permute-done.24.refs_6_), channel_id=1, source_target_pairs={{0,4},{4,0},{8,12},{12,8},{16,20},{20,16},{24,28},{28,24},{32,36},... | collective-permute-start | bytes 2949128 | tf_op jit(solution)/shard_map/ppermute | solution.py:44
  90.1 118.0 %collective-permute-start.5 = (bf16[8,3,80,384]{3,2,1,0:T(8,128)(2,1)S(1)}, bf16[8,3,80,384]{3,2,1,0:T(8,128)(2,1)}, u32[]{:S(2)}, u32[]{:S(2)}) collective-permute-start(bf16[8,3,80,384]{3,2,1,0:T(8,128)(2,1)S(1)} %pad_maximum_fusion.refs_0_), channel_id=1, source_target_pairs={{0,4},{4,0},{8,12},{12,8},{16,20},{20,16},{24,28},{28,24},{32,36},... | collective-permute-start | bytes 4423688 | tf_op jit(solution)/shard_map/ppermute | solution.py:44
  91.5 116.6 %collective-permute-start.11 = (bf16[8,3,80,384]{3,2,1,0:T(8,128)(2,1)S(1)}, bf16[8,3,80,384]{3,2,1,0:T(8,128)(2,1)}, u32[]{:S(2)}, u32[]{:S(2)}) collective-permute-start(bf16[8,3,80,384]{3,2,1,0:T(8,128)(2,1)S(1)} %pad_maximum_fusion.1.refs_4_), channel_id=1, source_target_pairs={{0,4},{4,0},{8,12},{12,8},{16,20},{20,16},{24,28},{28,24},{32,36},... | collective-permute-start | bytes 4423688 | tf_op jit(solution)/shard_map/ppermute | solution.py:44
  100.5 107.6 %collective-permute-start.7 = (bf16[8,3,80,384]{3,2,1,0:T(8,128)(2,1)}, bf16[8,3,80,384]{3,2,1,0:T(8,128)(2,1)}, u32[]{:S(2)}, u32[]{:S(2)}) collective-permute-start(bf16[8,3,80,384]{3,2,1,0:T(8,128)(2,1)} %collective-permute-done.6.refs_2_), channel_id=1, source_target_pairs={{0,4},{4,0},{8,12},{12,8},{16,20},{20,16},{24,28},{28,24},{32,36},... | collective-permute-start | bytes 4423688 | tf_op jit(solution)/shard_map/ppermute | solution.py:44
  100.5 107.6 %collective-permute-start.13 = (bf16[8,3,80,384]{3,2,1,0:T(8,128)(2,1)}, bf16[8,3,80,384]{3,2,1,0:T(8,128)(2,1)}, u32[]{:S(2)}, u32[]{:S(2)}) collective-permute-start(bf16[8,3,80,384]{3,2,1,0:T(8,128)(2,1)} %collective-permute-done.12.refs_6_), channel_id=1, source_target_pairs={{0,4},{4,0},{8,12},{12,8},{16,20},{20,16},{24,28},{28,24},{32,36},... | collective-permute-start | bytes 4423688 | tf_op jit(solution)/shard_map/ppermute | solution.py:44
  101.0 1.2 copy-start.9
  102.2 1.2 copy-start.11
  107.7 3.1 %copy-start.1 = (bf16[3,5120,256]{2,1,0:T(8,128)(2,1)}, bf16[3,5120,256]{2,1,0:T(8,128)(2,1)S(1)}, u32[]{:S(2)}) copy-start(bf16[3,5120,256]{2,1,0:T(8,128)(2,1)S(1)} %shard_map.71.weight) | copy-start | bytes 23592964
  110.8 3.2 %copy-start.2 = (bf16[3,5120,256]{2,1,0:T(8,128)(2,1)S(1)}, bf16[3,5120,256]{2,1,0:T(8,128)(2,1)}, u32[]{:S(2)}) copy-start(bf16[3,5120,256]{2,1,0:T(8,128)(2,1)} %copy-done.1) | copy-start | bytes 23592964
  114.0 2.0 copy-start.4
  122.3 73.3 %all-to-all-start.2 = ((bf16[64,31,128]{2,1,0:T(8,128)(2,1)}), bf16[64,31,128]{2,1,0:T(8,128)(2,1)}, u32[]{:S(2)}, u32[]{:S(2)}) async-start(bf16[64,31,128]{2,1,0:T(8,128)(2,1)} %copy.90), calls=%async_computation.2 | async-start | bytes 1048576 | tf_op jit(solution)/shard_map/all_to_all | solution.py:158
  184.1 3.2 %copy-start.3 = (bf16[3,5120,256]{2,1,0:T(8,128)(2,1)S(1)}, bf16[3,5120,256]{2,1,0:T(8,128)(2,1)}, u32[]{:S(2)}) copy-start(bf16[3,5120,256]{2,1,0:T(8,128)(2,1)} %copy-done.1) | copy-start | bytes 23592964
  187.3 1.9 copy-start.6
  194.4 13.6 %copy-start.17 = (s32[3]{0:T(128)S(1)}, s32[3]{0:T(128)}, u32[]{:S(2)}) copy-start(s32[3]{0:T(128)} %param.9) | copy-start | bytes 40
  195.6 40.9 %all-to-all-start = ((bf16[64,31,128]{2,1,0:T(8,128)(2,1)}), bf16[64,31,128]{2,1,0:T(8,128)(2,1)}, u32[]{:S(2)}, u32[]{:S(2)}) async-start(bf16[64,31,128]{2,1,0:T(8,128)(2,1)} %copy.82), calls=%async_computation | async-start | bytes 1048576 | tf_op jit(solution)/shard_map/all_to_all | solution.py:158
  208.1 9.4 %copy-start.5 = (bf16[320,5120]{1,0:T(8,128)(2,1)S(1)}, bf16[320,5120]{1,0:T(8,128)(2,1)}, u32[]{:S(2)}) copy-start(bf16[320,5120]{1,0:T(8,128)(2,1)} %all-gather.5.cloned.1.call-done.tokens) | copy-start | bytes 9830404
  213.1 4.3 %copy-start = (bf16[3,5120,384]{2,1,0:T(8,128)(2,1)}, bf16[3,5120,384]{2,1,0:T(8,128)(2,1)S(1)}, u32[]{:S(2)}) copy-start(bf16[3,5120,384]{2,1,0:T(8,128)(2,1)S(1)} %shard_map.68.weight) | copy-start | bytes 35389444
  217.5 8.1 %copy-start.7 = (bf16[320,5120]{1,0:T(8,128)(2,1)S(1)}, bf16[320,5120]{1,0:T(8,128)(2,1)}, u32[]{:S(2)}) copy-start(bf16[320,5120]{1,0:T(8,128)(2,1)} %all-gather.3.cloned.1.call-done.tokens) | copy-start | bytes 9830404
  239.2 26.8 %all-to-all-start.3 = ((bf16[64,10,128]{2,1,0:T(8,128)(2,1)}), bf16[64,10,128]{2,1,0:T(8,128)(2,1)S(1)}, u32[]{:S(2)}, u32[]{:S(2)}) async-start(bf16[64,10,128]{2,1,0:T(8,128)(2,1)} %copy.94), calls=%async_computation.3 | async-start | bytes 524288 | tf_op jit(solution)/shard_map/all_to_all | solution.py:176
  253.4 0.7 copy-start.18
  254.1 16.4 %copy-start.14 = (pred[640,640]{0,1:T(8,128)(4,1)S(1)}, pred[640,640]{0,1:T(8,128)(4,1)}, u32[]{:S(2)}) copy-start(pred[640,640]{0,1:T(8,128)(4,1)} %get-tuple-element.27) | copy-start | bytes 1228804
  254.1 16.4 %copy-start.15 = (pred[640,640]{0,1:T(8,128)(4,1)S(1)}, pred[640,640]{0,1:T(8,128)(4,1)}, u32[]{:S(2)}) copy-start(pred[640,640]{0,1:T(8,128)(4,1)} %get-tuple-element.28) | copy-start | bytes 1228804
  265.9 18.6 %all-to-all-start.1 = ((bf16[64,10,128]{2,1,0:T(8,128)(2,1)}), bf16[64,10,128]{2,1,0:T(8,128)(2,1)S(1)}, u32[]{:S(2)}, u32[]{:S(2)}) async-start(bf16[64,10,128]{2,1,0:T(8,128)(2,1)} %copy.86), calls=%async_computation.1 | async-start | bytes 524288 | tf_op jit(solution)/shard_map/all_to_all | solution.py:176
Sparse Core Ops, SparseCore 0:
  25.9 76.0 all-gather.4
  103.7 80.3 all-gather.2

commit v2 on v1

--- a/solution.py
+++ b/solution.py
@@ -11,7 +11,7 @@
 HD = 128
 BLK = 128
 NY, NX, NH, NC = 4, 4, 2, 2
-CHUNKS = (320, 320)
+NZ = 4
 
 
 def seq_pairs(move):
@@ -92,34 +92,79 @@
         cost_estimate=pl.CostEstimate(
             flops=0, bytes_accessed=4 * 3 * total * cols, transcendentals=0
         ),
-    )(place, *pieces)
-
-
-def project_kernel(tokens, weight, out):
-    out[0] = jnp.dot(
-        tokens[...], weight[0], preferred_element_type=jnp.float32
-    ).astype(out.dtype)
-
-
-def project(tokens, weight):
+    )(place, *[pltpu.with_memory_space_constraint(piece, pltpu.HBM) for piece in pieces])
+
+
+def project_kernel(tokens, weight, out, held, sem, *loaded):
+    depth = held.shape[1] // NZ
+
+    def copy(k):
+        cols = pl.ds(k * depth, depth)
+        return pltpu.make_async_copy(tokens.at[:, cols], held.at[:, cols], sem.at[k])
+
+    def load(j, k):
+        rows = pl.ds(k * depth, depth)
+        return pltpu.make_async_copy(
+            weight.at[j, rows, :], loaded[0].at[j, rows, :], loaded[1].at[j, k]
+        )
+
+    factor = loaded[0] if loaded else weight
+    for k in range(NZ):
+        copy(k).start()
+        if loaded:
+            load(0, k).start()
+    if loaded:
+        for j in range(1, 3):
+            for k in range(NZ):
+                load(j, k).start()
+    acc = None
+    for k in range(NZ):
+        copy(k).wait()
+        if loaded:
+            load(0, k).wait()
+        cols = slice(k * depth, (k + 1) * depth)
+        term = jnp.dot(held[:, cols], factor[0, cols], preferred_element_type=jnp.float32)
+        acc = term if acc is None else acc + term
+    out[0] = acc.astype(out.dtype)
+
+    def step(j, carry):
+        if loaded:
+            for k in range(NZ):
+                load(j, k).wait()
+        out[j] = jnp.dot(
+            held[...], factor[j], preferred_element_type=jnp.float32
+        ).astype(out.dtype)
+        return carry
+
+    lax.fori_loop(1, 3, step, 0)
+
+
+def project(tokens, weight, load):
     rows, total = tokens.shape
     cols = weight.shape[2]
+    scratch = [pltpu.VMEM((rows, total), jnp.bfloat16), pltpu.SemaphoreType.DMA((NZ,))]
+    if load:
+        weight = pltpu.with_memory_space_constraint(weight, pltpu.HBM)
+        scratch += [
+            pltpu.VMEM((3, total, cols), jnp.bfloat16),
+            pltpu.SemaphoreType.DMA((3, NZ)),
+        ]
     return pl.pallas_call(
         project_kernel,
-        grid=(3,),
         out_shape=jax.ShapeDtypeStruct((3, rows, cols), jnp.bfloat16),
         in_specs=[
-            pl.BlockSpec((rows, total), lambda j: (0, 0)),
-            pl.BlockSpec((1, total, cols), lambda j: (j, 0, 0)),
+            pl.BlockSpec(memory_space=pltpu.HBM),
+            pl.BlockSpec(memory_space=pltpu.HBM if load else pltpu.VMEM),
         ],
-        out_specs=pl.BlockSpec((1, rows, cols), lambda j: (j, 0, 0)),
-        compiler_params=pltpu.CompilerParams(vmem_limit_bytes=40 * 1024 * 1024),
+        out_specs=pl.BlockSpec(memory_space=pltpu.VMEM),
+        scratch_shapes=scratch,
+        compiler_params=pltpu.CompilerParams(vmem_limit_bytes=20 * 1024 * 1024),
         cost_estimate=pl.CostEstimate(
             flops=2 * rows * total * 3 * cols,
             bytes_accessed=2 * (rows * total + 3 * total * cols + 3 * rows * cols),
             transcendentals=0,
         ),
-    )(tokens, weight)
+    )(pltpu.with_memory_space_constraint(tokens, pltpu.HBM), weight)
 
 
 def local_attend(qkv, valid_day, reach):
@@ -193,22 +238,11 @@
     own_local = jnp.transpose(w_local, (1, 0, 2))
     other_strided = swap(own_strided, "h")
     other_local = swap(own_local, "h")
-    tokens, other_strided, other_local = lax.optimization_barrier(
-        (tokens, other_strided, other_local)
-    )
     weight_strided = place_weights(place, own_strided, other_strided, 0)
     weight_local = place_weights(place, own_local, other_local, 1)
-    out_strided, qkv_local = [], []
-    start = 0
-    for size in CHUNKS:
-        rows = slice(start, start + size)
-        gathered = lax.all_gather(tokens[rows], "fsdp", axis=1, tiled=True)
-        qkv = project(gathered, weight_strided)
-        out_strided.append(strided_attend(qkv, valid[0, rows]))
-        qkv_local.append(project(gathered, weight_local))
-        start += size
-    out_strided = jnp.concatenate(out_strided, axis=0)
-    qkv_local = jnp.concatenate(qkv_local, axis=1)
+    gathered = lax.all_gather(tokens, "fsdp", axis=1, tiled=True)
+    out_strided = strided_attend(project(gathered, weight_strided, True), valid[0])
+    qkv_local = project(gathered, weight_local, False)
     out_local = local_attend(qkv_local, valid[0], band_reach)
     return (out_local, out_strided)
 

time: 294 us -> 230 us (0.78); the launches traced: 292 us -> 225 us
  local copies, waits for them, and re-layouts: 40.1 us -> 12.4 us
  waiting for transfers between devices: 96.3 us -> 72.8 us
  starting transfers between devices: 96.9 us -> 80.3 us
    unnamed x43 -> x37, local copies, waits for them, and re-layouts: 23.3 us -> 6.05 us
    all_gather x2 -> x1, waiting for transfers between devices: 47.3 us -> 30.8 us  [body(): gathered = lax.all_gather(tokens, 'fsdp', axis=1, tiled=True)]
    all_to_all x2 -> x1, starting transfers between devices: 25.5 us -> 12.1 us  [strided_attend(): lax.all_to_all(packed, 'seq', split_axis=0, concat_axis=0, tiled=True)]
    all_to_all x2 -> x1, starting transfers between devices: 17.3 us -> 9.31 us  [strided_attend(): lax.all_to_all(result, 'seq', split_axis=0, concat_axis=0, tiled=True)]
    all_to_all x2 -> x1, waiting for transfers between devices: 15.6 us -> 8.84 us  [strided_attend(): lax.all_to_all(result, 'seq', split_axis=0, concat_axis=0, tiled=True)]
    ppermute x26, starting transfers between devices: 54 us -> 58.8 us  [swap(): return lax.ppermute(value, 'seq', seq_pairs(MOVES[kind]))]
    ppermute x26, waiting for transfers between devices: 32.7 us -> 29 us  [swap(): return lax.ppermute(value, 'seq', seq_pairs(MOVES[kind]))]
    reshape x4 -> x2, local copies, waits for them, and re-layouts: 4.06 us -> 0.47 us  [strided_attend(): packed = qkv.reshape(3, peers, count, heads, HD).transpose(1, 0, 3, 2, 4)]
  transfers between devices with their start and end apart: 32 -> 29, of which waited for: 13 -> 12; matrix products, arithmetic and copies ran while one was open for 8% -> 6% of each run, Pallas kernels for 11% -> 15%
where the time goes in v2:
time: 230 us; the launch traced here: 225 us
  starting transfers between devices  80.3 us (35%)
  waiting for transfers between devices  72.8 us (32%)
  Pallas kernels  32.9 us (14%)
  between operations  14.5 us (6%)
  local copies, waits for them, and re-layouts  12.4 us (5%)
  matrix products  8.14 us (4%)
  other arithmetic  4.4 us (2%)
    ppermute x26, starting transfers between devices, swap(): return lax.ppermute(value, 'seq', seq_pairs(MOVES[kind]))  58.8 us
    all_gather x1, waiting for transfers between devices, body(): gathered = lax.all_gather(tokens, 'fsdp', axis=1, tiled=True)  30.8 us
    ppermute x26, waiting for transfers between devices, swap(): return lax.ppermute(value, 'seq', seq_pairs(MOVES[kind]))  29 us
    pallas_call x2, Pallas kernels, project(): pl.pallas_call(project_kernel, out_shape=jax.ShapeDtypeStruct((3, rows, c...  23.9 us
    all_to_all x1, starting transfers between devices, strided_attend(): lax.all_to_all(packed, 'seq', split_axis=0, concat_axis=0, tiled=True)  12.1 us
    all_to_all x1, starting transfers between devices, strided_attend(): lax.all_to_all(result, 'seq', split_axis=0, concat_axis=0, tiled=True)  9.31 us
    pallas_call x2, Pallas kernels, place_weights(): pl.pallas_call(functools.partial(place_kernel, (OWN_ORDERS[which], OTHER_...  8.98 us
    all_to_all x1, waiting for transfers between devices, strided_attend(): lax.all_to_all(result, 'seq', split_axis=0, concat_axis=0, tiled=True)  8.84 us
  transfers between devices with their start and end apart: 29, of which 12 were waited for; matrix products, arithmetic and copies ran while one was open for 6% of the time, Pallas kernels for 15%

profile of v2, /device:TPU:1, one launch (start us, length us, event | category | flops | bytes accessed | tf_op | source)
XLA Modules:
  0.0 225.5 jit_solution(13415475888572733904)
XLA Ops:
  7.2 0.7 all-gather.2.cloned.1.call-update
  7.9 0.1 copy-done.6
  8.1 7.7 %collective-permute-start.19 = (bf16[3,80,256]{2,1,0:T(8,128)(2,1)S(1)}, bf16[3,80,256]{2,1,0:T(8,128)(2,1)S(1)}, u32[]{:S(2)}, u32[]{:S(2)}) collective-permute-start(bf16[3,80,256]{2,1,0:T(8,128)(2,1)S(1)} %bitcast.68), channel_id=1, source_target_pairs={{0,8},{4,12},{8,0},{12,4},{16,24},{20,28},{24,16},{28,20},{32,40},... | collective-permute-start | bytes 368648 | tf_op jit(solution)/shard_map/ppermute | solution.py:44
  15.8 1.2 collective-permute-start.13
  17.1 1.3 collective-permute-start
  18.4 3.0 %collective-permute-start.20 = (bf16[1,3,80,256]{3,2,1,0:T(8,128)(2,1)S(1)}, bf16[1,3,80,256]{3,2,1,0:T(8,128)(2,1)S(1)}, u32[]{:S(2)}, u32[]{:S(2)}) collective-permute-start(bf16[1,3,80,256]{3,2,1,0:T(8,128)(2,1)S(1)} %bitcast.73), channel_id=1, source_target_pairs={{0,48},{4,52},{8,56},{12,60},{16,32},{20,36},{24,40},{28,44},{32,1... | collective-permute-start | bytes 368648 | tf_op jit(solution)/shard_map/ppermute | solution.py:44
  21.4 0.9 collective-permute-start.14
  22.3 6.9 %collective-permute-done.6 = bf16[3,80,384]{2,1,0:T(8,128)(2,1)S(1)} collective-permute-done((bf16[3,80,384]{2,1,0:T(8,128)(2,1)S(1)}, bf16[3,80,384]{2,1,0:T(8,128)(2,1)S(1)}, u32[]{:S(2)}, u32[]{:S(2)}) %collective-permute-start.6) | collective-permute-done | bytes 184352 | tf_op jit(solution)/shard_map/ppermute | solution.py:44
  29.2 2.7 %collective-permute-start.7 = (bf16[1,3,80,384]{3,2,1,0:T(8,128)(2,1)S(1)}, bf16[1,3,80,384]{3,2,1,0:T(8,128)(2,1)S(1)}, u32[]{:S(2)}, u32[]{:S(2)}) collective-permute-start(bf16[1,3,80,384]{3,2,1,0:T(8,128)(2,1)S(1)} %bitcast.62), channel_id=1, source_target_pairs={{0,192},{4,196},{8,200},{12,204},{16,208},{20,212},{24,216},{28,22... | collective-permute-start | bytes 552968 | tf_op jit(solution)/shard_map/ppermute | solution.py:44
  32.3 3.0 %collective-permute-done.7 = bf16[1,3,80,384]{3,2,1,0:T(8,128)(2,1)S(1)} collective-permute-done((bf16[1,3,80,384]{3,2,1,0:T(8,128)(2,1)S(1)}, bf16[1,3,80,384]{3,2,1,0:T(8,128)(2,1)S(1)}, u32[]{:S(2)}, u32[]{:S(2)}) %collective-permute-start.7) | collective-permute-done | bytes 184352 | tf_op jit(solution)/shard_map/ppermute | solution.py:44
  35.6 2.1 collective-permute-done.21
  37.7 2.7 %collective-permute-start.22 = (bf16[4,3,80,256]{3,2,1,0:T(8,128)(2,1)S(1)}, bf16[4,3,80,256]{3,2,1,0:T(8,128)(2,1)S(1)}, u32[]{:S(2)}, u32[]{:S(2)}) collective-permute-start(bf16[4,3,80,256]{3,2,1,0:T(8,128)(2,1)S(1)} %pad_maximum_fusion.7), channel_id=1, source_target_pairs={{0,192},{4,196},{8,200},{12,204},{16,208},{20,212},{24,216},{28,22... | collective-permute-start | bytes 1474568 | tf_op jit(solution)/shard_map/ppermute | solution.py:44
  40.5 2.1 collective-permute-done.1
  42.6 0.3 collective-permute-start.2
  43.1 2.6 %collective-permute-start.9 = (bf16[4,3,80,384]{3,2,1,0:T(8,128)(2,1)S(1)}, bf16[4,3,80,384]{3,2,1,0:T(8,128)(2,1)S(1)}, u32[]{:S(2)}, u32[]{:S(2)}) collective-permute-start(bf16[4,3,80,384]{3,2,1,0:T(8,128)(2,1)S(1)} %pad_maximum_fusion.5), channel_id=1, source_target_pairs={{0,48},{4,52},{8,56},{12,60},{16,32},{20,36},{24,40},{28,44},{32,1... | collective-permute-start | bytes 2211848 | tf_op jit(solution)/shard_map/ppermute | solution.py:44
  45.7 1.4 collective-permute-done.15
  47.2 7.1 %collective-permute-start.16 = (bf16[8,3,80,256]{3,2,1,0:T(8,128)(2,1)S(1)}, bf16[8,3,80,256]{3,2,1,0:T(8,128)(2,1)S(1)}, u32[]{:S(2)}, u32[]{:S(2)}) collective-permute-start(bf16[8,3,80,256]{3,2,1,0:T(8,128)(2,1)S(1)} %pad_maximum_fusion.2.refs_0_), channel_id=1, source_target_pairs={{0,4},{4,0},{8,12},{12,8},{16,20},{20,16},{24,28},{28,24},{32,36},... | collective-permute-start | bytes 2949128 | tf_op jit(solution)/shard_map/ppermute | solution.py:44
  54.3 2.4 %collective-permute-start.17 = (bf16[8,3,80,256]{3,2,1,0:T(8,128)(2,1)S(1)}, bf16[8,3,80,256]{3,2,1,0:T(8,128)(2,1)}, u32[]{:S(2)}, u32[]{:S(2)}) collective-permute-start(bf16[8,3,80,256]{3,2,1,0:T(8,128)(2,1)S(1)} %pad_maximum_fusion.2.refs_0_), channel_id=1, source_target_pairs={{0,192},{4,196},{8,200},{12,204},{16,208},{20,212},{24,216},{28,22... | collective-permute-start | bytes 2949128 | tf_op jit(solution)/shard_map/ppermute | solution.py:44
  56.8 1.7 collective-permute-start.24
  58.5 2.4 %collective-permute-done.2 = bf16[4,3,80,384]{3,2,1,0:T(8,128)(2,1)S(1)} collective-permute-done((bf16[4,3,80,384]{3,2,1,0:T(8,128)(2,1)S(1)}, bf16[4,3,80,384]{3,2,1,0:T(8,128)(2,1)S(1)}, u32[]{:S(2)}, u32[]{:S(2)}) %collective-permute-start.2) | collective-permute-done | bytes 737312 | tf_op jit(solution)/shard_map/ppermute | solution.py:44
  60.9 0.2 pad_maximum_fusion.refs_0_
  61.2 1.1 collective-permute-start.4
  62.2 1.3 pad_maximum_fusion.1.refs_4_
  63.6 8.6 %collective-permute-start.23 = (bf16[8,3,80,256]{3,2,1,0:T(8,128)(2,1)S(1)}, bf16[8,3,80,256]{3,2,1,0:T(8,128)(2,1)}, u32[]{:S(2)}, u32[]{:S(2)}) collective-permute-start(bf16[8,3,80,256]{3,2,1,0:T(8,128)(2,1)S(1)} %pad_maximum_fusion.3.refs_4_), channel_id=1, source_target_pairs={{0,4},{4,0},{8,12},{12,8},{16,20},{20,16},{24,28},{28,24},{32,36},... | collective-permute-start | bytes 2949128 | tf_op jit(solution)/shard_map/ppermute | solution.py:44
  72.2 6.8 %collective-permute-done.17.refs_2_ = bf16[8,3,80,256]{3,2,1,0:T(8,128)(2,1)} collective-permute-done((bf16[8,3,80,256]{3,2,1,0:T(8,128)(2,1)S(1)}, bf16[8,3,80,256]{3,2,1,0:T(8,128)(2,1)}, u32[]{:S(2)}, u32[]{:S(2)}) %collective-permute-start.17) | collective-permute-done | bytes 983072 | tf_op jit(solution)/shard_map/ppermute | solution.py:44
  78.9 0.9 collective-permute-start.18
  79.8 2.2 collective-permute-done.24.refs_6_
  82.0 4.5 %collective-permute-start.25 = (bf16[8,3,80,256]{3,2,1,0:T(8,128)(2,1)}, bf16[8,3,80,256]{3,2,1,0:T(8,128)(2,1)}, u32[]{:S(2)}, u32[]{:S(2)}) collective-permute-start(bf16[8,3,80,256]{3,2,1,0:T(8,128)(2,1)} %collective-permute-done.24.refs_6_), channel_id=1, source_target_pairs={{0,4},{4,0},{8,12},{12,8},{16,20},{20,16},{24,28},{28,24},{32,36},... | collective-permute-start | bytes 2949128 | tf_op jit(solution)/shard_map/ppermute | solution.py:44
  86.5 0.2 convert_element_type.37
  86.8 2.0 collective-permute-done.4.refs_2_
  88.8 8.9 %collective-permute-start.10 = (bf16[8,3,80,384]{3,2,1,0:T(8,128)(2,1)}, bf16[8,3,80,384]{3,2,1,0:T(8,128)(2,1)}, u32[]{:S(2)}, u32[]{:S(2)}) collective-permute-start(bf16[8,3,80,384]{3,2,1,0:T(8,128)(2,1)} %pad_maximum_fusion.1.refs_4_), channel_id=1, source_target_pairs={{0,4},{4,0},{8,12},{12,8},{16,20},{20,16},{24,28},{28,24},{32,36},... | collective-permute-start | bytes 4423688 | tf_op jit(solution)/shard_map/ppermute | solution.py:44
  97.8 0.7 collective-permute-start.12
  98.6 0.1 copy-done.8
  98.7 4.0 %shard_map.70.weight = bf16[3,5120,256]{2,1,0:T(8,128)(2,1)S(1)} custom-call(s32[5]{0:T(128)S(1)} %stack.23.place, bf16[8,3,80,256]{3,2,1,0:T(8,128)(2,1)} %copy-done.2, bf16[8,3,80,256]{3,2,1,0:T(8,128)(2,1)} %copy-done.7, bf16[8,3,80,256]{3,2,1,0:T(8,128)(2,1)} %collective-permute-done.17.refs_2_, bf16[8,3,80,256]{3,2,1,0:T(8,128)(2,1)} %copy-done.8, ...), custom_call_target="tpu_custom_call" | custom-call | bytes 15728640 | tf_op jit(solution)/shard_map/pallas_call | solution.py:84
  102.7 3.0 %copy-done = bf16[3,5120,256]{2,1,0:T(8,128)(2,1)} copy-done((bf16[3,5120,256]{2,1,0:T(8,128)(2,1)}, bf16[3,5120,256]{2,1,0:T(8,128)(2,1)S(1)}, u32[]{:S(2)}) %copy-start) | copy-done | bytes 7864344
  105.7 30.8 %all-gather.2.cloned.1.call-done.tokens = bf16[640,5120]{1,0:T(8,128)(2,1)} async-done(((bf16[640,1280]{1,0:T(8,128)(2,1)}), bf16[640,5120]{1,0:T(8,128)(2,1)}) %all-gather.2.cloned.1.call-update) | async-done | bytes 6553616 | tf_op jit(solution)/shard_map/all_gather | solution.py:243
  136.5 11.3 %shard_map.71 = bf16[3,640,256]{2,1,0:T(8,128)(2,1)S(1)} custom-call(bf16[640,5120]{1,0:T(8,128)(2,1)} %all-gather.2.cloned.1.call-done.tokens, bf16[3,5120,256]{2,1,0:T(8,128)(2,1)} %copy-done), custom_call_target="tpu_custom_call" | custom-call | flops 5033164800 | bytes 15400960 | tf_op jit(solution)/shard_map/pallas_call | solution.py:152
  147.8 0.2 reshape.172
  148.0 0.2 copy.60
  148.3 1.6 copy.61
  150.0 12.1 %all-to-all-start = ((bf16[64,61,128]{2,1,0:T(8,128)(2,1)}), bf16[64,61,128]{2,1,0:T(8,128)(2,1)S(1)}, u32[]{:S(2)}, u32[]{:S(2)}) async-start(bf16[64,61,128]{2,1,0:T(8,128)(2,1)} %copy.61), calls=%async_computation | async-start | bytes 2097152 | tf_op jit(solution)/shard_map/all_to_all | solution.py:203
  162.2 0.7 broadcast_subtract_fusion
  162.9 1.1 iota_compare_fusion.2
  164.0 5.0 %shard_map.68.weight = bf16[3,5120,384]{2,1,0:T(8,128)(2,1)S(1)} custom-call(s32[5]{0:T(128)S(1)} %stack.23.place, bf16[8,3,80,384]{3,2,1,0:T(8,128)(2,1)} %copy-done.1, bf16[8,3,80,384]{3,2,1,0:T(8,128)(2,1)} %collective-permute-done.3.refs_1_, bf16[8,3,80,384]{3,2,1,0:T(8,128)(2,1)} %collective-permute-done.4.refs_2_, ...), custom_call_target="tpu_custom_call" | custom-call | bytes 23592960 | tf_op jit(solution)/shard_map/pallas_call | solution.py:84
  169.0 12.7 %shard_map.69 = bf16[3,640,384]{2,1,0:T(8,128)(2,1)S(1)} custom-call(bf16[640,5120]{1,0:T(8,128)(2,1)} %all-gather.2.cloned.1.call-done.tokens, bf16[3,5120,384]{2,1,0:T(8,128)(2,1)S(1)} %shard_map.68.weight), custom_call_target="tpu_custom_call" | custom-call | flops 7549747200 | bytes 19824640 | tf_op jit(solution)/shard_map/pallas_call | solution.py:152
  181.7 0.1 fusion.30
  181.9 0.3 copy.54
  182.2 0.3 copy.55
  182.4 0.3 copy.56
  182.7 3.5 %all-to-all-done = bf16[64,61,128]{2,1,0:T(8,128)(2,1)S(1)} async-done(((bf16[64,61,128]{2,1,0:T(8,128)(2,1)}), bf16[64,61,128]{2,1,0:T(8,128)(2,1)S(1)}, u32[]{:S(2)}, u32[]{:S(2)}) %all-to-all-start) | async-done | bytes 999456 | tf_op jit(solution)/shard_map/all_to_all | solution.py:203
  186.1 0.6 copy.62
  186.9 0.2 or_and_fusion
  187.1 0.3 fusion.15
  187.4 0.8 copy-done.16
  188.2 0.2 fusion.32
  188.5 2.4 %convolution_convert_fusion = bf16[2,10,128,64]{2,3,1,0:T(8,128)(2,1)} fusion(bf16[64,3,2,10,128]{4,0,3,2,1:T(8,128)(2,1)S(1)} %bitcast.78, f32[2,10,64]{2,1,0:T(8,128)S(1)} %fusion.32, f32[2,10,64,64]{2,3,1,0:T(8,128)} %copy-done.16), kind=kOutput, calls=%fused_computation.25 | convolution fusion | flops 21382464 | bytes 1982464 | tf_op jit(solution)/shard_map/hsde,ehsc->dhsc/dot_general | solution.py:219
  190.9 1.9 copy.65
  192.8 9.3 %all-to-all-start.1 = ((bf16[64,20,128]{2,1,0:T(8,128)(2,1)}), bf16[64,20,128]{2,1,0:T(8,128)(2,1)S(1)}, u32[]{:S(2)}, u32[]{:S(2)}) async-start(bf16[64,20,128]{2,1,0:T(8,128)(2,1)} %copy.65), calls=%async_computation.1 | async-start | bytes 786432 | tf_op jit(solution)/shard_map/all_to_all | solution.py:221
  202.2 2.5 %fusion.31 = f32[3,640]{1,0:T(4,128)S(1)} fusion(s32[3,640]{1,0:T(4,128)S(1)} %copy-done.14, s32[640]{0:T(1024)S(1)} %copy-done.12, pred[640,640]{0,1:T(8,128)(4,1)S(1)} %copy-done.10, pred[640,640]{0,1:T(8,128)(4,1)S(1)} %copy-done.9, bf16[640,3,128]{0,2,1:T(8,128)(2,1)S(1)} %bitcast.80, bf16[640,3,128]{0,2,1:T(8,128)(2,1)S(1)} %bitcast.82), kind=kOutput, calls=%fused_computation.64 | convolution fusion | flops 323175040 | bytes 1820160 | tf_op jit(solution)/shard_map/sub | solution.py:187
  204.7 2.9 %fusion.13 = bf16[3,128,640]{2,1,0:T(8,128)(2,1)S(1)} fusion(bf16[640,3,128]{0,2,1:T(8,128)(2,1)S(1)} %bitcast.79, f32[3,640]{1,0:T(4,128)S(1)} %fusion.31, s32[3,640]{1,0:T(4,128)S(1)} %copy-done.14, s32[640]{0:T(1024)S(1)} %copy-done.12, pred[640,640]{0,1:T(8,128)(4,1)S(1)} %copy-done.10, pred[640,640]{0,1:T(8,128)(4,1)S(1)} %copy-done.9, ...), kind=kOutput, calls=%fused_computation.21 | convolution fusion | flops 639224320 | bytes 2803200 | tf_op jit(solution)/shard_map/hqk,khc->qhc/dot_general | solution.py:189
  207.6 1.0 copy.68
  208.6 8.8 %all-to-all-done.1 = bf16[64,20,128]{2,1,0:T(8,128)(2,1)S(1)} async-done(((bf16[64,20,128]{2,1,0:T(8,128)(2,1)}), bf16[64,20,128]{2,1,0:T(8,128)(2,1)S(1)}, u32[]{:S(2)}, u32[]{:S(2)}) %all-to-all-start.1) | async-done | bytes 327712 | tf_op jit(solution)/shard_map/all_to_all | solution.py:221
  217.5 0.3 copy.67
  217.9 0.8 copy.76
  (76 shorter events, 1.8 us)
Async XLA Ops:
  7.2 0.9 copy-start.6
  7.2 9.8 %copy-start.4 = (bf16[80,3,384]{2,0,1:T(8,128)(2,1)S(1)}, bf16[80,3,384]{2,0,1:T(8,128)(2,1)}, u32[]{:S(2)}) copy-start(bf16[80,3,384]{2,0,1:T(8,128)(2,1)} %param.6) | copy-start | bytes 552964
  7.2 129.3 %all-gather.2.cloned.1.call-start = ((), (), s32[]{:S(2)}) async-start(), calls=%async_computation.2 | async-start | bytes 8192000 | tf_op jit(solution)/shard_map/all_gather | solution.py:243
  8.1 10.3 %collective-permute-start.19 = (bf16[3,80,256]{2,1,0:T(8,128)(2,1)S(1)}, bf16[3,80,256]{2,1,0:T(8,128)(2,1)S(1)}, u32[]{:S(2)}, u32[]{:S(2)}) collective-permute-start(bf16[3,80,256]{2,1,0:T(8,128)(2,1)S(1)} %bitcast.68), channel_id=1, source_target_pairs={{0,8},{4,12},{8,0},{12,4},{16,24},{20,28},{24,16},{28,20},{32,40},... | collective-permute-start | bytes 368648 | tf_op jit(solution)/shard_map/ppermute | solution.py:44
  15.8 5.5 %collective-permute-start.13 = (bf16[1,3,80,256]{3,2,1,0:T(8,128)(2,1)S(1)}, bf16[1,3,80,256]{3,2,1,0:T(8,128)(2,1)S(1)}, u32[]{:S(2)}, u32[]{:S(2)}) collective-permute-start(bf16[1,3,80,256]{3,2,1,0:T(8,128)(2,1)S(1)} %bitcast.69), channel_id=1, source_target_pairs={{0,16},{4,20},{8,24},{12,28},{16,0},{20,4},{24,8},{28,12},{32,48},... | collective-permute-start | bytes 368648 | tf_op jit(solution)/shard_map/ppermute | solution.py:44
  17.0 12.2 %collective-permute-start.6 = (bf16[3,80,384]{2,1,0:T(8,128)(2,1)S(1)}, bf16[3,80,384]{2,1,0:T(8,128)(2,1)S(1)}, u32[]{:S(2)}, u32[]{:S(2)}) collective-permute-start(bf16[3,80,384]{2,1,0:T(8,128)(2,1)S(1)} %bitcast.57), channel_id=1, source_target_pairs={{0,8},{4,12},{8,0},{12,4},{16,24},{20,28},{24,16},{28,20},{32,40},... | collective-permute-start | bytes 552968 | tf_op jit(solution)/shard_map/ppermute | solution.py:44
  17.1 14.9 %collective-permute-start = (bf16[1,3,80,384]{3,2,1,0:T(8,128)(2,1)S(1)}, bf16[1,3,80,384]{3,2,1,0:T(8,128)(2,1)S(1)}, u32[]{:S(2)}, u32[]{:S(2)}) collective-permute-start(bf16[1,3,80,384]{3,2,1,0:T(8,128)(2,1)S(1)} %bitcast.58), channel_id=1, source_target_pairs={{0,64},{4,68},{8,72},{12,76},{16,80},{20,84},{24,88},{28,92},{32,9... | collective-permute-start | bytes 552968 | tf_op jit(solution)/shard_map/ppermute | solution.py:44
  18.4 13.7 %collective-permute-start.20 = (bf16[1,3,80,256]{3,2,1,0:T(8,128)(2,1)S(1)}, bf16[1,3,80,256]{3,2,1,0:T(8,128)(2,1)S(1)}, u32[]{:S(2)}, u32[]{:S(2)}) collective-permute-start(bf16[1,3,80,256]{3,2,1,0:T(8,128)(2,1)S(1)} %bitcast.73), channel_id=1, source_target_pairs={{0,48},{4,52},{8,56},{12,60},{16,32},{20,36},{24,40},{28,44},{32,1... | collective-permute-start | bytes 368648 | tf_op jit(solution)/shard_map/ppermute | solution.py:44
  21.4 14.1 %collective-permute-start.14 = (bf16[2,3,80,256]{3,2,1,0:T(8,128)(2,1)S(1)}, bf16[2,3,80,256]{3,2,1,0:T(8,128)(2,1)S(1)}, u32[]{:S(2)}, u32[]{:S(2)}) collective-permute-start(bf16[2,3,80,256]{3,2,1,0:T(8,128)(2,1)S(1)} %pad_maximum_fusion.10), channel_id=1, source_target_pairs={{0,48},{4,52},{8,56},{12,60},{16,32},{20,36},{24,40},{28,44},{32,1... | collective-permute-start | bytes 737288 | tf_op jit(solution)/shard_map/ppermute | solution.py:44
  29.2 6.1 %collective-permute-start.7 = (bf16[1,3,80,384]{3,2,1,0:T(8,128)(2,1)S(1)}, bf16[1,3,80,384]{3,2,1,0:T(8,128)(2,1)S(1)}, u32[]{:S(2)}, u32[]{:S(2)}) collective-permute-start(bf16[1,3,80,384]{3,2,1,0:T(8,128)(2,1)S(1)} %bitcast.62), channel_id=1, source_target_pairs={{0,192},{4,196},{8,200},{12,204},{16,208},{20,212},{24,216},{28,22... | collective-permute-start | bytes 552968 | tf_op jit(solution)/shard_map/ppermute | solution.py:44
  32.0 10.5 %collective-permute-start.1 = (bf16[2,3,80,384]{3,2,1,0:T(8,128)(2,1)S(1)}, bf16[2,3,80,384]{3,2,1,0:T(8,128)(2,1)S(1)}, u32[]{:S(2)}, u32[]{:S(2)}) collective-permute-start(bf16[2,3,80,384]{3,2,1,0:T(8,128)(2,1)S(1)} %pad_maximum_fusion.8), channel_id=1, source_target_pairs={{0,192},{4,196},{8,200},{12,204},{16,208},{20,212},{24,216},{28,22... | collective-permute-start | bytes 1105928 | tf_op jit(solution)/shard_map/ppermute | solution.py:44
  32.2 5.5 %collective-permute-start.21 = (bf16[2,3,80,256]{3,2,1,0:T(8,128)(2,1)S(1)}, bf16[2,3,80,256]{3,2,1,0:T(8,128)(2,1)S(1)}, u32[]{:S(2)}, u32[]{:S(2)}) collective-permute-start(bf16[2,3,80,256]{3,2,1,0:T(8,128)(2,1)S(1)} %pad_maximum_fusion.11), channel_id=1, source_target_pairs={{0,64},{4,68},{8,72},{12,76},{16,80},{20,84},{24,88},{28,92},{32,9... | collective-permute-start | bytes 737288 | tf_op jit(solution)/shard_map/ppermute | solution.py:44
  35.3 7.6 %collective-permute-start.8 = (bf16[2,3,80,384]{3,2,1,0:T(8,128)(2,1)S(1)}, bf16[2,3,80,384]{3,2,1,0:T(8,128)(2,1)S(1)}, u32[]{:S(2)}, u32[]{:S(2)}) collective-permute-start(bf16[2,3,80,384]{3,2,1,0:T(8,128)(2,1)S(1)} %pad_maximum_fusion.9), channel_id=1, source_target_pairs={{0,16},{4,20},{8,24},{12,28},{16,0},{20,4},{24,8},{28,12},{32,48},... | collective-permute-start | bytes 1105928 | tf_op jit(solution)/shard_map/ppermute | solution.py:44
  35.5 11.6 %collective-permute-start.15 = (bf16[4,3,80,256]{3,2,1,0:T(8,128)(2,1)S(1)}, bf16[4,3,80,256]{3,2,1,0:T(8,128)(2,1)S(1)}, u32[]{:S(2)}, u32[]{:S(2)}) collective-permute-start(bf16[4,3,80,256]{3,2,1,0:T(8,128)(2,1)S(1)} %pad_maximum_fusion.6), channel_id=1, source_target_pairs={{0,64},{4,68},{8,72},{12,76},{16,80},{20,84},{24,88},{28,92},{32,9... | collective-permute-start | bytes 1474568 | tf_op jit(solution)/shard_map/ppermute | solution.py:44
  37.7 18.9 %collective-permute-start.22 = (bf16[4,3,80,256]{3,2,1,0:T(8,128)(2,1)S(1)}, bf16[4,3,80,256]{3,2,1,0:T(8,128)(2,1)S(1)}, u32[]{:S(2)}, u32[]{:S(2)}) collective-permute-start(bf16[4,3,80,256]{3,2,1,0:T(8,128)(2,1)S(1)} %pad_maximum_fusion.7), channel_id=1, source_target_pairs={{0,192},{4,196},{8,200},{12,204},{16,208},{20,212},{24,216},{28,22... | collective-permute-start | bytes 1474568 | tf_op jit(solution)/shard_map/ppermute | solution.py:44
  42.6 18.3 %collective-permute-start.2 = (bf16[4,3,80,384]{3,2,1,0:T(8,128)(2,1)S(1)}, bf16[4,3,80,384]{3,2,1,0:T(8,128)(2,1)S(1)}, u32[]{:S(2)}, u32[]{:S(2)}) collective-permute-start(bf16[4,3,80,384]{3,2,1,0:T(8,128)(2,1)S(1)} %pad_maximum_fusion.4), channel_id=1, source_target_pairs={{0,16},{4,20},{8,24},{12,28},{16,0},{20,4},{24,8},{28,12},{32,48},... | collective-permute-start | bytes 2211848 | tf_op jit(solution)/shard_map/ppermute | solution.py:44
  43.1 17.9 %copy-start.5 = (bf16[80,3,384]{2,0,1:T(8,128)(2,1)S(1)}, bf16[80,3,384]{2,0,1:T(8,128)(2,1)}, u32[]{:S(2)}) copy-start(bf16[80,3,384]{2,0,1:T(8,128)(2,1)} %param.6) | copy-start | bytes 552964
  43.1 19.1 %collective-permute-start.9 = (bf16[4,3,80,384]{3,2,1,0:T(8,128)(2,1)S(1)}, bf16[4,3,80,384]{3,2,1,0:T(8,128)(2,1)S(1)}, u32[]{:S(2)}, u32[]{:S(2)}) collective-permute-start(bf16[4,3,80,384]{3,2,1,0:T(8,128)(2,1)S(1)} %pad_maximum_fusion.5), channel_id=1, source_target_pairs={{0,48},{4,52},{8,56},{12,60},{16,32},{20,36},{24,40},{28,44},{32,1... | collective-permute-start | bytes 2211848 | tf_op jit(solution)/shard_map/ppermute | solution.py:44
  47.2 13.9 %copy-start.2 = (bf16[8,3,80,256]{3,2,1,0:T(8,128)(2,1)}, bf16[8,3,80,256]{3,2,1,0:T(8,128)(2,1)S(1)}, u32[]{:S(2)}) copy-start(bf16[8,3,80,256]{3,2,1,0:T(8,128)(2,1)S(1)} %pad_maximum_fusion.2.refs_0_) | copy-start | bytes 2949124
  47.2 16.3 %collective-permute-start.16 = (bf16[8,3,80,256]{3,2,1,0:T(8,128)(2,1)S(1)}, bf16[8,3,80,256]{3,2,1,0:T(8,128)(2,1)S(1)}, u32[]{:S(2)}, u32[]{:S(2)}) collective-permute-start(bf16[8,3,80,256]{3,2,1,0:T(8,128)(2,1)S(1)} %pad_maximum_fusion.2.refs_0_), channel_id=1, source_target_pairs={{0,4},{4,0},{8,12},{12,8},{16,20},{20,16},{24,28},{28,24},{32,36},... | collective-permute-start | bytes 2949128 | tf_op jit(solution)/shard_map/ppermute | solution.py:44
  54.3 24.6 %collective-permute-start.17 = (bf16[8,3,80,256]{3,2,1,0:T(8,128)(2,1)S(1)}, bf16[8,3,80,256]{3,2,1,0:T(8,128)(2,1)}, u32[]{:S(2)}, u32[]{:S(2)}) collective-permute-start(bf16[8,3,80,256]{3,2,1,0:T(8,128)(2,1)S(1)} %pad_maximum_fusion.2.refs_0_), channel_id=1, source_target_pairs={{0,192},{4,196},{8,200},{12,204},{16,208},{20,212},{24,216},{28,22... | collective-permute-start | bytes 2949128 | tf_op jit(solution)/shard_map/ppermute | solution.py:44
  56.8 6.8 %copy-start.3 = (bf16[8,3,80,256]{3,2,1,0:T(8,128)(2,1)}, bf16[8,3,80,256]{3,2,1,0:T(8,128)(2,1)S(1)}, u32[]{:S(2)}) copy-start(bf16[8,3,80,256]{3,2,1,0:T(8,128)(2,1)S(1)} %pad_maximum_fusion.3.refs_4_) | copy-start | bytes 2949124
  56.8 25.2 %collective-permute-start.24 = (bf16[8,3,80,256]{3,2,1,0:T(8,128)(2,1)S(1)}, bf16[8,3,80,256]{3,2,1,0:T(8,128)(2,1)}, u32[]{:S(2)}, u32[]{:S(2)}) collective-permute-start(bf16[8,3,80,256]{3,2,1,0:T(8,128)(2,1)S(1)} %pad_maximum_fusion.3.refs_4_), channel_id=1, source_target_pairs={{0,16},{4,20},{8,24},{12,28},{16,0},{20,4},{24,8},{28,12},{32,48},... | collective-permute-start | bytes 2949128 | tf_op jit(solution)/shard_map/ppermute | solution.py:44
  61.1 41.5 %copy-start.1 = (bf16[8,3,80,384]{3,2,1,0:T(8,128)(2,1)}, bf16[8,3,80,384]{3,2,1,0:T(8,128)(2,1)S(1)}, u32[]{:S(2)}) copy-start(bf16[8,3,80,384]{3,2,1,0:T(8,128)(2,1)S(1)} %pad_maximum_fusion.refs_0_) | copy-start | bytes 4423684
  61.1 25.3 %copy-start.13 = (s32[1,640]{1,0:T(1,128)S(1)}, s32[1,640]{1,0:T(1,128)}, u32[]{:S(2)}) copy-start(s32[1,640]{1,0:T(1,128)} %param.8) | copy-start | bytes 7684
  61.2 27.7 %collective-permute-start.4 = (bf16[8,3,80,384]{3,2,1,0:T(8,128)(2,1)S(1)}, bf16[8,3,80,384]{3,2,1,0:T(8,128)(2,1)}, u32[]{:S(2)}, u32[]{:S(2)}) collective-permute-start(bf16[8,3,80,384]{3,2,1,0:T(8,128)(2,1)S(1)} %pad_maximum_fusion.refs_0_), channel_id=1, source_target_pairs={{0,48},{4,52},{8,56},{12,60},{16,32},{20,36},{24,40},{28,44},{32,1... | collective-permute-start | bytes 4423688 | tf_op jit(solution)/shard_map/ppermute | solution.py:44
  63.5 34.3 %collective-permute-start.11 = (bf16[8,3,80,384]{3,2,1,0:T(8,128)(2,1)}, bf16[8,3,80,384]{3,2,1,0:T(8,128)(2,1)}, u32[]{:S(2)}, u32[]{:S(2)}) collective-permute-start(bf16[8,3,80,384]{3,2,1,0:T(8,128)(2,1)} %pad_maximum_fusion.1.refs_4_), channel_id=1, source_target_pairs={{0,64},{4,68},{8,72},{12,76},{16,80},{20,84},{24,88},{28,92},{32,9... | collective-permute-start | bytes 4423688 | tf_op jit(solution)/shard_map/ppermute | solution.py:44
  63.5 18.4 %copy-start.7 = (bf16[8,3,80,256]{3,2,1,0:T(8,128)(2,1)}, bf16[8,3,80,256]{3,2,1,0:T(8,128)(2,1)S(1)}, u32[]{:S(2)}) copy-start(bf16[8,3,80,256]{3,2,1,0:T(8,128)(2,1)S(1)} %collective-permute-done.16.refs_1_) | copy-start | bytes 2949124
  63.6 23.2 %collective-permute-start.23 = (bf16[8,3,80,256]{3,2,1,0:T(8,128)(2,1)S(1)}, bf16[8,3,80,256]{3,2,1,0:T(8,128)(2,1)}, u32[]{:S(2)}, u32[]{:S(2)}) collective-permute-start(bf16[8,3,80,256]{3,2,1,0:T(8,128)(2,1)S(1)} %pad_maximum_fusion.3.refs_4_), channel_id=1, source_target_pairs={{0,4},{4,0},{8,12},{12,8},{16,20},{20,16},{24,28},{28,24},{32,36},... | collective-permute-start | bytes 2949128 | tf_op jit(solution)/shard_map/ppermute | solution.py:44
  78.9 18.8 %collective-permute-start.18 = (bf16[8,3,80,256]{3,2,1,0:T(8,128)(2,1)}, bf16[8,3,80,256]{3,2,1,0:T(8,128)(2,1)S(1)}, u32[]{:S(2)}, u32[]{:S(2)}) collective-permute-start(bf16[8,3,80,256]{3,2,1,0:T(8,128)(2,1)} %collective-permute-done.17.refs_2_), channel_id=1, source_target_pairs={{0,4},{4,0},{8,12},{12,8},{16,20},{20,16},{24,28},{28,24},{32,36},... | collective-permute-start | bytes 2949128 | tf_op jit(solution)/shard_map/ppermute | solution.py:44
  82.0 16.6 %collective-permute-start.25 = (bf16[8,3,80,256]{3,2,1,0:T(8,128)(2,1)}, bf16[8,3,80,256]{3,2,1,0:T(8,128)(2,1)}, u32[]{:S(2)}, u32[]{:S(2)}) collective-permute-start(bf16[8,3,80,256]{3,2,1,0:T(8,128)(2,1)} %collective-permute-done.24.refs_6_), channel_id=1, source_target_pairs={{0,4},{4,0},{8,12},{12,8},{16,20},{20,16},{24,28},{28,24},{32,36},... | collective-permute-start | bytes 2949128 | tf_op jit(solution)/shard_map/ppermute | solution.py:44
  86.8 77.2 %collective-permute-start.3 = (bf16[8,3,80,384]{3,2,1,0:T(8,128)(2,1)S(1)}, bf16[8,3,80,384]{3,2,1,0:T(8,128)(2,1)}, u32[]{:S(2)}, u32[]{:S(2)}) collective-permute-start(bf16[8,3,80,384]{3,2,1,0:T(8,128)(2,1)S(1)} %pad_maximum_fusion.refs_0_), channel_id=1, source_target_pairs={{0,4},{4,0},{8,12},{12,8},{16,20},{20,16},{24,28},{28,24},{32,36},... | collective-permute-start | bytes 4423688 | tf_op jit(solution)/shard_map/ppermute | solution.py:44
  88.8 75.2 %collective-permute-start.10 = (bf16[8,3,80,384]{3,2,1,0:T(8,128)(2,1)}, bf16[8,3,80,384]{3,2,1,0:T(8,128)(2,1)}, u32[]{:S(2)}, u32[]{:S(2)}) collective-permute-start(bf16[8,3,80,384]{3,2,1,0:T(8,128)(2,1)} %pad_maximum_fusion.1.refs_4_), channel_id=1, source_target_pairs={{0,4},{4,0},{8,12},{12,8},{16,20},{20,16},{24,28},{28,24},{32,36},... | collective-permute-start | bytes 4423688 | tf_op jit(solution)/shard_map/ppermute | solution.py:44
  97.7 1.0 copy-start.8
  97.7 66.3 %collective-permute-start.5 = (bf16[8,3,80,384]{3,2,1,0:T(8,128)(2,1)}, bf16[8,3,80,384]{3,2,1,0:T(8,128)(2,1)}, u32[]{:S(2)}, u32[]{:S(2)}) collective-permute-start(bf16[8,3,80,384]{3,2,1,0:T(8,128)(2,1)} %collective-permute-done.4.refs_2_), channel_id=1, source_target_pairs={{0,4},{4,0},{8,12},{12,8},{16,20},{20,16},{24,28},{28,24},{32,36},... | collective-permute-start | bytes 4423688 | tf_op jit(solution)/shard_map/ppermute | solution.py:44
  97.8 66.2 %collective-permute-start.12 = (bf16[8,3,80,384]{3,2,1,0:T(8,128)(2,1)}, bf16[8,3,80,384]{3,2,1,0:T(8,128)(2,1)}, u32[]{:S(2)}, u32[]{:S(2)}) collective-permute-start(bf16[8,3,80,384]{3,2,1,0:T(8,128)(2,1)} %collective-permute-done.11.refs_6_), channel_id=1, source_target_pairs={{0,4},{4,0},{8,12},{12,8},{16,20},{20,16},{24,28},{28,24},{32,36},... | collective-permute-start | bytes 4423688 | tf_op jit(solution)/shard_map/ppermute | solution.py:44
  102.6 3.1 %copy-start = (bf16[3,5120,256]{2,1,0:T(8,128)(2,1)}, bf16[3,5120,256]{2,1,0:T(8,128)(2,1)S(1)}, u32[]{:S(2)}) copy-start(bf16[3,5120,256]{2,1,0:T(8,128)(2,1)S(1)} %shard_map.70.weight) | copy-start | bytes 23592964
  148.3 13.9 %copy-start.15 = (s32[3]{0:T(128)S(1)}, s32[3]{0:T(128)}, u32[]{:S(2)}) copy-start(s32[3]{0:T(128)} %param.9) | copy-start | bytes 40
  150.0 36.1 %all-to-all-start = ((bf16[64,61,128]{2,1,0:T(8,128)(2,1)}), bf16[64,61,128]{2,1,0:T(8,128)(2,1)S(1)}, u32[]{:S(2)}, u32[]{:S(2)}) async-start(bf16[64,61,128]{2,1,0:T(8,128)(2,1)} %copy.61), calls=%async_computation | async-start | bytes 2097152 | tf_op jit(solution)/shard_map/all_to_all | solution.py:203
  162.1 6.9 %copy-start.11 = (s32[640]{0:T(1024)}, s32[640]{0:T(1024)S(1)}, u32[]{:S(2)}) copy-start(s32[640]{0:T(1024)S(1)} %add_select_fusion) | copy-start | bytes 7684
  187.4 0.8 copy-start.16
  188.4 13.7 %copy-start.9 = (pred[640,640]{0,1:T(8,128)(4,1)S(1)}, pred[640,640]{0,1:T(8,128)(4,1)}, u32[]{:S(2)}) copy-start(pred[640,640]{0,1:T(8,128)(4,1)} %get-tuple-element.15) | copy-start | bytes 1228804
  188.4 13.7 %copy-start.10 = (pred[640,640]{0,1:T(8,128)(4,1)S(1)}, pred[640,640]{0,1:T(8,128)(4,1)}, u32[]{:S(2)}) copy-start(pred[640,640]{0,1:T(8,128)(4,1)} %get-tuple-element.16) | copy-start | bytes 1228804
  188.4 13.7 %copy-start.12 = (s32[640]{0:T(1024)S(1)}, s32[640]{0:T(1024)}, u32[]{:S(2)}) copy-start(s32[640]{0:T(1024)} %copy-done.11) | copy-start | bytes 7684
  188.4 13.7 %copy-start.14 = (s32[3,640]{1,0:T(4,128)S(1)}, s32[3,640]{1,0:T(4,128)}, u32[]{:S(2)}) copy-start(s32[3,640]{1,0:T(4,128)} %broadcast_subtract_fusion) | copy-start | bytes 23044
  192.8 24.6 %all-to-all-start.1 = ((bf16[64,20,128]{2,1,0:T(8,128)(2,1)}), bf16[64,20,128]{2,1,0:T(8,128)(2,1)S(1)}, u32[]{:S(2)}, u32[]{:S(2)}) async-start(bf16[64,20,128]{2,1,0:T(8,128)(2,1)} %copy.65), calls=%async_computation.1 | async-start | bytes 786432 | tf_op jit(solution)/shard_map/all_to_all | solution.py:221
Sparse Core Ops, SparseCore 0:
  9.8 126.6 all-gather.1

commit v3 on v1

--- a/solution.py
+++ b/solution.py
@@ -11,7 +11,7 @@
 HD = 128
 BLK = 128
 NY, NX, NH, NC = 4, 4, 2, 2
-CHUNKS = (320, 320)
+NZ = 4
 
 
 def seq_pairs(move):
@@ -36,20 +36,16 @@
     "c": lambda y, x, h, c: (y, x, h, 1 - c),
 }
 FLIPS = {"x1": (0, 1), "x3": (0, 3), "y1": (1, 0), "y3": (3, 0)}
-OWN_ORDERS = (("x1", "x3", "y1", "y3"), ("y1", "y3", "x1", "x3"))
-OTHER_ORDERS = (("x3", "y1", "y3", "x1"), ("y3", "x1", "x3", "y1"))
+OWN_ORDERS = (("x1", "x3", "y1", "y3"), ("x1", "x3", "y3", "y1"))
+OTHER_ORDERS = (("y1", "y3", "x1", "x3"), ("y1", "y3", "x3", "x1"))
 
 
 def swap(value, kind):
     return lax.ppermute(value, "seq", seq_pairs(MOVES[kind]))
 
 
-def double_up(value, order):
-    value = value[None]
-    for kind in order[:-1]:
-        value = jnp.concatenate([value, swap(value, kind)], axis=0)
-    received = swap(value, order[-1])
-    return [value, received]
+def advance(value, kind):
+    return jnp.concatenate([value, swap(value, kind)], axis=0)
 
 
 def place_kernel(orders, place, *refs):
@@ -74,12 +70,14 @@
     pltpu.make_async_copy(out, out, sem).wait()
 
 
-def place_weights(place, own, other, which):
+def place_weights(place, held, received, which):
+    held_swapped = [swap(piece, "c") for piece in held]
+    received_swapped = [swap(piece, "c") for piece in received]
     pieces = []
-    for value, order in ((own, OWN_ORDERS[which]), (other, OTHER_ORDERS[which])):
-        for piece in double_up(value, order):
-            pieces += [piece, swap(piece, "c")]
-    part, cols = own.shape[1:]
+    for group in range(2):
+        pieces += [held[group], held_swapped[group]]
+        pieces += [received[group], received_swapped[group]]
+    part, cols = pieces[0].shape[2:]
     total = NY * NX * NH * NC * part
     return pl.pallas_call(
         functools.partial(place_kernel, (OWN_ORDERS[which], OTHER_ORDERS[which])),
@@ -92,34 +90,248 @@
         cost_estimate=pl.CostEstimate(
             flops=0, bytes_accessed=4 * 3 * total * cols, transcendentals=0
         ),
-    )(place, *pieces)
-
-
-def project_kernel(tokens, weight, out):
-    out[0] = jnp.dot(
-        tokens[...], weight[0], preferred_element_type=jnp.float32
-    ).astype(out.dtype)
-
-
-def project(tokens, weight):
-    rows, total = tokens.shape
+    )(place, *[pltpu.with_memory_space_constraint(piece, pltpu.HBM) for piece in pieces])
+
+
+def send_z(value, pairs):
+    return lax.ppermute(value, "fsdp", pairs)
+
+
+def advance_both(pair, which, step):
+    return [
+        advance(value, orders[which][step])
+        for value, orders in zip(pair, (OWN_ORDERS, OTHER_ORDERS))
+    ]
+
+
+def finish_both(pair, which):
+    return [
+        swap(value, orders[which][3]) for value, orders in zip(pair, (OWN_ORDERS, OTHER_ORDERS))
+    ]
+
+
+def gather_all(tokens, own_strided, own_local):
+    split = own_strided.shape[2]
+    own = jnp.concatenate([own_strided, own_local], axis=2)[None]
+    other = swap(own, "h")
+    tokens, other = lax.optimization_barrier((tokens, other))
+    near = send_z(tokens, [(0, 1), (1, 0), (2, 3), (3, 2)])
+    middle = send_z(tokens, [(1, 2), (2, 1)])
+    pair = [own, other]
+    for step in range(2):
+        pair = advance_both(pair, 0, step)
+    strided = advance_both([value[..., :split] for value in pair], 0, 2)
+    local = [value[..., split:] for value in pair]
+    near, middle, strided, local = lax.optimization_barrier((near, middle, strided, local))
+    across = send_z(near, [(1, 2), (2, 1)])
+    outward = send_z(middle, [(2, 3), (1, 0)])
+    local = advance_both(local, 1, 2)
+    received = finish_both(strided, 0)
+    across, outward, received, local = lax.optimization_barrier(
+        (across, outward, received, local)
+    )
+    far = send_z(across, [(2, 3), (1, 0)])
+    received_local = finish_both(local, 1)
+    gathered = (tokens, near, middle, across, outward, far)
+    return gathered, (strided, received), (local, received_local)
+
+
+def shard_slots(z, f):
+    if f == z:
+        return 0
+    if abs(f - z) == 3:
+        return 5
+    if abs(f - z) == 2:
+        return 3 if z in (1, 2) else 4
+    return 2 if {f, z} == {1, 2} else 1
+
+
+def for_shard(z, f, slots, action):
+    for slot in slots:
+        planes = [plane for plane in range(NZ) if shard_slots(plane, f) == slot]
+        if planes:
+            here = z == planes[0]
+            for plane in planes[1:]:
+                here = here | (z == plane)
+
+            @pl.when(here)
+            def _(slot=slot):
+                action(slot)
+
+
+def early_kernel(place, *refs):
+    tokens, weight = refs[:5], refs[5]
+    acc, held, factor, token_sem, weight_sem = refs[6:]
+    z = place[4]
+    depth = held.shape[2]
+
+    def load(f):
+        rows = pl.ds(pl.multiple_of(f * depth, depth), depth)
+        return pltpu.make_async_copy(
+            weight.at[:, rows, :], factor.at[:, rows, :], weight_sem.at[f]
+        )
+
+    for f in range(NZ):
+        load(f).start()
+        for_shard(
+            z,
+            f,
+            range(5),
+            lambda slot, f=f: pltpu.make_async_copy(
+                tokens[slot], held.at[f], token_sem.at[f]
+            ).start(),
+        )
+    acc[...] = jnp.zeros_like(acc)
+
+    def step(f, carry):
+        load(f).wait()
+
+        @pl.when(jnp.abs(f - z) < NZ - 1)
+        def _():
+            pltpu.make_async_copy(tokens[0], held.at[f], token_sem.at[f]).wait()
+            rows = pl.ds(pl.multiple_of(f * depth, depth), depth)
+            for j in range(3):
+                acc[j] += jnp.dot(
+                    held[f], factor[j, rows, :], preferred_element_type=jnp.float32
+                )
+
+        return carry
+
+    lax.fori_loop(0, NZ, step, 0)
+
+
+def late_kernel(place, far, weight, acc, out, held, factor, token_sem, weight_sem):
+    z = place[4]
+    depth = held.shape[1]
+    last = (z == 0) | (z == NZ - 1)
+    start = pl.multiple_of(jnp.where(z == 0, (NZ - 1) * depth, 0), depth)
+
+    def load(j):
+        return pltpu.make_async_copy(
+            weight.at[j, pl.ds(start, depth), :], factor.at[j], weight_sem.at[j]
+        )
+
+    @pl.when(last)
+    def _():
+        pltpu.make_async_copy(far, held, token_sem).start()
+        for j in range(3):
+            load(j).start()
+        pltpu.make_async_copy(far, held, token_sem).wait()
+
+        def step(j, carry):
+            load(j).wait()
+            term = jnp.dot(held[...], factor[j], preferred_element_type=jnp.float32)
+            out[j] = (acc[j] + term).astype(out.dtype)
+            return carry
+
+        lax.fori_loop(0, 3, step, 0)
+
+    @pl.when(jnp.logical_not(last))
+    def _():
+        out[...] = acc[...].astype(out.dtype)
+
+
+HBM = pl.BlockSpec(memory_space=pltpu.HBM)
+VMEM = pl.BlockSpec(memory_space=pltpu.VMEM)
+SMEM = pl.BlockSpec(memory_space=pltpu.SMEM)
+
+
+def in_hbm(values):
+    return [pltpu.with_memory_space_constraint(value, pltpu.HBM) for value in values]
+
+
+def project_early(place, gathered, weight):
+    rows, depth = gathered[0].shape
+    _, total, cols = weight.shape
+    return pl.pallas_call(
+        early_kernel,
+        out_shape=jax.ShapeDtypeStruct((3, rows, cols), jnp.float32),
+        in_specs=[SMEM] + [HBM] * 6,
+        out_specs=VMEM,
+        scratch_shapes=[
+            pltpu.VMEM((NZ, rows, depth), jnp.bfloat16),
+            pltpu.VMEM((3, total, cols), jnp.bfloat16),
+            pltpu.SemaphoreType.DMA((NZ,)),
+            pltpu.SemaphoreType.DMA((NZ,)),
+        ],
+        compiler_params=pltpu.CompilerParams(vmem_limit_bytes=24 * 1024 * 1024),
+        cost_estimate=pl.CostEstimate(
+            flops=6 * rows * total * cols,
+            bytes_accessed=2 * (rows * total + 3 * total * cols) + 12 * rows * cols,
+            transcendentals=0,
+        ),
+    )(place, *in_hbm(gathered[:5] + (weight,)))
+
+
+def project_late(place, gathered, weight, acc):
+    rows, depth = gathered[0].shape
     cols = weight.shape[2]
     return pl.pallas_call(
+        late_kernel,
+        out_shape=jax.ShapeDtypeStruct((3, rows, cols), jnp.bfloat16),
+        in_specs=[SMEM, HBM, HBM, VMEM],
+        out_specs=VMEM,
+        scratch_shapes=[
+            pltpu.VMEM((rows, depth), jnp.bfloat16),
+            pltpu.VMEM((3, depth, cols), jnp.bfloat16),
+            pltpu.SemaphoreType.DMA,
+            pltpu.SemaphoreType.DMA((3,)),
+        ],
+        compiler_params=pltpu.CompilerParams(vmem_limit_bytes=16 * 1024 * 1024),
+        cost_estimate=pl.CostEstimate(
+            flops=6 * rows * depth * cols,
+            bytes_accessed=2 * (rows * depth + 3 * depth * cols) + 18 * rows * cols,
+            transcendentals=0,
+        ),
+    )(place, *in_hbm((gathered[5], weight)), acc)
+
+
+def project_kernel(place, *refs):
+    tokens, weight = refs[:6], refs[6]
+    out, held, sem = refs[7:]
+    depth = held.shape[1] // NZ
+    for f in range(NZ):
+        cols = held.at[:, pl.ds(f * depth, depth)]
+        for_shard(
+            place[4],
+            f,
+            range(6),
+            lambda slot, f=f, cols=cols: pltpu.make_async_copy(
+                tokens[slot], cols, sem.at[f]
+            ).start(),
+        )
+    for f in range(NZ):
+        cols = held.at[:, pl.ds(f * depth, depth)]
+        pltpu.make_async_copy(tokens[0], cols, sem.at[f]).wait()
+
+    def step(j, carry):
+        out[j] = jnp.dot(
+            held[...], weight[j], preferred_element_type=jnp.float32
+        ).astype(out.dtype)
+        return carry
+
+    lax.fori_loop(0, 3, step, 0)
+
+
+def project_local(place, gathered, weight):
+    rows, depth = gathered[0].shape
+    _, total, cols = weight.shape
+    return pl.pallas_call(
         project_kernel,
-        grid=(3,),
         out_shape=jax.ShapeDtypeStruct((3, rows, cols), jnp.bfloat16),
-        in_specs=[
-            pl.BlockSpec((rows, total), lambda j: (0, 0)),
-            pl.BlockSpec((1, total, cols), lambda j: (j, 0, 0)),
+        in_specs=[SMEM] + [HBM] * 6 + [VMEM],
+        out_specs=VMEM,
+        scratch_shapes=[
+            pltpu.VMEM((rows, total), jnp.bfloat16),
+            pltpu.SemaphoreType.DMA((NZ,)),
         ],
-        out_specs=pl.BlockSpec((1, rows, cols), lambda j: (j, 0, 0)),
-        compiler_params=pltpu.CompilerParams(vmem_limit_bytes=40 * 1024 * 1024),
+        compiler_params=pltpu.CompilerParams(vmem_limit_bytes=20 * 1024 * 1024),
         cost_estimate=pl.CostEstimate(
-            flops=2 * rows * total * 3 * cols,
+            flops=6 * rows * total * cols,
             bytes_accessed=2 * (rows * total + 3 * total * cols + 3 * rows * cols),
             transcendentals=0,
         ),
-    )(tokens, weight)
+    )(place, *in_hbm(gathered), weight)
 
 
 def local_attend(qkv, valid_day, reach):
@@ -145,6 +357,35 @@
     return result.astype(jnp.bfloat16).reshape(seconds, -1)
 
 
+def strided_kernel(count, heads, packed, out):
+    days = packed.shape[1]
+    flags = jnp.transpose(packed[3 * heads * count].astype(jnp.float32))
+    span = 2 * days
+    row = lax.broadcasted_iota(jnp.int32, (span, span), 0)
+    col = lax.broadcasted_iota(jnp.int32, (span, span), 1)
+    paired = (row // days) == (col // days)
+    earlier = paired & (col < row)
+    for second in range(0, count, 2):
+        seen = jnp.concatenate(
+            [flags[second : second + 1, :], flags[second + 1 : second + 2, :]], axis=1
+        )
+        allowed = (earlier & (seen > 0)) | (row == col)
+        for head in range(heads):
+            at = head * count + second
+            query, keys, values = (
+                packed[pl.ds(at + j * heads * count, 2)].reshape(span, HD) for j in range(3)
+            )
+            scores = lax.dot_general(
+                query, keys, (((1,), (1,)), ((), ())), preferred_element_type=jnp.float32
+            ) / math.sqrt(HD)
+            scores = jnp.where(allowed, scores, -jnp.inf)
+            row_max = jnp.max(scores, axis=1, keepdims=True)
+            expo = jnp.exp(scores - row_max)
+            probs = (expo / jnp.sum(expo, axis=1, keepdims=True)).astype(jnp.bfloat16)
+            result = jnp.dot(probs, values, preferred_element_type=jnp.float32)
+            out[pl.ds(at, 2)] = result.astype(jnp.bfloat16).reshape(2, days, HD)
+
+
 def strided_attend(qkv, marks):
     rows, cols = qkv.shape[1:]
     peers = NY * NX * NH * NC
@@ -156,23 +397,20 @@
     flags = jnp.pad(flags, ((0, 0), (0, 0), (0, HD - count)))
     packed = jnp.concatenate([packed, flags], axis=1)
     packed = lax.all_to_all(packed, "seq", split_axis=0, concat_axis=0, tiled=True)
-    days = packed.shape[0]
-    split_up = packed[:, :-1].reshape(days, 3, heads, count, HD)
-    query, keys, values = split_up[:, 0], split_up[:, 1], split_up[:, 2]
-    scores = jnp.einsum(
-        "dhsc,ehsc->hsde", query, keys, preferred_element_type=jnp.float32
-    ) / math.sqrt(HD)
-    day = jnp.arange(days)
-    causal = day[None, :] <= day[:, None]
-    same = day[None, :] == day[:, None]
-    seen = jnp.transpose(packed[:, -1, :count]) > 0
-    allowed = causal[None] & (seen[:, None, :] | same[None])
-    scores = jnp.where(allowed[None], scores, -jnp.inf)
-    row_max = jnp.max(scores, axis=-1, keepdims=True)
-    expo = jnp.exp(scores - row_max)
-    probs = (expo / jnp.sum(expo, axis=-1, keepdims=True)).astype(jnp.bfloat16)
-    result = jnp.einsum("hsde,ehsc->dhsc", probs, values, preferred_element_type=jnp.float32)
-    result = result.astype(jnp.bfloat16).reshape(days, heads * count, HD)
+    packed = packed.transpose(1, 0, 2)
+    result = pl.pallas_call(
+        functools.partial(strided_kernel, count, heads),
+        out_shape=jax.ShapeDtypeStruct((heads * count, peers, HD), jnp.bfloat16),
+        in_specs=[VMEM],
+        out_specs=VMEM,
+        compiler_params=pltpu.CompilerParams(vmem_limit_bytes=8 * 1024 * 1024),
+        cost_estimate=pl.CostEstimate(
+            flops=8 * heads * count * peers * peers * HD,
+            bytes_accessed=2 * 4 * heads * count * peers * HD,
+            transcendentals=2 * heads * count * peers * peers,
+        ),
+    )(packed)
+    result = result.transpose(1, 0, 2)
     result = lax.all_to_all(result, "seq", split_axis=0, concat_axis=0, tiled=True)
     result = result.reshape(peers, heads, count, HD).transpose(0, 2, 1, 3)
     return result.reshape(rows, cols)
@@ -191,24 +429,14 @@
     ).astype(jnp.int32)
     own_strided = jnp.transpose(w_strided, (1, 0, 2))
     own_local = jnp.transpose(w_local, (1, 0, 2))
-    other_strided = swap(own_strided, "h")
-    other_local = swap(own_local, "h")
-    tokens, other_strided, other_local = lax.optimization_barrier(
-        (tokens, other_strided, other_local)
-    )
-    weight_strided = place_weights(place, own_strided, other_strided, 0)
-    weight_local = place_weights(place, own_local, other_local, 1)
-    out_strided, qkv_local = [], []
-    start = 0
-    for size in CHUNKS:
-        rows = slice(start, start + size)
-        gathered = lax.all_gather(tokens[rows], "fsdp", axis=1, tiled=True)
-        qkv = project(gathered, weight_strided)
-        out_strided.append(strided_attend(qkv, valid[0, rows]))
-        qkv_local.append(project(gathered, weight_local))
-        start += size
-    out_strided = jnp.concatenate(out_strided, axis=0)
-    qkv_local = jnp.concatenate(qkv_local, axis=1)
+    gathered, strided, local = gather_all(tokens, own_strided, own_local)
+    weight_strided = place_weights(place, *strided, 0)
+    acc = project_early(place, gathered, weight_strided)
+    acc, received = lax.optimization_barrier((acc, local[1]))
+    weight_local = place_weights(place, local[0], received, 1)
+    qkv_strided = project_late(place, gathered, weight_strided, acc)
+    out_strided = strided_attend(qkv_strided, valid[0])
+    qkv_local = project_local(place, gathered, weight_local)
     out_local = local_attend(qkv_local, valid[0], band_reach)
     return (out_local, out_strided)
 

time: 294 us -> 226 us (0.77)
  starting transfers between devices: 96.9 us -> 65.4 us
  local copies, waits for them, and re-layouts: 40.1 us -> 11.9 us
  between operations: 14.6 us -> 1.07 us
  Pallas kernels: 31.4 us -> 38.6 us
  matrix products: 8.61 us -> 5.44 us
    all_gather x2 -> x0, waiting for transfers between devices: 47.3 us -> none  [body(): gathered = lax.all_gather(tokens[rows], 'fsdp', axis=1, tiled=True)]
    ppermute x26 -> x21, waiting for transfers between devices: 32.7 us -> 65.6 us  [swap(): return lax.ppermute(value, 'seq', seq_pairs(MOVES[kind]))]
    ppermute x26 -> x21, starting transfers between devices: 54 us -> 32.9 us  [swap(): return lax.ppermute(value, 'seq', seq_pairs(MOVES[kind]))]
    unnamed x43 -> x30, local copies, waits for them, and re-layouts: 23.3 us -> 6.35 us
    ppermute x0 -> x5, waiting for transfers between devices: none -> 16.4 us  [send_z(): return lax.ppermute(value, 'fsdp', pairs)]
    all_to_all x2 -> x1, starting transfers between devices: 25.5 us -> 11.9 us  [strided_attend(): lax.all_to_all(packed, 'seq', split_axis=0, concat_axis=0, tiled=True)]
    ppermute x0 -> x5, starting transfers between devices: none -> 11.3 us  [send_z(): return lax.ppermute(value, 'fsdp', pairs)]
    all_to_all x2 -> x1, starting transfers between devices: 17.3 us -> 9.27 us  [strided_attend(): lax.all_to_all(result, 'seq', split_axis=0, concat_axis=0, tiled=True)]
  transfers between devices with their start and end apart: 32 -> 28, of which waited for: 13 -> 15; matrix products, arithmetic and copies ran while one was open for 8% -> 6% of each run, Pallas kernels for 11% -> 16%
where the time goes in v3:
time: 226 us
  waiting for transfers between devices  97.8 us (43%)
  starting transfers between devices  65.4 us (29%)
  Pallas kernels  38.6 us (17%)
  local copies, waits for them, and re-layouts  11.9 us (5%)
  matrix products  5.44 us (2%)
  other arithmetic  5.31 us (2%)
    ppermute x21, waiting for transfers between devices, swap(): return lax.ppermute(value, 'seq', seq_pairs(MOVES[kind]))  65.6 us
    ppermute x21, starting transfers between devices, swap(): return lax.ppermute(value, 'seq', seq_pairs(MOVES[kind]))  32.9 us
    ppermute x5, waiting for transfers between devices, send_z(): return lax.ppermute(value, 'fsdp', pairs)  16.4 us
    pallas_call x1, Pallas kernels, project_local(): pl.pallas_call(project_kernel, out_shape=jax.ShapeDtypeStruct((3, rows, c...  14.2 us
    all_to_all x1, starting transfers between devices, strided_attend(): lax.all_to_all(packed, 'seq', split_axis=0, concat_axis=0, tiled=True)  11.9 us
    ppermute x5, starting transfers between devices, send_z(): return lax.ppermute(value, 'fsdp', pairs)  11.3 us
    all_to_all x1, starting transfers between devices, strided_attend(): lax.all_to_all(result, 'seq', split_axis=0, concat_axis=0, tiled=True)  9.27 us
    pallas_call x2, Pallas kernels, place_weights(): pl.pallas_call(functools.partial(place_kernel, (OWN_ORDERS[which], OTHER_...  8.93 us
  transfers between devices with their start and end apart: 28, of which 15 were waited for; matrix products, arithmetic and copies ran while one was open for 6% of the time, Pallas kernels for 16%

profile of v3, /device:TPU:1, one launch (start us, length us, event | category | flops | bytes accessed | tf_op | source)
XLA Modules:
  0.0 225.5 jit_solution(10455791818958305951)
XLA Ops:
  0.6 1.0 maximum_bitcast_fusion
  1.7 7.8 %collective-permute-start = (bf16[1,3,80,640]{3,2,1,0:T(8,128)(2,1)S(1)}, bf16[1,3,80,640]{3,2,1,0:T(8,128)(2,1)S(1)}, u32[]{:S(2)}, u32[]{:S(2)}) collective-permute-start(bf16[1,3,80,640]{3,2,1,0:T(8,128)(2,1)S(1)} %maximum_bitcast_fusion), channel_id=1, source_target_pairs={{0,8},{4,12},{8,0},{12,4},{16,24},{20,28},{24,16},{28,20},{32,40},... | collective-permute-start | bytes 921608 | tf_op jit(solution)/shard_map/ppermute | solution.py:44
  9.5 1.2 collective-permute-start.3
  10.7 6.2 %collective-permute-done = bf16[1,3,80,640]{3,2,1,0:T(8,128)(2,1)S(1)} collective-permute-done((bf16[1,3,80,640]{3,2,1,0:T(8,128)(2,1)S(1)}, bf16[1,3,80,640]{3,2,1,0:T(8,128)(2,1)S(1)}, u32[]{:S(2)}, u32[]{:S(2)}) %collective-permute-start) | collective-permute-done | bytes 307232 | tf_op jit(solution)/shard_map/ppermute | solution.py:44
  16.9 1.8 collective-permute-start.6
  18.8 6.1 %collective-permute-start.1 = (bf16[640,1280]{1,0:T(8,128)(2,1)}, bf16[640,1280]{1,0:T(8,128)(2,1)S(1)}, u32[]{:S(2)}, u32[]{:S(2)}) collective-permute-start(bf16[640,1280]{1,0:T(8,128)(2,1)} %refs_0_.1), channel_id=1, source_target_pairs={{0,1},{1,0},{2,3},{3,2},{4,5},{5,4},{6,7},{7,6},{8,9},{9,8},{10,11... | collective-permute-start | bytes 4915208 | tf_op jit(solution)/shard_map/ppermute | solution.py:97
  24.9 0.8 collective-permute-start.2
  25.7 2.6 %collective-permute-start.4 = (bf16[2,3,80,640]{3,2,1,0:T(8,128)(2,1)S(1)}, bf16[2,3,80,640]{3,2,1,0:T(8,128)(2,1)S(1)}, u32[]{:S(2)}, u32[]{:S(2)}) collective-permute-start(bf16[2,3,80,640]{3,2,1,0:T(8,128)(2,1)S(1)} %pad_maximum_fusion.6), channel_id=1, source_target_pairs={{0,48},{4,52},{8,56},{12,60},{16,32},{20,36},{24,40},{28,44},{32,1... | collective-permute-start | bytes 1843208 | tf_op jit(solution)/shard_map/ppermute | solution.py:44
  28.3 2.0 collective-permute-start.7
  30.4 9.9 %collective-permute-done.4 = bf16[2,3,80,640]{3,2,1,0:T(8,128)(2,1)S(1)} collective-permute-done((bf16[2,3,80,640]{3,2,1,0:T(8,128)(2,1)S(1)}, bf16[2,3,80,640]{3,2,1,0:T(8,128)(2,1)S(1)}, u32[]{:S(2)}, u32[]{:S(2)}) %collective-permute-start.4) | collective-permute-done | bytes 614432 | tf_op jit(solution)/shard_map/ppermute | solution.py:44
  40.3 0.3 collective-permute-start.5
  40.6 2.0 collective-permute-done.7
  43.0 7.1 %collective-permute-done.5 = bf16[4,3,80,256]{3,2,1,0:T(8,128)(2,1)S(1)} collective-permute-done((bf16[4,3,80,256]{3,2,1,0:T(8,128)(2,1)S(1)}, bf16[4,3,80,256]{3,2,1,0:T(8,128)(2,1)S(1)}, u32[]{:S(2)}, u32[]{:S(2)}) %collective-permute-start.5) | collective-permute-done | bytes 491552 | tf_op jit(solution)/shard_map/ppermute | solution.py:44
  50.2 2.1 collective-permute-done.8
  52.4 7.0 %collective-permute-done.1.refs_1_ = bf16[640,1280]{1,0:T(8,128)(2,1)S(1)} collective-permute-done((bf16[640,1280]{1,0:T(8,128)(2,1)}, bf16[640,1280]{1,0:T(8,128)(2,1)S(1)}, u32[]{:S(2)}, u32[]{:S(2)}) %collective-permute-start.1) | collective-permute-done | bytes 1638432 | tf_op jit(solution)/shard_map/ppermute | solution.py:97
  59.4 2.0 collective-permute-start.11
  61.4 2.5 %collective-permute-start.14 = (bf16[4,3,80,384]{3,2,1,0:T(8,128)(2,1)S(1)}, bf16[4,3,80,384]{3,2,1,0:T(8,128)(2,1)S(1)}, u32[]{:S(2)}, u32[]{:S(2)}) collective-permute-start(bf16[4,3,80,384]{3,2,1,0:T(8,128)(2,1)S(1)} %slice.29), channel_id=1, source_target_pairs={{0,48},{4,52},{8,56},{12,60},{16,32},{20,36},{24,40},{28,44},{32,1... | collective-permute-start | bytes 2211848 | tf_op jit(solution)/shard_map/ppermute | solution.py:44
  63.8 0.8 collective-permute-start.13
  64.6 1.3 collective-permute-start.10
  65.9 1.9 collective-permute-start.9
  67.8 10.0 %collective-permute-done.14 = bf16[4,3,80,384]{3,2,1,0:T(8,128)(2,1)S(1)} collective-permute-done((bf16[4,3,80,384]{3,2,1,0:T(8,128)(2,1)S(1)}, bf16[4,3,80,384]{3,2,1,0:T(8,128)(2,1)S(1)}, u32[]{:S(2)}, u32[]{:S(2)}) %collective-permute-start.14) | collective-permute-done | bytes 737312 | tf_op jit(solution)/shard_map/ppermute | solution.py:44
  77.8 2.5 %collective-permute-start.12 = (bf16[8,3,80,256]{3,2,1,0:T(8,128)(2,1)S(1)}, bf16[8,3,80,256]{3,2,1,0:T(8,128)(2,1)}, u32[]{:S(2)}, u32[]{:S(2)}) collective-permute-start(bf16[8,3,80,256]{3,2,1,0:T(8,128)(2,1)S(1)} %pad_maximum_fusion.3.refs_4_), channel_id=1, source_target_pairs={{0,48},{4,52},{8,56},{12,60},{16,32},{20,36},{24,40},{28,44},{32,1... | collective-permute-start | bytes 2949128 | tf_op jit(solution)/shard_map/ppermute | solution.py:44
  80.3 17.1 %collective-permute-done.13 = bf16[4,3,80,384]{3,2,1,0:T(8,128)(2,1)S(1)} collective-permute-done((bf16[4,3,80,384]{3,2,1,0:T(8,128)(2,1)S(1)}, bf16[4,3,80,384]{3,2,1,0:T(8,128)(2,1)S(1)}, u32[]{:S(2)}, u32[]{:S(2)}) %collective-permute-start.13) | collective-permute-done | bytes 737312 | tf_op jit(solution)/shard_map/ppermute | solution.py:44
  97.4 3.3 %collective-permute-start.17 = (bf16[8,3,80,256]{3,2,1,0:T(8,128)(2,1)S(1)}, bf16[8,3,80,256]{3,2,1,0:T(8,128)(2,1)S(1)}, u32[]{:S(2)}, u32[]{:S(2)}) collective-permute-start(bf16[8,3,80,256]{3,2,1,0:T(8,128)(2,1)S(1)} %pad_maximum_fusion.2.refs_0_), channel_id=1, source_target_pairs={{0,4},{4,0},{8,12},{12,8},{16,20},{20,16},{24,28},{28,24},{32,36},... | collective-permute-start | bytes 2949128 | tf_op jit(solution)/shard_map/ppermute | solution.py:44
  100.7 1.4 pad_maximum_fusion.1.refs_4_
  102.1 1.3 pad_maximum_fusion.refs_0_
  103.5 1.3 collective-permute-start.22
  104.8 1.1 collective-permute-start.18
  106.0 0.8 copy-done.4
  106.9 1.3 collective-permute-start.15
  108.3 0.3 collective-permute-done.18.refs_3_
  108.6 0.4 collective-permute-start.16
  109.0 0.8 collective-permute-done.20.refs_7_
  109.7 0.4 collective-permute-start.24
  110.1 0.6 copy-done.6
  110.7 3.9 %shard_map.68.refs_5_.weight = bf16[3,5120,256]{2,1,0:T(8,128)(2,1)S(1)} custom-call(s32[5]{0:T(128)S(1)} %stack.23.place, bf16[8,3,80,256]{3,2,1,0:T(8,128)(2,1)} %copy-done.1, bf16[8,3,80,256]{3,2,1,0:T(8,128)(2,1)} %copy-done.4, bf16[8,3,80,256]{3,2,1,0:T(8,128)(2,1)} %copy-done.3, bf16[8,3,80,256]{3,2,1,0:T(8,128)(2,1)} %collective-permute-done.18.refs_3_, ...), custom_call_target="tpu_custom_call" | custom-call | bytes 15728640 | tf_op jit(solution)/shard_map/pallas_call | solution.py:82
  114.6 3.1 %copy-done = bf16[3,5120,256]{2,1,0:T(8,128)(2,1)} copy-done((bf16[3,5120,256]{2,1,0:T(8,128)(2,1)}, bf16[3,5120,256]{2,1,0:T(8,128)(2,1)S(1)}, u32[]{:S(2)}) %copy-start) | copy-done | bytes 7864344
  117.7 8.0 %shard_map.69.acc = f32[3,640,256]{2,1,0:T(8,128)S(1)} custom-call(s32[5]{0:T(128)S(1)} %stack.23.place, bf16[640,1280]{1,0:T(8,128)(2,1)} %refs_0_.1, bf16[640,1280]{1,0:T(8,128)(2,1)} %copy-done.10, bf16[640,1280]{1,0:T(8,128)(2,1)} %copy-done.11, bf16[640,1280]{1,0:T(8,128)(2,1)} %collective-permute-done.9.refs_3_, bf16[640,1280]{1,0:T(8,128)(2,1)} %copy-done.12, ...), custom_call_target="tpu_custom_call" | custom-call | flops 5033164800 | bytes 16384000 | tf_op jit(solution)/shard_map/pallas_call | solution.py:246
  125.7 9.8 %collective-permute-done.21.refs_2_ = bf16[8,3,80,384]{3,2,1,0:T(8,128)(2,1)} collective-permute-done((bf16[8,3,80,384]{3,2,1,0:T(8,128)(2,1)}, bf16[8,3,80,384]{3,2,1,0:T(8,128)(2,1)}, u32[]{:S(2)}, u32[]{:S(2)}) %collective-permute-start.21) | collective-permute-done | bytes 1474592 | tf_op jit(solution)/shard_map/ppermute | solution.py:44
  135.5 0.4 collective-permute-done.22.refs_6_
  135.9 2.7 %collective-permute-start.23 = (bf16[8,3,80,384]{3,2,1,0:T(8,128)(2,1)}, bf16[8,3,80,384]{3,2,1,0:T(8,128)(2,1)}, u32[]{:S(2)}, u32[]{:S(2)}) collective-permute-start(bf16[8,3,80,384]{3,2,1,0:T(8,128)(2,1)} %collective-permute-done.21.refs_2_), channel_id=1, source_target_pairs={{0,4},{4,0},{8,12},{12,8},{16,20},{20,16},{24,28},{28,24},{32,36},... | collective-permute-start | bytes 4423688 | tf_op jit(solution)/shard_map/ppermute | solution.py:44
  138.8 9.4 %collective-permute-done.15.refs_5_.far = bf16[640,1280]{1,0:T(8,128)(2,1)} collective-permute-done((bf16[640,1280]{1,0:T(8,128)(2,1)}, bf16[640,1280]{1,0:T(8,128)(2,1)}, u32[]{:S(2)}, u32[]{:S(2)}) %collective-permute-start.15) | collective-permute-done | bytes 1638432 | tf_op jit(solution)/shard_map/ppermute | solution.py:97
  148.2 4.2 %shard_map.72 = bf16[3,640,256]{2,1,0:T(8,128)(2,1)S(1)} custom-call(s32[5]{0:T(128)S(1)} %stack.23.place, bf16[640,1280]{1,0:T(8,128)(2,1)} %collective-permute-done.15.refs_5_.far, bf16[3,5120,256]{2,1,0:T(8,128)(2,1)} %copy-done, f32[3,640,256]{2,1,0:T(8,128)S(1)} %shard_map.69.acc), custom_call_target="tpu_custom_call" | custom-call | flops 1258291200 | bytes 6553600 | tf_op jit(solution)/shard_map/pallas_call | solution.py:269
  152.4 0.2 reshape.134
  152.7 0.2 copy.53
  153.0 1.6 copy.54
  154.6 11.9 %all-to-all-start = ((bf16[64,61,128]{2,1,0:T(8,128)(2,1)}), bf16[64,61,128]{2,1,0:T(8,128)(2,1)S(1)}, u32[]{:S(2)}, u32[]{:S(2)}) async-start(bf16[64,61,128]{2,1,0:T(8,128)(2,1)} %copy.54), calls=%async_computation | async-start | bytes 2097152 | tf_op jit(solution)/shard_map/all_to_all | solution.py:399
  166.7 1.0 iota_compare_fusion.2
  167.7 5.0 %shard_map.70.refs_6_ = bf16[3,5120,384]{2,1,0:T(8,128)(2,1)S(1)} custom-call(s32[5]{0:T(128)S(1)} %stack.23.place, bf16[8,3,80,384]{3,2,1,0:T(8,128)(2,1)} %pad_maximum_fusion.refs_0_, bf16[8,3,80,384]{3,2,1,0:T(8,128)(2,1)} %collective-permute-done.16.refs_1_, bf16[8,3,80,384]{3,2,1,0:T(8,128)(2,1)} %collective-permute-done.21.refs_2_, ...), custom_call_target="tpu_custom_call" | custom-call | bytes 23592960 | tf_op jit(solution)/shard_map/pallas_call | solution.py:82
  172.7 14.2 %shard_map.71 = bf16[3,640,384]{2,1,0:T(8,128)(2,1)S(1)} custom-call(s32[5]{0:T(128)S(1)} %stack.23.place, bf16[640,1280]{1,0:T(8,128)(2,1)} %refs_0_.1, bf16[640,1280]{1,0:T(8,128)(2,1)} %copy-done.10, bf16[640,1280]{1,0:T(8,128)(2,1)} %copy-done.11, bf16[640,1280]{1,0:T(8,128)(2,1)} %collective-permute-done.9.refs_3_, bf16[640,1280]{1,0:T(8,128)(2,1)} %copy-done.12, ...), custom_call_target="tpu_custom_call" | custom-call | flops 7549747200 | bytes 19824640 | tf_op jit(solution)/shard_map/pallas_call | solution.py:319
  187.1 0.3 copy.49
  187.3 0.3 copy.48
  187.6 0.3 copy.47
  187.9 6.9 %all-to-all-done = bf16[64,61,128]{2,1,0:T(8,128)(2,1)S(1)} async-done(((bf16[64,61,128]{2,1,0:T(8,128)(2,1)}), bf16[64,61,128]{2,1,0:T(8,128)(2,1)S(1)}, u32[]{:S(2)}, u32[]{:S(2)}) %all-to-all-start) | async-done | bytes 999456 | tf_op jit(solution)/shard_map/all_to_all | solution.py:399
  194.8 0.7 copy.66
  195.4 3.3 %shard_map.73 = bf16[20,64,128]{2,1,0:T(8,128)(2,1)S(1)} custom-call(bf16[61,64,128]{2,1,0:T(8,128)(2,1)S(1)} %bitcast.35), custom_call_target="tpu_custom_call" | custom-call | flops 83886080 | bytes 1310720 | tf_op jit(solution)/shard_map/pallas_call | solution.py:401
  198.8 1.0 copy.56
  199.8 9.3 %all-to-all-start.1 = ((bf16[64,20,128]{2,1,0:T(8,128)(2,1)}), bf16[64,20,128]{2,1,0:T(8,128)(2,1)S(1)}, u32[]{:S(2)}, u32[]{:S(2)}) async-start(bf16[64,20,128]{2,1,0:T(8,128)(2,1)} %copy.56), calls=%async_computation.1 | async-start | bytes 786432 | tf_op jit(solution)/shard_map/all_to_all | solution.py:414
  209.0 2.5 %fusion.25 = f32[3,640]{1,0:T(4,128)S(1)} fusion(s32[3,640]{1,0:T(4,128)S(1)} %broadcast_subtract_fusion, s32[640]{0:T(1024)S(1)} %add_select_fusion, pred[640,640]{0,1:T(8,128)(4,1)S(1)} %copy-done.7, pred[640,640]{0,1:T(8,128)(4,1)S(1)} %get-tuple-element.49, bf16[640,3,128]{0,2,1:T(8,128)(2,1)S(1)} %bitcast.42, bf16[640,3,128]{0,2,1:T(8,128)(2,1)S(1)} %bitcast.40), kind=kOutput, calls=%fused_computation.50 | convolution fusion | flops 323175040 | bytes 1820160 | tf_op jit(solution)/shard_map/sub | solution.py:354
  211.5 2.9 %fusion.11 = bf16[3,128,640]{2,1,0:T(8,128)(2,1)S(1)} fusion(bf16[640,3,128]{0,2,1:T(8,128)(2,1)S(1)} %bitcast.44, f32[3,640]{1,0:T(4,128)S(1)} %fusion.25, s32[3,640]{1,0:T(4,128)S(1)} %broadcast_subtract_fusion, s32[640]{0:T(1024)S(1)} %add_select_fusion, pred[640,640]{0,1:T(8,128)(4,1)S(1)} %copy-done.7, pred[640,640]{0,1:T(8,128)(4,1)S(1)} %get-tuple-element.49, ...), kind=kOutput, calls=%fused_computation.19 | convolution fusion | flops 639224320 | bytes 2803200 | tf_op jit(solution)/shard_map/hqk,khc->qhc/dot_general | solution.py:356
  214.5 1.0 copy.59
  215.5 8.8 %all-to-all-done.1 = bf16[64,20,128]{2,1,0:T(8,128)(2,1)S(1)} async-done(((bf16[64,20,128]{2,1,0:T(8,128)(2,1)}), bf16[64,20,128]{2,1,0:T(8,128)(2,1)S(1)}, u32[]{:S(2)}, u32[]{:S(2)}) %all-to-all-start.1) | async-done | bytes 327712 | tf_op jit(solution)/shard_map/all_to_all | solution.py:414
  224.4 0.3 copy.58
  224.8 0.8 copy.67
  (61 shorter events, 1.8 us)
Async XLA Ops:
  1.7 15.3 %collective-permute-start = (bf16[1,3,80,640]{3,2,1,0:T(8,128)(2,1)S(1)}, bf16[1,3,80,640]{3,2,1,0:T(8,128)(2,1)S(1)}, u32[]{:S(2)}, u32[]{:S(2)}) collective-permute-start(bf16[1,3,80,640]{3,2,1,0:T(8,128)(2,1)S(1)} %maximum_bitcast_fusion), channel_id=1, source_target_pairs={{0,8},{4,12},{8,0},{12,4},{16,24},{20,28},{24,16},{28,20},{32,40},... | collective-permute-start | bytes 921608 | tf_op jit(solution)/shard_map/ppermute | solution.py:44
  9.5 16.1 %collective-permute-start.3 = (bf16[1,3,80,640]{3,2,1,0:T(8,128)(2,1)S(1)}, bf16[1,3,80,640]{3,2,1,0:T(8,128)(2,1)S(1)}, u32[]{:S(2)}, u32[]{:S(2)}) collective-permute-start(bf16[1,3,80,640]{3,2,1,0:T(8,128)(2,1)S(1)} %maximum_bitcast_fusion), channel_id=1, source_target_pairs={{0,16},{4,20},{8,24},{12,28},{16,0},{20,4},{24,8},{28,12},{32,48},... | collective-permute-start | bytes 921608 | tf_op jit(solution)/shard_map/ppermute | solution.py:44
  16.9 11.3 %collective-permute-start.6 = (bf16[1,3,80,640]{3,2,1,0:T(8,128)(2,1)S(1)}, bf16[1,3,80,640]{3,2,1,0:T(8,128)(2,1)S(1)}, u32[]{:S(2)}, u32[]{:S(2)}) collective-permute-start(bf16[1,3,80,640]{3,2,1,0:T(8,128)(2,1)S(1)} %collective-permute-done), channel_id=1, source_target_pairs={{0,64},{4,68},{8,72},{12,76},{16,80},{20,84},{24,88},{28,92},{32,9... | collective-permute-start | bytes 921608 | tf_op jit(solution)/shard_map/ppermute | solution.py:44
  18.8 40.6 %collective-permute-start.1 = (bf16[640,1280]{1,0:T(8,128)(2,1)}, bf16[640,1280]{1,0:T(8,128)(2,1)S(1)}, u32[]{:S(2)}, u32[]{:S(2)}) collective-permute-start(bf16[640,1280]{1,0:T(8,128)(2,1)} %refs_0_.1), channel_id=1, source_target_pairs={{0,1},{1,0},{2,3},{3,2},{4,5},{5,4},{6,7},{7,6},{8,9},{9,8},{10,11... | collective-permute-start | bytes 4915208 | tf_op jit(solution)/shard_map/ppermute | solution.py:97
  24.9 34.5 %collective-permute-start.2 = (bf16[640,1280]{1,0:T(8,128)(2,1)}, bf16[640,1280]{1,0:T(8,128)(2,1)S(1)}, u32[]{:S(2)}, u32[]{:S(2)}) collective-permute-start(bf16[640,1280]{1,0:T(8,128)(2,1)} %refs_0_.1), channel_id=1, source_target_pairs={{1,2},{2,1},{5,6},{6,5},{9,10},{10,9},{13,14},{14,13},{17,18},{18,... | collective-permute-start | bytes 4915208 | tf_op jit(solution)/shard_map/ppermute | solution.py:97
  25.7 14.6 %collective-permute-start.4 = (bf16[2,3,80,640]{3,2,1,0:T(8,128)(2,1)S(1)}, bf16[2,3,80,640]{3,2,1,0:T(8,128)(2,1)S(1)}, u32[]{:S(2)}, u32[]{:S(2)}) collective-permute-start(bf16[2,3,80,640]{3,2,1,0:T(8,128)(2,1)S(1)} %pad_maximum_fusion.6), channel_id=1, source_target_pairs={{0,48},{4,52},{8,56},{12,60},{16,32},{20,36},{24,40},{28,44},{32,1... | collective-permute-start | bytes 1843208 | tf_op jit(solution)/shard_map/ppermute | solution.py:44
  28.3 14.3 %collective-permute-start.7 = (bf16[2,3,80,640]{3,2,1,0:T(8,128)(2,1)S(1)}, bf16[2,3,80,640]{3,2,1,0:T(8,128)(2,1)S(1)}, u32[]{:S(2)}, u32[]{:S(2)}) collective-permute-start(bf16[2,3,80,640]{3,2,1,0:T(8,128)(2,1)S(1)} %pad_maximum_fusion.7), channel_id=1, source_target_pairs={{0,192},{4,196},{8,200},{12,204},{16,208},{20,212},{24,216},{28,22... | collective-permute-start | bytes 1843208 | tf_op jit(solution)/shard_map/ppermute | solution.py:44
  40.3 9.8 %collective-permute-start.5 = (bf16[4,3,80,256]{3,2,1,0:T(8,128)(2,1)S(1)}, bf16[4,3,80,256]{3,2,1,0:T(8,128)(2,1)S(1)}, u32[]{:S(2)}, u32[]{:S(2)}) collective-permute-start(bf16[4,3,80,256]{3,2,1,0:T(8,128)(2,1)S(1)} %pad_maximum_fusion.8), channel_id=1, source_target_pairs={{0,64},{4,68},{8,72},{12,76},{16,80},{20,84},{24,88},{28,92},{32,9... | collective-permute-start | bytes 1474568 | tf_op jit(solution)/shard_map/ppermute | solution.py:44
  42.8 9.5 %collective-permute-start.8 = (bf16[4,3,80,256]{3,2,1,0:T(8,128)(2,1)S(1)}, bf16[4,3,80,256]{3,2,1,0:T(8,128)(2,1)S(1)}, u32[]{:S(2)}, u32[]{:S(2)}) collective-permute-start(bf16[4,3,80,256]{3,2,1,0:T(8,128)(2,1)S(1)} %slice.28), channel_id=1, source_target_pairs={{0,16},{4,20},{8,24},{12,28},{16,0},{20,4},{24,8},{28,12},{32,48},... | collective-permute-start | bytes 1474568 | tf_op jit(solution)/shard_map/ppermute | solution.py:44
  50.2 51.9 %copy-start.1 = (bf16[8,3,80,256]{3,2,1,0:T(8,128)(2,1)}, bf16[8,3,80,256]{3,2,1,0:T(8,128)(2,1)S(1)}, u32[]{:S(2)}) copy-start(bf16[8,3,80,256]{3,2,1,0:T(8,128)(2,1)S(1)} %pad_maximum_fusion.2.refs_0_) | copy-start | bytes 2949124
  52.4 51.0 %copy-start.2 = (bf16[8,3,80,256]{3,2,1,0:T(8,128)(2,1)}, bf16[8,3,80,256]{3,2,1,0:T(8,128)(2,1)S(1)}, u32[]{:S(2)}) copy-start(bf16[8,3,80,256]{3,2,1,0:T(8,128)(2,1)S(1)} %pad_maximum_fusion.3.refs_4_) | copy-start | bytes 2949124
  59.4 44.0 %copy-start.10 = (bf16[640,1280]{1,0:T(8,128)(2,1)}, bf16[640,1280]{1,0:T(8,128)(2,1)S(1)}, u32[]{:S(2)}) copy-start(bf16[640,1280]{1,0:T(8,128)(2,1)S(1)} %collective-permute-done.1.refs_1_) | copy-start | bytes 4915204
  59.4 44.0 %copy-start.11 = (bf16[640,1280]{1,0:T(8,128)(2,1)}, bf16[640,1280]{1,0:T(8,128)(2,1)S(1)}, u32[]{:S(2)}) copy-start(bf16[640,1280]{1,0:T(8,128)(2,1)S(1)} %collective-permute-done.2.refs_2_) | copy-start | bytes 4915204
  59.4 41.3 %collective-permute-start.11 = (bf16[8,3,80,256]{3,2,1,0:T(8,128)(2,1)S(1)}, bf16[8,3,80,256]{3,2,1,0:T(8,128)(2,1)S(1)}, u32[]{:S(2)}, u32[]{:S(2)}) collective-permute-start(bf16[8,3,80,256]{3,2,1,0:T(8,128)(2,1)S(1)} %pad_maximum_fusion.2.refs_0_), channel_id=1, source_target_pairs={{0,192},{4,196},{8,200},{12,204},{16,208},{20,212},{24,216},{28,22... | collective-permute-start | bytes 2949128 | tf_op jit(solution)/shard_map/ppermute | solution.py:44
  61.4 16.5 %collective-permute-start.14 = (bf16[4,3,80,384]{3,2,1,0:T(8,128)(2,1)S(1)}, bf16[4,3,80,384]{3,2,1,0:T(8,128)(2,1)S(1)}, u32[]{:S(2)}, u32[]{:S(2)}) collective-permute-start(bf16[4,3,80,384]{3,2,1,0:T(8,128)(2,1)S(1)} %slice.29), channel_id=1, source_target_pairs={{0,48},{4,52},{8,56},{12,60},{16,32},{20,36},{24,40},{28,44},{32,1... | collective-permute-start | bytes 2211848 | tf_op jit(solution)/shard_map/ppermute | solution.py:44
  63.8 33.5 %collective-permute-start.13 = (bf16[4,3,80,384]{3,2,1,0:T(8,128)(2,1)S(1)}, bf16[4,3,80,384]{3,2,1,0:T(8,128)(2,1)S(1)}, u32[]{:S(2)}, u32[]{:S(2)}) collective-permute-start(bf16[4,3,80,384]{3,2,1,0:T(8,128)(2,1)S(1)} %pad_maximum_fusion.4), channel_id=1, source_target_pairs={{0,192},{4,196},{8,200},{12,204},{16,208},{20,212},{24,216},{28,22... | collective-permute-start | bytes 2211848 | tf_op jit(solution)/shard_map/ppermute | solution.py:44
  64.6 38.8 %collective-permute-start.10 = (bf16[640,1280]{1,0:T(8,128)(2,1)S(1)}, bf16[640,1280]{1,0:T(8,128)(2,1)S(1)}, u32[]{:S(2)}, u32[]{:S(2)}) collective-permute-start(bf16[640,1280]{1,0:T(8,128)(2,1)S(1)} %collective-permute-done.2.refs_2_), channel_id=1, source_target_pairs={{2,3},{1,0},{6,7},{5,4},{10,11},{9,8},{14,15},{13,12},{18,19},{17,... | collective-permute-start | bytes 4915208 | tf_op jit(solution)/shard_map/ppermute | solution.py:97
  65.9 37.5 %collective-permute-start.9 = (bf16[640,1280]{1,0:T(8,128)(2,1)S(1)}, bf16[640,1280]{1,0:T(8,128)(2,1)}, u32[]{:S(2)}, u32[]{:S(2)}) collective-permute-start(bf16[640,1280]{1,0:T(8,128)(2,1)S(1)} %collective-permute-done.1.refs_1_), channel_id=1, source_target_pairs={{1,2},{2,1},{5,6},{6,5},{9,10},{10,9},{13,14},{14,13},{17,18},{18,... | collective-permute-start | bytes 4915208 | tf_op jit(solution)/shard_map/ppermute | solution.py:97
  77.8 25.6 %collective-permute-start.12 = (bf16[8,3,80,256]{3,2,1,0:T(8,128)(2,1)S(1)}, bf16[8,3,80,256]{3,2,1,0:T(8,128)(2,1)}, u32[]{:S(2)}, u32[]{:S(2)}) collective-permute-start(bf16[8,3,80,256]{3,2,1,0:T(8,128)(2,1)S(1)} %pad_maximum_fusion.3.refs_4_), channel_id=1, source_target_pairs={{0,48},{4,52},{8,56},{12,60},{16,32},{20,36},{24,40},{28,44},{32,1... | collective-permute-start | bytes 2949128 | tf_op jit(solution)/shard_map/ppermute | solution.py:44
  97.4 8.6 %collective-permute-start.17 = (bf16[8,3,80,256]{3,2,1,0:T(8,128)(2,1)S(1)}, bf16[8,3,80,256]{3,2,1,0:T(8,128)(2,1)S(1)}, u32[]{:S(2)}, u32[]{:S(2)}) collective-permute-start(bf16[8,3,80,256]{3,2,1,0:T(8,128)(2,1)S(1)} %pad_maximum_fusion.2.refs_0_), channel_id=1, source_target_pairs={{0,4},{4,0},{8,12},{12,8},{16,20},{20,16},{24,28},{28,24},{32,36},... | collective-permute-start | bytes 2949128 | tf_op jit(solution)/shard_map/ppermute | solution.py:44
  100.6 4.2 %copy-start.3 = (bf16[8,3,80,256]{3,2,1,0:T(8,128)(2,1)}, bf16[8,3,80,256]{3,2,1,0:T(8,128)(2,1)S(1)}, u32[]{:S(2)}) copy-start(bf16[8,3,80,256]{3,2,1,0:T(8,128)(2,1)S(1)} %collective-permute-done.11.refs_2_) | copy-start | bytes 2949124
  100.6 5.4 %collective-permute-start.19 = (bf16[8,3,80,256]{3,2,1,0:T(8,128)(2,1)S(1)}, bf16[8,3,80,256]{3,2,1,0:T(8,128)(2,1)S(1)}, u32[]{:S(2)}, u32[]{:S(2)}) collective-permute-start(bf16[8,3,80,256]{3,2,1,0:T(8,128)(2,1)S(1)} %pad_maximum_fusion.3.refs_4_), channel_id=1, source_target_pairs={{0,4},{4,0},{8,12},{12,8},{16,20},{20,16},{24,28},{28,24},{32,36},... | collective-permute-start | bytes 2949128 | tf_op jit(solution)/shard_map/ppermute | solution.py:44
  103.4 4.8 %copy-start.12 = (bf16[640,1280]{1,0:T(8,128)(2,1)}, bf16[640,1280]{1,0:T(8,128)(2,1)S(1)}, u32[]{:S(2)}) copy-start(bf16[640,1280]{1,0:T(8,128)(2,1)S(1)} %collective-permute-done.10.refs_4_) | copy-start | bytes 4915204
  103.4 32.1 %collective-permute-start.21 = (bf16[8,3,80,384]{3,2,1,0:T(8,128)(2,1)}, bf16[8,3,80,384]{3,2,1,0:T(8,128)(2,1)}, u32[]{:S(2)}, u32[]{:S(2)}) collective-permute-start(bf16[8,3,80,384]{3,2,1,0:T(8,128)(2,1)} %pad_maximum_fusion.refs_0_), channel_id=1, source_target_pairs={{0,64},{4,68},{8,72},{12,76},{16,80},{20,84},{24,88},{28,92},{32,9... | collective-permute-start | bytes 4423688 | tf_op jit(solution)/shard_map/ppermute | solution.py:44
  103.5 32.4 %collective-permute-start.22 = (bf16[8,3,80,384]{3,2,1,0:T(8,128)(2,1)}, bf16[8,3,80,384]{3,2,1,0:T(8,128)(2,1)}, u32[]{:S(2)}, u32[]{:S(2)}) collective-permute-start(bf16[8,3,80,384]{3,2,1,0:T(8,128)(2,1)} %pad_maximum_fusion.1.refs_4_), channel_id=1, source_target_pairs={{0,16},{4,20},{8,24},{12,28},{16,0},{20,4},{24,8},{28,12},{32,48},... | collective-permute-start | bytes 4423688 | tf_op jit(solution)/shard_map/ppermute | solution.py:44
  104.8 3.8 %collective-permute-start.18 = (bf16[8,3,80,256]{3,2,1,0:T(8,128)(2,1)S(1)}, bf16[8,3,80,256]{3,2,1,0:T(8,128)(2,1)}, u32[]{:S(2)}, u32[]{:S(2)}) collective-permute-start(bf16[8,3,80,256]{3,2,1,0:T(8,128)(2,1)S(1)} %collective-permute-done.11.refs_2_), channel_id=1, source_target_pairs={{0,4},{4,0},{8,12},{12,8},{16,20},{20,16},{24,28},{28,24},{32,36},... | collective-permute-start | bytes 2949128 | tf_op jit(solution)/shard_map/ppermute | solution.py:44
  105.9 0.9 copy-start.4
  105.9 3.8 %collective-permute-start.20 = (bf16[8,3,80,256]{3,2,1,0:T(8,128)(2,1)}, bf16[8,3,80,256]{3,2,1,0:T(8,128)(2,1)S(1)}, u32[]{:S(2)}, u32[]{:S(2)}) collective-permute-start(bf16[8,3,80,256]{3,2,1,0:T(8,128)(2,1)} %collective-permute-done.12.refs_6_), channel_id=1, source_target_pairs={{0,4},{4,0},{8,12},{12,8},{16,20},{20,16},{24,28},{28,24},{32,36},... | collective-permute-start | bytes 2949128 | tf_op jit(solution)/shard_map/ppermute | solution.py:44
  106.9 1.3 copy-start.5
  106.9 41.3 %collective-permute-start.15 = (bf16[640,1280]{1,0:T(8,128)(2,1)}, bf16[640,1280]{1,0:T(8,128)(2,1)}, u32[]{:S(2)}, u32[]{:S(2)}) collective-permute-start(bf16[640,1280]{1,0:T(8,128)(2,1)} %collective-permute-done.9.refs_3_), channel_id=1, source_target_pairs={{2,3},{1,0},{6,7},{5,4},{10,11},{9,8},{14,15},{13,12},{18,19},{17,... | collective-permute-start | bytes 4915208 | tf_op jit(solution)/shard_map/ppermute | solution.py:97
  108.6 59.1 %collective-permute-start.16 = (bf16[8,3,80,384]{3,2,1,0:T(8,128)(2,1)}, bf16[8,3,80,384]{3,2,1,0:T(8,128)(2,1)}, u32[]{:S(2)}, u32[]{:S(2)}) collective-permute-start(bf16[8,3,80,384]{3,2,1,0:T(8,128)(2,1)} %pad_maximum_fusion.refs_0_), channel_id=1, source_target_pairs={{0,4},{4,0},{8,12},{12,8},{16,20},{20,16},{24,28},{28,24},{32,36},... | collective-permute-start | bytes 4423688 | tf_op jit(solution)/shard_map/ppermute | solution.py:44
  109.7 1.0 copy-start.6
  109.7 58.0 %collective-permute-start.24 = (bf16[8,3,80,384]{3,2,1,0:T(8,128)(2,1)}, bf16[8,3,80,384]{3,2,1,0:T(8,128)(2,1)}, u32[]{:S(2)}, u32[]{:S(2)}) collective-permute-start(bf16[8,3,80,384]{3,2,1,0:T(8,128)(2,1)} %pad_maximum_fusion.1.refs_4_), channel_id=1, source_target_pairs={{0,4},{4,0},{8,12},{12,8},{16,20},{20,16},{24,28},{28,24},{32,36},... | collective-permute-start | bytes 4423688 | tf_op jit(solution)/shard_map/ppermute | solution.py:44
  114.6 3.1 %copy-start = (bf16[3,5120,256]{2,1,0:T(8,128)(2,1)}, bf16[3,5120,256]{2,1,0:T(8,128)(2,1)S(1)}, u32[]{:S(2)}) copy-start(bf16[3,5120,256]{2,1,0:T(8,128)(2,1)S(1)} %shard_map.68.refs_5_.weight) | copy-start | bytes 23592964
  117.7 20.9 %copy-start.8 = (s32[1,640]{1,0:T(1,128)S(1)}, s32[1,640]{1,0:T(1,128)}, u32[]{:S(2)}) copy-start(s32[1,640]{1,0:T(1,128)} %param.8) | copy-start | bytes 7684
  135.9 31.8 %collective-permute-start.23 = (bf16[8,3,80,384]{3,2,1,0:T(8,128)(2,1)}, bf16[8,3,80,384]{3,2,1,0:T(8,128)(2,1)}, u32[]{:S(2)}, u32[]{:S(2)}) collective-permute-start(bf16[8,3,80,384]{3,2,1,0:T(8,128)(2,1)} %collective-permute-done.21.refs_2_), channel_id=1, source_target_pairs={{0,4},{4,0},{8,12},{12,8},{16,20},{20,16},{24,28},{28,24},{32,36},... | collective-permute-start | bytes 4423688 | tf_op jit(solution)/shard_map/ppermute | solution.py:44
  138.6 29.1 %collective-permute-start.25 = (bf16[8,3,80,384]{3,2,1,0:T(8,128)(2,1)}, bf16[8,3,80,384]{3,2,1,0:T(8,128)(2,1)}, u32[]{:S(2)}, u32[]{:S(2)}) collective-permute-start(bf16[8,3,80,384]{3,2,1,0:T(8,128)(2,1)} %collective-permute-done.22.refs_6_), channel_id=1, source_target_pairs={{0,4},{4,0},{8,12},{12,8},{16,20},{20,16},{24,28},{28,24},{32,36},... | collective-permute-start | bytes 4423688 | tf_op jit(solution)/shard_map/ppermute | solution.py:44
  153.0 13.6 %copy-start.9 = (s32[3]{0:T(128)S(1)}, s32[3]{0:T(128)}, u32[]{:S(2)}) copy-start(s32[3]{0:T(128)} %param.9) | copy-start | bytes 40
  154.6 40.1 %all-to-all-start = ((bf16[64,61,128]{2,1,0:T(8,128)(2,1)}), bf16[64,61,128]{2,1,0:T(8,128)(2,1)S(1)}, u32[]{:S(2)}, u32[]{:S(2)}) async-start(bf16[64,61,128]{2,1,0:T(8,128)(2,1)} %copy.54), calls=%async_computation | async-start | bytes 2097152 | tf_op jit(solution)/shard_map/all_to_all | solution.py:399
  195.4 13.6 %copy-start.7 = (pred[640,640]{0,1:T(8,128)(4,1)S(1)}, pred[640,640]{0,1:T(8,128)(4,1)}, u32[]{:S(2)}) copy-start(pred[640,640]{0,1:T(8,128)(4,1)} %get-tuple-element.50) | copy-start | bytes 1228804
  199.8 24.6 %all-to-all-start.1 = ((bf16[64,20,128]{2,1,0:T(8,128)(2,1)}), bf16[64,20,128]{2,1,0:T(8,128)(2,1)S(1)}, u32[]{:S(2)}, u32[]{:S(2)}) async-start(bf16[64,20,128]{2,1,0:T(8,128)(2,1)} %copy.56), calls=%async_computation.1 | async-start | bytes 786432 | tf_op jit(solution)/shard_map/all_to_all | solution.py:414

commit v4 on v3

--- a/solution.py
+++ b/solution.py
@@ -12,6 +12,15 @@
 BLK = 128
 NY, NX, NH, NC = 4, 4, 2, 2
 NZ = 4
+
+
+HBM = pl.BlockSpec(memory_space=pltpu.HBM)
+VMEM = pl.BlockSpec(memory_space=pltpu.VMEM)
+SMEM = pl.BlockSpec(memory_space=pltpu.SMEM)
+
+
+def in_hbm(values):
+    return [pltpu.with_memory_space_constraint(value, pltpu.HBM) for value in values]
 
 
 def seq_pairs(move):
@@ -161,7 +170,7 @@
 
 def early_kernel(place, *refs):
     tokens, weight = refs[:5], refs[5]
-    acc, held, factor, token_sem, weight_sem = refs[6:]
+    acc, spare, held, factor, token_sem, weight_sem = refs[6:]
     z = place[4]
     depth = held.shape[2]
 
@@ -198,46 +207,47 @@
         return carry
 
     lax.fori_loop(0, NZ, step, 0)
-
-
-def late_kernel(place, far, weight, acc, out, held, factor, token_sem, weight_sem):
+    start = pl.multiple_of(jnp.where(z == 0, (NZ - 1) * depth, 0), depth)
+    spare[...] = factor[:, pl.ds(start, depth), :]
+
+
+def late_kernel(place, far, factor, acc, flags, out, held, token_sem):
     z = place[4]
-    depth = held.shape[1]
     last = (z == 0) | (z == NZ - 1)
-    start = pl.multiple_of(jnp.where(z == 0, (NZ - 1) * depth, 0), depth)
-
-    def load(j):
-        return pltpu.make_async_copy(
-            weight.at[j, pl.ds(start, depth), :], factor.at[j], weight_sem.at[j]
-        )
+    peers = out.shape[1]
+    count = held.shape[0] // peers
+    heads = factor.shape[2] // HD
+
+    def store(j, value):
+        value = value.astype(out.dtype)
+        for head in range(heads):
+            for k in range(count):
+                out[(j * heads + head) * count + k] = value[
+                    k * peers : (k + 1) * peers, head * HD : (head + 1) * HD
+                ]
+
+    out[3 * heads * count] = flags[...]
 
     @pl.when(last)
     def _():
-        pltpu.make_async_copy(far, held, token_sem).start()
-        for j in range(3):
-            load(j).start()
-        pltpu.make_async_copy(far, held, token_sem).wait()
+        copy = pltpu.make_async_copy(far, held, token_sem)
+        copy.start()
+        copy.wait()
 
         def step(j, carry):
-            load(j).wait()
             term = jnp.dot(held[...], factor[j], preferred_element_type=jnp.float32)
-            out[j] = (acc[j] + term).astype(out.dtype)
+            store(j, acc[j] + term)
             return carry
 
         lax.fori_loop(0, 3, step, 0)
 
     @pl.when(jnp.logical_not(last))
     def _():
-        out[...] = acc[...].astype(out.dtype)
-
-
-HBM = pl.BlockSpec(memory_space=pltpu.HBM)
-VMEM = pl.BlockSpec(memory_space=pltpu.VMEM)
-SMEM = pl.BlockSpec(memory_space=pltpu.SMEM)
-
-
-def in_hbm(values):
-    return [pltpu.with_memory_space_constraint(value, pltpu.HBM) for value in values]
+        def step(j, carry):
+            store(j, acc[j])
+            return carry
+
+        lax.fori_loop(0, 3, step, 0)
 
 
 def project_early(place, gathered, weight):
@@ -245,9 +255,12 @@
     _, total, cols = weight.shape
     return pl.pallas_call(
         early_kernel,
-        out_shape=jax.ShapeDtypeStruct((3, rows, cols), jnp.float32),
+        out_shape=[
+            jax.ShapeDtypeStruct((3, rows, cols), jnp.float32),
+            jax.ShapeDtypeStruct((3, depth, cols), jnp.bfloat16),
+        ],
         in_specs=[SMEM] + [HBM] * 6,
-        out_specs=VMEM,
+        out_specs=[VMEM, VMEM],
         scratch_shapes=[
             pltpu.VMEM((NZ, rows, depth), jnp.bfloat16),
             pltpu.VMEM((3, total, cols), jnp.bfloat16),
@@ -263,27 +276,26 @@
     )(place, *in_hbm(gathered[:5] + (weight,)))
 
 
-def project_late(place, gathered, weight, acc):
-    rows, depth = gathered[0].shape
-    cols = weight.shape[2]
+def project_late(place, far, factor, acc, marks):
+    rows, depth = far.shape
+    cols = factor.shape[2]
+    peers = NY * NX * NH * NC
+    count = rows // peers
+    flags = jnp.transpose(marks.astype(jnp.bfloat16).reshape(count, peers))
+    flags = jnp.pad(flags, ((0, 0), (0, HD - count)))
     return pl.pallas_call(
         late_kernel,
-        out_shape=jax.ShapeDtypeStruct((3, rows, cols), jnp.bfloat16),
-        in_specs=[SMEM, HBM, HBM, VMEM],
+        out_shape=jax.ShapeDtypeStruct((3 * cols // HD * count + 1, peers, HD), jnp.bfloat16),
+        in_specs=[SMEM, HBM, VMEM, VMEM, VMEM],
         out_specs=VMEM,
-        scratch_shapes=[
-            pltpu.VMEM((rows, depth), jnp.bfloat16),
-            pltpu.VMEM((3, depth, cols), jnp.bfloat16),
-            pltpu.SemaphoreType.DMA,
-            pltpu.SemaphoreType.DMA((3,)),
-        ],
+        scratch_shapes=[pltpu.VMEM((rows, depth), jnp.bfloat16), pltpu.SemaphoreType.DMA],
         compiler_params=pltpu.CompilerParams(vmem_limit_bytes=16 * 1024 * 1024),
         cost_estimate=pl.CostEstimate(
             flops=6 * rows * depth * cols,
             bytes_accessed=2 * (rows * depth + 3 * depth * cols) + 18 * rows * cols,
             transcendentals=0,
         ),
-    )(place, *in_hbm((gathered[5], weight)), acc)
+    )(place, *in_hbm((far,)), factor, acc, flags)
 
 
 def project_kernel(place, *refs):
@@ -386,16 +398,10 @@
             out[pl.ds(at, 2)] = result.astype(jnp.bfloat16).reshape(2, days, HD)
 
 
-def strided_attend(qkv, marks):
-    rows, cols = qkv.shape[1:]
-    peers = NY * NX * NH * NC
-    count = rows // peers
-    heads = cols // HD
-    packed = qkv.reshape(3, peers, count, heads, HD).transpose(1, 0, 3, 2, 4)
-    packed = packed.reshape(peers, 3 * heads * count, HD)
-    flags = marks.astype(jnp.bfloat16).reshape(peers, 1, count)
-    flags = jnp.pad(flags, ((0, 0), (0, 0), (0, HD - count)))
-    packed = jnp.concatenate([packed, flags], axis=1)
+def strided_attend(packed, heads):
+    slots, peers, _ = packed.shape
+    count = slots // (3 * heads)
+    packed = packed.transpose(1, 0, 2)
     packed = lax.all_to_all(packed, "seq", split_axis=0, concat_axis=0, tiled=True)
     packed = packed.transpose(1, 0, 2)
     result = pl.pallas_call(
@@ -412,8 +418,8 @@
     )(packed)
     result = result.transpose(1, 0, 2)
     result = lax.all_to_all(result, "seq", split_axis=0, concat_axis=0, tiled=True)
-    result = result.reshape(peers, heads, count, HD).transpose(0, 2, 1, 3)
-    return result.reshape(rows, cols)
+    result = result.reshape(peers, heads, count, HD).transpose(2, 0, 1, 3)
+    return result.reshape(count * peers, heads * HD)
 
 
 def body(tokens, w_local, w_strided, valid, band_reach):
@@ -431,11 +437,11 @@
     own_local = jnp.transpose(w_local, (1, 0, 2))
     gathered, strided, local = gather_all(tokens, own_strided, own_local)
     weight_strided = place_weights(place, *strided, 0)
-    acc = project_early(place, gathered, weight_strided)
+    acc, factor = project_early(place, gathered, weight_strided)
     acc, received = lax.optimization_barrier((acc, local[1]))
     weight_local = place_weights(place, local[0], received, 1)
-    qkv_strided = project_late(place, gathered, weight_strided, acc)
-    out_strided = strided_attend(qkv_strided, valid[0])
+    packed = project_late(place, gathered[5], factor, acc, valid[0])
+    out_strided = strided_attend(packed, w_strided.shape[2] // HD)
     qkv_local = project_local(place, gathered, weight_local)
     out_local = local_attend(qkv_local, valid[0], band_reach)
     return (out_local, out_strided)

time: 226 us -> 227 us (level)
  waiting for transfers between devices: 97.8 us -> 94.3 us
  local copies, waits for them, and re-layouts: 11.9 us -> 14.4 us
    ppermute x21, waiting for transfers between devices: 65.6 us -> 62.3 us  [swap(): return lax.ppermute(value, 'seq', seq_pairs(MOVES[kind]))]
    ppermute x21, starting transfers between devices: 32.9 us -> 35.3 us  [swap(): return lax.ppermute(value, 'seq', seq_pairs(MOVES[kind]))]
    unnamed x30 -> x38, local copies, waits for them, and re-layouts: 6.35 us -> 8.62 us
  transfers between devices with their start and end apart: 28 -> 28, of which waited for: 15 -> 14; matrix products, arithmetic and copies ran while one was open for 6% -> 6% of each run, Pallas kernels for 16% -> 15%
where the time goes in v4:
time: 227 us; the launch traced here: 226 us
  waiting for transfers between devices  94.3 us (42%)
  starting transfers between devices  67.5 us (30%)
  Pallas kernels  38.3 us (17%)
  local copies, waits for them, and re-layouts  14.4 us (6%)
  matrix products  6.44 us (3%)
  other arithmetic  4.17 us (2%)
    ppermute x21, waiting for transfers between devices, swap(): return lax.ppermute(value, 'seq', seq_pairs(MOVES[kind]))  62.3 us
    ppermute x21, starting transfers between devices, swap(): return lax.ppermute(value, 'seq', seq_pairs(MOVES[kind]))  35.3 us
    ppermute x5, waiting for transfers between devices, send_z(): return lax.ppermute(value, 'fsdp', pairs)  17.5 us
    pallas_call x1, Pallas kernels, project_local(): pl.pallas_call(project_kernel, out_shape=jax.ShapeDtypeStruct((3, rows, c...  14.1 us
    all_to_all x1, starting transfers between devices, strided_attend(): lax.all_to_all(packed, 'seq', split_axis=0, concat_axis=0, tiled=True)  11.9 us
    ppermute x5, starting transfers between devices, send_z(): return lax.ppermute(value, 'fsdp', pairs)  11.3 us
    all_to_all x1, starting transfers between devices, strided_attend(): lax.all_to_all(result, 'seq', split_axis=0, concat_axis=0, tiled=True)  9 us
    pallas_call x2, Pallas kernels, place_weights(): pl.pallas_call(functools.partial(place_kernel, (OWN_ORDERS[which], OTHER_...  8.93 us
  transfers between devices with their start and end apart: 28, of which 14 were waited for; matrix products, arithmetic and copies ran while one was open for 6% of the time, Pallas kernels for 15%

profile of v4, /device:TPU:1, one launch (start us, length us, event | category | flops | bytes accessed | tf_op | source)
XLA Modules:
  0.0 226.3 jit_solution(16825826166545346211)
XLA Ops:
  0.6 1.0 maximum_bitcast_fusion
  1.7 7.8 %collective-permute-start = (bf16[1,3,80,640]{3,2,1,0:T(8,128)(2,1)S(1)}, bf16[1,3,80,640]{3,2,1,0:T(8,128)(2,1)S(1)}, u32[]{:S(2)}, u32[]{:S(2)}) collective-permute-start(bf16[1,3,80,640]{3,2,1,0:T(8,128)(2,1)S(1)} %maximum_bitcast_fusion), channel_id=1, source_target_pairs={{0,8},{4,12},{8,0},{12,4},{16,24},{20,28},{24,16},{28,20},{32,40},... | collective-permute-start | bytes 921608 | tf_op jit(solution)/shard_map/ppermute | solution.py:53
  9.5 1.2 collective-permute-start.3
  10.7 6.2 %collective-permute-done = bf16[1,3,80,640]{3,2,1,0:T(8,128)(2,1)S(1)} collective-permute-done((bf16[1,3,80,640]{3,2,1,0:T(8,128)(2,1)S(1)}, bf16[1,3,80,640]{3,2,1,0:T(8,128)(2,1)S(1)}, u32[]{:S(2)}, u32[]{:S(2)}) %collective-permute-start) | collective-permute-done | bytes 307232 | tf_op jit(solution)/shard_map/ppermute | solution.py:53
  16.9 1.8 collective-permute-start.6
  18.8 6.1 %collective-permute-start.1 = (bf16[640,1280]{1,0:T(8,128)(2,1)}, bf16[640,1280]{1,0:T(8,128)(2,1)S(1)}, u32[]{:S(2)}, u32[]{:S(2)}) collective-permute-start(bf16[640,1280]{1,0:T(8,128)(2,1)} %refs_0_.1), channel_id=1, source_target_pairs={{0,1},{1,0},{2,3},{3,2},{4,5},{5,4},{6,7},{7,6},{8,9},{9,8},{10,11... | collective-permute-start | bytes 4915208 | tf_op jit(solution)/shard_map/ppermute | solution.py:106
  24.9 0.8 collective-permute-start.2
  25.7 2.6 %collective-permute-start.4 = (bf16[2,3,80,640]{3,2,1,0:T(8,128)(2,1)S(1)}, bf16[2,3,80,640]{3,2,1,0:T(8,128)(2,1)S(1)}, u32[]{:S(2)}, u32[]{:S(2)}) collective-permute-start(bf16[2,3,80,640]{3,2,1,0:T(8,128)(2,1)S(1)} %pad_maximum_fusion.6), channel_id=1, source_target_pairs={{0,48},{4,52},{8,56},{12,60},{16,32},{20,36},{24,40},{28,44},{32,1... | collective-permute-start | bytes 1843208 | tf_op jit(solution)/shard_map/ppermute | solution.py:53
  28.3 2.0 collective-permute-start.7
  30.4 9.9 %collective-permute-done.4 = bf16[2,3,80,640]{3,2,1,0:T(8,128)(2,1)S(1)} collective-permute-done((bf16[2,3,80,640]{3,2,1,0:T(8,128)(2,1)S(1)}, bf16[2,3,80,640]{3,2,1,0:T(8,128)(2,1)S(1)}, u32[]{:S(2)}, u32[]{:S(2)}) %collective-permute-start.4) | collective-permute-done | bytes 614432 | tf_op jit(solution)/shard_map/ppermute | solution.py:53
  40.3 0.3 collective-permute-start.5
  40.6 2.0 collective-permute-done.7
  43.0 7.1 %collective-permute-done.5 = bf16[4,3,80,256]{3,2,1,0:T(8,128)(2,1)S(1)} collective-permute-done((bf16[4,3,80,256]{3,2,1,0:T(8,128)(2,1)S(1)}, bf16[4,3,80,256]{3,2,1,0:T(8,128)(2,1)S(1)}, u32[]{:S(2)}, u32[]{:S(2)}) %collective-permute-start.5) | collective-permute-done | bytes 491552 | tf_op jit(solution)/shard_map/ppermute | solution.py:53
  50.2 2.1 collective-permute-done.8
  52.4 7.0 %collective-permute-done.1.refs_1_ = bf16[640,1280]{1,0:T(8,128)(2,1)S(1)} collective-permute-done((bf16[640,1280]{1,0:T(8,128)(2,1)}, bf16[640,1280]{1,0:T(8,128)(2,1)S(1)}, u32[]{:S(2)}, u32[]{:S(2)}) %collective-permute-start.1) | collective-permute-done | bytes 1638432 | tf_op jit(solution)/shard_map/ppermute | solution.py:106
  59.4 2.0 collective-permute-start.11
  61.4 2.5 %collective-permute-start.14 = (bf16[4,3,80,384]{3,2,1,0:T(8,128)(2,1)S(1)}, bf16[4,3,80,384]{3,2,1,0:T(8,128)(2,1)S(1)}, u32[]{:S(2)}, u32[]{:S(2)}) collective-permute-start(bf16[4,3,80,384]{3,2,1,0:T(8,128)(2,1)S(1)} %slice.29), channel_id=1, source_target_pairs={{0,48},{4,52},{8,56},{12,60},{16,32},{20,36},{24,40},{28,44},{32,1... | collective-permute-start | bytes 2211848 | tf_op jit(solution)/shard_map/ppermute | solution.py:53
  63.8 0.8 collective-permute-start.13
  64.6 1.3 collective-permute-start.10
  65.9 1.9 collective-permute-start.9
  67.8 10.0 %collective-permute-done.14 = bf16[4,3,80,384]{3,2,1,0:T(8,128)(2,1)S(1)} collective-permute-done((bf16[4,3,80,384]{3,2,1,0:T(8,128)(2,1)S(1)}, bf16[4,3,80,384]{3,2,1,0:T(8,128)(2,1)S(1)}, u32[]{:S(2)}, u32[]{:S(2)}) %collective-permute-start.14) | collective-permute-done | bytes 737312 | tf_op jit(solution)/shard_map/ppermute | solution.py:53
  77.8 2.5 %collective-permute-start.12 = (bf16[8,3,80,256]{3,2,1,0:T(8,128)(2,1)S(1)}, bf16[8,3,80,256]{3,2,1,0:T(8,128)(2,1)S(1)}, u32[]{:S(2)}, u32[]{:S(2)}) collective-permute-start(bf16[8,3,80,256]{3,2,1,0:T(8,128)(2,1)S(1)} %pad_maximum_fusion.3.refs_4_), channel_id=1, source_target_pairs={{0,48},{4,52},{8,56},{12,60},{16,32},{20,36},{24,40},{28,44},{32,1... | collective-permute-start | bytes 2949128 | tf_op jit(solution)/shard_map/ppermute | solution.py:53
  80.3 17.0 %collective-permute-done.13 = bf16[4,3,80,384]{3,2,1,0:T(8,128)(2,1)S(1)} collective-permute-done((bf16[4,3,80,384]{3,2,1,0:T(8,128)(2,1)S(1)}, bf16[4,3,80,384]{3,2,1,0:T(8,128)(2,1)S(1)}, u32[]{:S(2)}, u32[]{:S(2)}) %collective-permute-start.13) | collective-permute-done | bytes 737312 | tf_op jit(solution)/shard_map/ppermute | solution.py:53
  97.3 3.4 %collective-permute-start.17 = (bf16[8,3,80,256]{3,2,1,0:T(8,128)(2,1)S(1)}, bf16[8,3,80,256]{3,2,1,0:T(8,128)(2,1)S(1)}, u32[]{:S(2)}, u32[]{:S(2)}) collective-permute-start(bf16[8,3,80,256]{3,2,1,0:T(8,128)(2,1)S(1)} %pad_maximum_fusion.2.refs_0_), channel_id=1, source_target_pairs={{0,4},{4,0},{8,12},{12,8},{16,20},{20,16},{24,28},{28,24},{32,36},... | collective-permute-start | bytes 2949128 | tf_op jit(solution)/shard_map/ppermute | solution.py:53
  100.7 0.2 pad_maximum_fusion.1.refs_4_
  100.9 1.4 pad_maximum_fusion.refs_0_
  102.5 1.3 collective-permute-start.22
  103.8 2.1 collective-permute-start.18
  105.9 0.1 collective-permute-start.20
  106.0 0.8 copy-done.8
  106.9 1.3 collective-permute-start.15
  108.4 0.4 collective-permute-start.16
  108.8 0.9 collective-permute-done.20.refs_7_
  109.7 0.4 collective-permute-start.24
  110.0 3.9 %shard_map.68.refs_5_ = bf16[3,5120,256]{2,1,0:T(8,128)(2,1)S(1)} custom-call(s32[5]{0:T(128)S(1)} %stack.23.place, bf16[8,3,80,256]{3,2,1,0:T(8,128)(2,1)} %copy-done.4, bf16[8,3,80,256]{3,2,1,0:T(8,128)(2,1)} %copy-done.8, bf16[8,3,80,256]{3,2,1,0:T(8,128)(2,1)} %copy-done.6, bf16[8,3,80,256]{3,2,1,0:T(8,128)(2,1)} %collective-permute-done.18.refs_3_, ...), custom_call_target="tpu_custom_call" | custom-call | bytes 15728640 | tf_op jit(solution)/shard_map/pallas_call | solution.py:91
  114.0 3.1 %copy-done = bf16[3,5120,256]{2,1,0:T(8,128)(2,1)} copy-done((bf16[3,5120,256]{2,1,0:T(8,128)(2,1)}, bf16[3,5120,256]{2,1,0:T(8,128)(2,1)S(1)}, u32[]{:S(2)}) %copy-start) | copy-done | bytes 7864344
  117.0 8.2 %shard_map.69 = (f32[3,640,256]{2,1,0:T(8,128)S(1)}, bf16[3,1280,256]{2,1,0:T(8,128)(2,1)S(1)}) custom-call(s32[5]{0:T(128)S(1)} %stack.23.place, bf16[640,1280]{1,0:T(8,128)(2,1)} %refs_0_.1, bf16[640,1280]{1,0:T(8,128)(2,1)} %copy-done.14, bf16[640,1280]{1,0:T(8,128)(2,1)} %copy-done.15, bf16[640,1280]{1,0:T(8,128)(2,1)} %collective-permute-done.9.refs_3_, ...), custom_call_target="tpu_custom_call" | custom-call | flops 5033164800 | bytes 16384000 | tf_op jit(solution)/shard_map/pallas_call | solution.py:256
  125.2 1.3 copy-done.1
  126.5 7.0 %collective-permute-done.21.refs_2_ = bf16[8,3,80,384]{3,2,1,0:T(8,128)(2,1)} collective-permute-done((bf16[8,3,80,384]{3,2,1,0:T(8,128)(2,1)}, bf16[8,3,80,384]{3,2,1,0:T(8,128)(2,1)}, u32[]{:S(2)}, u32[]{:S(2)}) %collective-permute-start.21) | collective-permute-done | bytes 1474592 | tf_op jit(solution)/shard_map/ppermute | solution.py:53
  133.6 4.0 %collective-permute-start.23 = (bf16[8,3,80,384]{3,2,1,0:T(8,128)(2,1)}, bf16[8,3,80,384]{3,2,1,0:T(8,128)(2,1)}, u32[]{:S(2)}, u32[]{:S(2)}) collective-permute-start(bf16[8,3,80,384]{3,2,1,0:T(8,128)(2,1)} %collective-permute-done.21.refs_2_), channel_id=1, source_target_pairs={{0,4},{4,0},{8,12},{12,8},{16,20},{20,16},{24,28},{28,24},{32,36},... | collective-permute-start | bytes 4423688 | tf_op jit(solution)/shard_map/ppermute | solution.py:53
  137.7 0.1 copy.52
  137.8 10.5 %collective-permute-done.15.refs_5_.far = bf16[640,1280]{1,0:T(8,128)(2,1)} collective-permute-done((bf16[640,1280]{1,0:T(8,128)(2,1)}, bf16[640,1280]{1,0:T(8,128)(2,1)}, u32[]{:S(2)}, u32[]{:S(2)}) %collective-permute-start.15) | collective-permute-done | bytes 1638432 | tf_op jit(solution)/shard_map/ppermute | solution.py:106
  148.2 1.5 copy-done.2
  149.8 3.8 %shard_map.72 = bf16[61,64,128]{2,1,0:T(8,128)(2,1)S(1)} custom-call(s32[5]{0:T(128)S(1)} %stack.23.place, bf16[640,1280]{1,0:T(8,128)(2,1)} %collective-permute-done.15.refs_5_.far, bf16[3,1280,256]{2,1,0:T(8,128)(2,1)S(1)} %copy-done.2, f32[3,640,256]{2,1,0:T(8,128)S(1)} %get-tuple-element.39.acc, bf16[64,128]{1,0:T(8,128)(2,1)S(1)} %pad.4.flags), custom_call_target="tpu_custom_call" | custom-call | flops 1258291200 | bytes 6553600 | tf_op jit(solution)/shard_map/pallas_call | solution.py:286
  153.6 1.6 copy.53
  155.2 11.9 %all-to-all-start = ((bf16[64,61,128]{2,1,0:T(8,128)(2,1)}), bf16[64,61,128]{2,1,0:T(8,128)(2,1)S(1)}, u32[]{:S(2)}, u32[]{:S(2)}) async-start(bf16[64,61,128]{2,1,0:T(8,128)(2,1)} %copy.53), calls=%async_computation | async-start | bytes 2097152 | tf_op jit(solution)/shard_map/all_to_all | solution.py:405
  167.2 1.0 iota_compare_fusion.1
  168.2 5.0 %shard_map.70.refs_6_ = bf16[3,5120,384]{2,1,0:T(8,128)(2,1)S(1)} custom-call(s32[5]{0:T(128)S(1)} %stack.23.place, bf16[8,3,80,384]{3,2,1,0:T(8,128)(2,1)} %pad_maximum_fusion.refs_0_, bf16[8,3,80,384]{3,2,1,0:T(8,128)(2,1)} %collective-permute-done.16.refs_1_, bf16[8,3,80,384]{3,2,1,0:T(8,128)(2,1)} %collective-permute-done.21.refs_2_, ...), custom_call_target="tpu_custom_call" | custom-call | bytes 23592960 | tf_op jit(solution)/shard_map/pallas_call | solution.py:91
  173.3 14.1 %shard_map.71 = bf16[3,640,384]{2,1,0:T(8,128)(2,1)S(1)} custom-call(s32[5]{0:T(128)S(1)} %stack.23.place, bf16[640,1280]{1,0:T(8,128)(2,1)} %refs_0_.1, bf16[640,1280]{1,0:T(8,128)(2,1)} %copy-done.14, bf16[640,1280]{1,0:T(8,128)(2,1)} %copy-done.15, bf16[640,1280]{1,0:T(8,128)(2,1)} %collective-permute-done.9.refs_3_, bf16[640,1280]{1,0:T(8,128)(2,1)} %copy-done.16, ...), custom_call_target="tpu_custom_call" | custom-call | flops 7549747200 | bytes 19824640 | tf_op jit(solution)/shard_map/pallas_call | solution.py:331
  187.4 0.1 fusion.22
  187.5 0.3 copy.48
  187.8 0.3 copy.47
  188.1 1.0 copy.46
  189.1 6.8 %all-to-all-done = bf16[64,61,128]{2,1,0:T(8,128)(2,1)S(1)} async-done(((bf16[64,61,128]{2,1,0:T(8,128)(2,1)}), bf16[64,61,128]{2,1,0:T(8,128)(2,1)S(1)}, u32[]{:S(2)}, u32[]{:S(2)}) %all-to-all-start) | async-done | bytes 999456 | tf_op jit(solution)/shard_map/all_to_all | solution.py:405
  195.8 0.7 copy.65
  196.5 3.3 %shard_map.73 = bf16[20,64,128]{2,1,0:T(8,128)(2,1)S(1)} custom-call(bf16[61,64,128]{2,1,0:T(8,128)(2,1)S(1)} %bitcast.35), custom_call_target="tpu_custom_call" | custom-call | flops 83886080 | bytes 1310720 | tf_op jit(solution)/shard_map/pallas_call | solution.py:407
  199.8 1.0 copy.55
  200.8 9.0 %all-to-all-start.1 = ((bf16[64,20,128]{2,1,0:T(8,128)(2,1)}), bf16[64,20,128]{2,1,0:T(8,128)(2,1)S(1)}, u32[]{:S(2)}, u32[]{:S(2)}) async-start(bf16[64,20,128]{2,1,0:T(8,128)(2,1)} %copy.55), calls=%async_computation.1 | async-start | bytes 786432 | tf_op jit(solution)/shard_map/all_to_all | solution.py:420
  209.8 2.5 %fusion.23 = f32[3,640]{1,0:T(4,128)S(1)} fusion(s32[3,640]{1,0:T(4,128)S(1)} %broadcast_subtract_fusion, s32[640]{0:T(1024)S(1)} %add_select_fusion, pred[640,640]{0,1:T(8,128)(4,1)S(1)} %get-tuple-element.54, pred[640,640]{0,1:T(8,128)(4,1)S(1)} %copy-done.11, bf16[640,3,128]{0,2,1:T(8,128)(2,1)S(1)} %bitcast.41, bf16[640,3,128]{0,2,1:T(8,128)(2,1)S(1)} %bitcast.39), kind=kOutput, calls=%fused_computation.47 | convolution fusion | flops 323175040 | bytes 1820160 | tf_op jit(solution)/shard_map/sub | solution.py:366
  212.3 3.9 %fusion.10 = bf16[3,128,640]{2,1,0:T(8,128)(2,1)S(1)} fusion(bf16[640,3,128]{0,2,1:T(8,128)(2,1)S(1)} %bitcast.43, f32[3,640]{1,0:T(4,128)S(1)} %fusion.23, s32[3,640]{1,0:T(4,128)S(1)} %broadcast_subtract_fusion, s32[640]{0:T(1024)S(1)} %add_select_fusion, pred[640,640]{0,1:T(8,128)(4,1)S(1)} %get-tuple-element.54, ...), kind=kOutput, calls=%fused_computation.17 | convolution fusion | flops 639224320 | bytes 2803200 | tf_op jit(solution)/shard_map/hqk,khc->qhc/dot_general | solution.py:368
  216.3 1.0 copy.58
  217.3 7.8 %all-to-all-done.1 = bf16[64,20,128]{2,1,0:T(8,128)(2,1)S(1)} async-done(((bf16[64,20,128]{2,1,0:T(8,128)(2,1)}), bf16[64,20,128]{2,1,0:T(8,128)(2,1)S(1)}, u32[]{:S(2)}, u32[]{:S(2)}) %all-to-all-start.1) | async-done | bytes 327712 | tf_op jit(solution)/shard_map/all_to_all | solution.py:420
  225.2 0.3 copy.57
  225.5 0.8 copy.66
  (68 shorter events, 1.5 us)
Async XLA Ops:
  1.7 15.3 %collective-permute-start = (bf16[1,3,80,640]{3,2,1,0:T(8,128)(2,1)S(1)}, bf16[1,3,80,640]{3,2,1,0:T(8,128)(2,1)S(1)}, u32[]{:S(2)}, u32[]{:S(2)}) collective-permute-start(bf16[1,3,80,640]{3,2,1,0:T(8,128)(2,1)S(1)} %maximum_bitcast_fusion), channel_id=1, source_target_pairs={{0,8},{4,12},{8,0},{12,4},{16,24},{20,28},{24,16},{28,20},{32,40},... | collective-permute-start | bytes 921608 | tf_op jit(solution)/shard_map/ppermute | solution.py:53
  9.5 16.1 %collective-permute-start.3 = (bf16[1,3,80,640]{3,2,1,0:T(8,128)(2,1)S(1)}, bf16[1,3,80,640]{3,2,1,0:T(8,128)(2,1)S(1)}, u32[]{:S(2)}, u32[]{:S(2)}) collective-permute-start(bf16[1,3,80,640]{3,2,1,0:T(8,128)(2,1)S(1)} %maximum_bitcast_fusion), channel_id=1, source_target_pairs={{0,16},{4,20},{8,24},{12,28},{16,0},{20,4},{24,8},{28,12},{32,48},... | collective-permute-start | bytes 921608 | tf_op jit(solution)/shard_map/ppermute | solution.py:53
  16.9 11.3 %collective-permute-start.6 = (bf16[1,3,80,640]{3,2,1,0:T(8,128)(2,1)S(1)}, bf16[1,3,80,640]{3,2,1,0:T(8,128)(2,1)S(1)}, u32[]{:S(2)}, u32[]{:S(2)}) collective-permute-start(bf16[1,3,80,640]{3,2,1,0:T(8,128)(2,1)S(1)} %collective-permute-done), channel_id=1, source_target_pairs={{0,64},{4,68},{8,72},{12,76},{16,80},{20,84},{24,88},{28,92},{32,9... | collective-permute-start | bytes 921608 | tf_op jit(solution)/shard_map/ppermute | solution.py:53
  18.8 40.6 %collective-permute-start.1 = (bf16[640,1280]{1,0:T(8,128)(2,1)}, bf16[640,1280]{1,0:T(8,128)(2,1)S(1)}, u32[]{:S(2)}, u32[]{:S(2)}) collective-permute-start(bf16[640,1280]{1,0:T(8,128)(2,1)} %refs_0_.1), channel_id=1, source_target_pairs={{0,1},{1,0},{2,3},{3,2},{4,5},{5,4},{6,7},{7,6},{8,9},{9,8},{10,11... | collective-permute-start | bytes 4915208 | tf_op jit(solution)/shard_map/ppermute | solution.py:106
  24.9 34.5 %collective-permute-start.2 = (bf16[640,1280]{1,0:T(8,128)(2,1)}, bf16[640,1280]{1,0:T(8,128)(2,1)S(1)}, u32[]{:S(2)}, u32[]{:S(2)}) collective-permute-start(bf16[640,1280]{1,0:T(8,128)(2,1)} %refs_0_.1), channel_id=1, source_target_pairs={{1,2},{2,1},{5,6},{6,5},{9,10},{10,9},{13,14},{14,13},{17,18},{18,... | collective-permute-start | bytes 4915208 | tf_op jit(solution)/shard_map/ppermute | solution.py:106
  25.7 14.6 %collective-permute-start.4 = (bf16[2,3,80,640]{3,2,1,0:T(8,128)(2,1)S(1)}, bf16[2,3,80,640]{3,2,1,0:T(8,128)(2,1)S(1)}, u32[]{:S(2)}, u32[]{:S(2)}) collective-permute-start(bf16[2,3,80,640]{3,2,1,0:T(8,128)(2,1)S(1)} %pad_maximum_fusion.6), channel_id=1, source_target_pairs={{0,48},{4,52},{8,56},{12,60},{16,32},{20,36},{24,40},{28,44},{32,1... | collective-permute-start | bytes 1843208 | tf_op jit(solution)/shard_map/ppermute | solution.py:53
  28.3 14.3 %collective-permute-start.7 = (bf16[2,3,80,640]{3,2,1,0:T(8,128)(2,1)S(1)}, bf16[2,3,80,640]{3,2,1,0:T(8,128)(2,1)S(1)}, u32[]{:S(2)}, u32[]{:S(2)}) collective-permute-start(bf16[2,3,80,640]{3,2,1,0:T(8,128)(2,1)S(1)} %pad_maximum_fusion.7), channel_id=1, source_target_pairs={{0,192},{4,196},{8,200},{12,204},{16,208},{20,212},{24,216},{28,22... | collective-permute-start | bytes 1843208 | tf_op jit(solution)/shard_map/ppermute | solution.py:53
  40.3 9.8 %collective-permute-start.5 = (bf16[4,3,80,256]{3,2,1,0:T(8,128)(2,1)S(1)}, bf16[4,3,80,256]{3,2,1,0:T(8,128)(2,1)S(1)}, u32[]{:S(2)}, u32[]{:S(2)}) collective-permute-start(bf16[4,3,80,256]{3,2,1,0:T(8,128)(2,1)S(1)} %pad_maximum_fusion.8), channel_id=1, source_target_pairs={{0,64},{4,68},{8,72},{12,76},{16,80},{20,84},{24,88},{28,92},{32,9... | collective-permute-start | bytes 1474568 | tf_op jit(solution)/shard_map/ppermute | solution.py:53
  42.8 9.5 %collective-permute-start.8 = (bf16[4,3,80,256]{3,2,1,0:T(8,128)(2,1)S(1)}, bf16[4,3,80,256]{3,2,1,0:T(8,128)(2,1)S(1)}, u32[]{:S(2)}, u32[]{:S(2)}) collective-permute-start(bf16[4,3,80,256]{3,2,1,0:T(8,128)(2,1)S(1)} %slice.28), channel_id=1, source_target_pairs={{0,16},{4,20},{8,24},{12,28},{16,0},{20,4},{24,8},{28,12},{32,48},... | collective-permute-start | bytes 1474568 | tf_op jit(solution)/shard_map/ppermute | solution.py:53
  50.2 50.7 %copy-start.4 = (bf16[8,3,80,256]{3,2,1,0:T(8,128)(2,1)}, bf16[8,3,80,256]{3,2,1,0:T(8,128)(2,1)S(1)}, u32[]{:S(2)}) copy-start(bf16[8,3,80,256]{3,2,1,0:T(8,128)(2,1)S(1)} %pad_maximum_fusion.2.refs_0_) | copy-start | bytes 2949124
  52.4 50.0 %copy-start.5 = (bf16[8,3,80,256]{3,2,1,0:T(8,128)(2,1)}, bf16[8,3,80,256]{3,2,1,0:T(8,128)(2,1)S(1)}, u32[]{:S(2)}) copy-start(bf16[8,3,80,256]{3,2,1,0:T(8,128)(2,1)S(1)} %pad_maximum_fusion.3.refs_4_) | copy-start | bytes 2949124
  59.4 43.0 %copy-start.14 = (bf16[640,1280]{1,0:T(8,128)(2,1)}, bf16[640,1280]{1,0:T(8,128)(2,1)S(1)}, u32[]{:S(2)}) copy-start(bf16[640,1280]{1,0:T(8,128)(2,1)S(1)} %collective-permute-done.1.refs_1_) | copy-start | bytes 4915204
  59.4 48.8 %copy-start.15 = (bf16[640,1280]{1,0:T(8,128)(2,1)}, bf16[640,1280]{1,0:T(8,128)(2,1)S(1)}, u32[]{:S(2)}) copy-start(bf16[640,1280]{1,0:T(8,128)(2,1)S(1)} %collective-permute-done.2.refs_2_) | copy-start | bytes 4915204
  59.4 41.3 %collective-permute-start.11 = (bf16[8,3,80,256]{3,2,1,0:T(8,128)(2,1)S(1)}, bf16[8,3,80,256]{3,2,1,0:T(8,128)(2,1)S(1)}, u32[]{:S(2)}, u32[]{:S(2)}) collective-permute-start(bf16[8,3,80,256]{3,2,1,0:T(8,128)(2,1)S(1)} %pad_maximum_fusion.2.refs_0_), channel_id=1, source_target_pairs={{0,192},{4,196},{8,200},{12,204},{16,208},{20,212},{24,216},{28,22... | collective-permute-start | bytes 2949128 | tf_op jit(solution)/shard_map/ppermute | solution.py:53
  61.4 16.5 %collective-permute-start.14 = (bf16[4,3,80,384]{3,2,1,0:T(8,128)(2,1)S(1)}, bf16[4,3,80,384]{3,2,1,0:T(8,128)(2,1)S(1)}, u32[]{:S(2)}, u32[]{:S(2)}) collective-permute-start(bf16[4,3,80,384]{3,2,1,0:T(8,128)(2,1)S(1)} %slice.29), channel_id=1, source_target_pairs={{0,48},{4,52},{8,56},{12,60},{16,32},{20,36},{24,40},{28,44},{32,1... | collective-permute-start | bytes 2211848 | tf_op jit(solution)/shard_map/ppermute | solution.py:53
  63.8 33.4 %collective-permute-start.13 = (bf16[4,3,80,384]{3,2,1,0:T(8,128)(2,1)S(1)}, bf16[4,3,80,384]{3,2,1,0:T(8,128)(2,1)S(1)}, u32[]{:S(2)}, u32[]{:S(2)}) collective-permute-start(bf16[4,3,80,384]{3,2,1,0:T(8,128)(2,1)S(1)} %pad_maximum_fusion.4), channel_id=1, source_target_pairs={{0,192},{4,196},{8,200},{12,204},{16,208},{20,212},{24,216},{28,22... | collective-permute-start | bytes 2211848 | tf_op jit(solution)/shard_map/ppermute | solution.py:53
  64.6 37.8 %collective-permute-start.10 = (bf16[640,1280]{1,0:T(8,128)(2,1)S(1)}, bf16[640,1280]{1,0:T(8,128)(2,1)S(1)}, u32[]{:S(2)}, u32[]{:S(2)}) collective-permute-start(bf16[640,1280]{1,0:T(8,128)(2,1)S(1)} %collective-permute-done.2.refs_2_), channel_id=1, source_target_pairs={{2,3},{1,0},{6,7},{5,4},{10,11},{9,8},{14,15},{13,12},{18,19},{17,... | collective-permute-start | bytes 4915208 | tf_op jit(solution)/shard_map/ppermute | solution.py:106
  65.9 36.5 %collective-permute-start.9 = (bf16[640,1280]{1,0:T(8,128)(2,1)S(1)}, bf16[640,1280]{1,0:T(8,128)(2,1)}, u32[]{:S(2)}, u32[]{:S(2)}) collective-permute-start(bf16[640,1280]{1,0:T(8,128)(2,1)S(1)} %collective-permute-done.1.refs_1_), channel_id=1, source_target_pairs={{1,2},{2,1},{5,6},{6,5},{9,10},{10,9},{13,14},{14,13},{17,18},{18,... | collective-permute-start | bytes 4915208 | tf_op jit(solution)/shard_map/ppermute | solution.py:106
  77.8 24.6 %collective-permute-start.12 = (bf16[8,3,80,256]{3,2,1,0:T(8,128)(2,1)S(1)}, bf16[8,3,80,256]{3,2,1,0:T(8,128)(2,1)S(1)}, u32[]{:S(2)}, u32[]{:S(2)}) collective-permute-start(bf16[8,3,80,256]{3,2,1,0:T(8,128)(2,1)S(1)} %pad_maximum_fusion.3.refs_4_), channel_id=1, source_target_pairs={{0,48},{4,52},{8,56},{12,60},{16,32},{20,36},{24,40},{28,44},{32,1... | collective-permute-start | bytes 2949128 | tf_op jit(solution)/shard_map/ppermute | solution.py:53
  97.3 8.7 %collective-permute-start.17 = (bf16[8,3,80,256]{3,2,1,0:T(8,128)(2,1)S(1)}, bf16[8,3,80,256]{3,2,1,0:T(8,128)(2,1)S(1)}, u32[]{:S(2)}, u32[]{:S(2)}) collective-permute-start(bf16[8,3,80,256]{3,2,1,0:T(8,128)(2,1)S(1)} %pad_maximum_fusion.2.refs_0_), channel_id=1, source_target_pairs={{0,4},{4,0},{8,12},{12,8},{16,20},{20,16},{24,28},{28,24},{32,36},... | collective-permute-start | bytes 2949128 | tf_op jit(solution)/shard_map/ppermute | solution.py:53
  100.6 3.2 %copy-start.6 = (bf16[8,3,80,256]{3,2,1,0:T(8,128)(2,1)}, bf16[8,3,80,256]{3,2,1,0:T(8,128)(2,1)S(1)}, u32[]{:S(2)}) copy-start(bf16[8,3,80,256]{3,2,1,0:T(8,128)(2,1)S(1)} %collective-permute-done.11.refs_2_) | copy-start | bytes 2949124
  100.6 5.4 %collective-permute-start.19 = (bf16[8,3,80,256]{3,2,1,0:T(8,128)(2,1)S(1)}, bf16[8,3,80,256]{3,2,1,0:T(8,128)(2,1)S(1)}, u32[]{:S(2)}, u32[]{:S(2)}) collective-permute-start(bf16[8,3,80,256]{3,2,1,0:T(8,128)(2,1)S(1)} %pad_maximum_fusion.3.refs_4_), channel_id=1, source_target_pairs={{0,4},{4,0},{8,12},{12,8},{16,20},{20,16},{24,28},{28,24},{32,36},... | collective-permute-start | bytes 2949128 | tf_op jit(solution)/shard_map/ppermute | solution.py:53
  100.9 13.0 %copy-start.3 = (bf16[8,3,80,384]{3,2,1,0:T(8,128)(2,1)}, bf16[8,3,80,384]{3,2,1,0:T(8,128)(2,1)S(1)}, u32[]{:S(2)}) copy-start(bf16[8,3,80,384]{3,2,1,0:T(8,128)(2,1)S(1)} %pad_maximum_fusion.1.refs_4_) | copy-start | bytes 4423684
  102.4 7.7 %copy-start.7 = (bf16[8,3,80,256]{3,2,1,0:T(8,128)(2,1)}, bf16[8,3,80,256]{3,2,1,0:T(8,128)(2,1)S(1)}, u32[]{:S(2)}) copy-start(bf16[8,3,80,256]{3,2,1,0:T(8,128)(2,1)S(1)} %collective-permute-done.12.refs_6_) | copy-start | bytes 2949124
  102.4 5.8 %copy-start.16 = (bf16[640,1280]{1,0:T(8,128)(2,1)}, bf16[640,1280]{1,0:T(8,128)(2,1)S(1)}, u32[]{:S(2)}) copy-start(bf16[640,1280]{1,0:T(8,128)(2,1)S(1)} %collective-permute-done.10.refs_4_) | copy-start | bytes 4915204
  102.4 31.1 %collective-permute-start.21 = (bf16[8,3,80,384]{3,2,1,0:T(8,128)(2,1)}, bf16[8,3,80,384]{3,2,1,0:T(8,128)(2,1)}, u32[]{:S(2)}, u32[]{:S(2)}) collective-permute-start(bf16[8,3,80,384]{3,2,1,0:T(8,128)(2,1)} %pad_maximum_fusion.refs_0_), channel_id=1, source_target_pairs={{0,64},{4,68},{8,72},{12,76},{16,80},{20,84},{24,88},{28,92},{32,9... | collective-permute-start | bytes 4423688 | tf_op jit(solution)/shard_map/ppermute | solution.py:53
  102.5 31.0 %collective-permute-start.22 = (bf16[8,3,80,384]{3,2,1,0:T(8,128)(2,1)S(1)}, bf16[8,3,80,384]{3,2,1,0:T(8,128)(2,1)}, u32[]{:S(2)}, u32[]{:S(2)}) collective-permute-start(bf16[8,3,80,384]{3,2,1,0:T(8,128)(2,1)S(1)} %pad_maximum_fusion.1.refs_4_), channel_id=1, source_target_pairs={{0,16},{4,20},{8,24},{12,28},{16,0},{20,4},{24,8},{28,12},{32,48},... | collective-permute-start | bytes 4423688 | tf_op jit(solution)/shard_map/ppermute | solution.py:53
  103.8 4.5 %collective-permute-start.18 = (bf16[8,3,80,256]{3,2,1,0:T(8,128)(2,1)S(1)}, bf16[8,3,80,256]{3,2,1,0:T(8,128)(2,1)}, u32[]{:S(2)}, u32[]{:S(2)}) collective-permute-start(bf16[8,3,80,256]{3,2,1,0:T(8,128)(2,1)S(1)} %collective-permute-done.11.refs_2_), channel_id=1, source_target_pairs={{0,4},{4,0},{8,12},{12,8},{16,20},{20,16},{24,28},{28,24},{32,36},... | collective-permute-start | bytes 2949128 | tf_op jit(solution)/shard_map/ppermute | solution.py:53
  105.9 1.0 copy-start.8
  105.9 3.7 %collective-permute-start.20 = (bf16[8,3,80,256]{3,2,1,0:T(8,128)(2,1)S(1)}, bf16[8,3,80,256]{3,2,1,0:T(8,128)(2,1)}, u32[]{:S(2)}, u32[]{:S(2)}) collective-permute-start(bf16[8,3,80,256]{3,2,1,0:T(8,128)(2,1)S(1)} %collective-permute-done.12.refs_6_), channel_id=1, source_target_pairs={{0,4},{4,0},{8,12},{12,8},{16,20},{20,16},{24,28},{28,24},{32,36},... | collective-permute-start | bytes 2949128 | tf_op jit(solution)/shard_map/ppermute | solution.py:53
  106.9 1.3 copy-start.9
  106.9 41.3 %collective-permute-start.15 = (bf16[640,1280]{1,0:T(8,128)(2,1)}, bf16[640,1280]{1,0:T(8,128)(2,1)}, u32[]{:S(2)}, u32[]{:S(2)}) collective-permute-start(bf16[640,1280]{1,0:T(8,128)(2,1)} %collective-permute-done.9.refs_3_), channel_id=1, source_target_pairs={{2,3},{1,0},{6,7},{5,4},{10,11},{9,8},{14,15},{13,12},{18,19},{17,... | collective-permute-start | bytes 4915208 | tf_op jit(solution)/shard_map/ppermute | solution.py:106
  108.4 59.8 %collective-permute-start.16 = (bf16[8,3,80,384]{3,2,1,0:T(8,128)(2,1)}, bf16[8,3,80,384]{3,2,1,0:T(8,128)(2,1)}, u32[]{:S(2)}, u32[]{:S(2)}) collective-permute-start(bf16[8,3,80,384]{3,2,1,0:T(8,128)(2,1)} %pad_maximum_fusion.refs_0_), channel_id=1, source_target_pairs={{0,4},{4,0},{8,12},{12,8},{16,20},{20,16},{24,28},{28,24},{32,36},... | collective-permute-start | bytes 4423688 | tf_op jit(solution)/shard_map/ppermute | solution.py:53
  109.7 58.5 %collective-permute-start.24 = (bf16[8,3,80,384]{3,2,1,0:T(8,128)(2,1)S(1)}, bf16[8,3,80,384]{3,2,1,0:T(8,128)(2,1)}, u32[]{:S(2)}, u32[]{:S(2)}) collective-permute-start(bf16[8,3,80,384]{3,2,1,0:T(8,128)(2,1)S(1)} %pad_maximum_fusion.1.refs_4_), channel_id=1, source_target_pairs={{0,4},{4,0},{8,12},{12,8},{16,20},{20,16},{24,28},{28,24},{32,36},... | collective-permute-start | bytes 4423688 | tf_op jit(solution)/shard_map/ppermute | solution.py:53
  114.0 3.1 %copy-start = (bf16[3,5120,256]{2,1,0:T(8,128)(2,1)}, bf16[3,5120,256]{2,1,0:T(8,128)(2,1)S(1)}, u32[]{:S(2)}) copy-start(bf16[3,5120,256]{2,1,0:T(8,128)(2,1)S(1)} %shard_map.68.refs_5_) | copy-start | bytes 23592964
  117.0 20.5 %copy-start.12 = (s32[1,640]{1,0:T(1,128)S(1)}, s32[1,640]{1,0:T(1,128)}, u32[]{:S(2)}) copy-start(s32[1,640]{1,0:T(1,128)} %param.8) | copy-start | bytes 7684
  125.2 1.3 copy-start.1
  133.6 34.6 %collective-permute-start.23 = (bf16[8,3,80,384]{3,2,1,0:T(8,128)(2,1)}, bf16[8,3,80,384]{3,2,1,0:T(8,128)(2,1)}, u32[]{:S(2)}, u32[]{:S(2)}) collective-permute-start(bf16[8,3,80,384]{3,2,1,0:T(8,128)(2,1)} %collective-permute-done.21.refs_2_), channel_id=1, source_target_pairs={{0,4},{4,0},{8,12},{12,8},{16,20},{20,16},{24,28},{28,24},{32,36},... | collective-permute-start | bytes 4423688 | tf_op jit(solution)/shard_map/ppermute | solution.py:53
  137.5 30.7 %collective-permute-start.25 = (bf16[8,3,80,384]{3,2,1,0:T(8,128)(2,1)}, bf16[8,3,80,384]{3,2,1,0:T(8,128)(2,1)}, u32[]{:S(2)}, u32[]{:S(2)}) collective-permute-start(bf16[8,3,80,384]{3,2,1,0:T(8,128)(2,1)} %collective-permute-done.22.refs_6_), channel_id=1, source_target_pairs={{0,4},{4,0},{8,12},{12,8},{16,20},{20,16},{24,28},{28,24},{32,36},... | collective-permute-start | bytes 4423688 | tf_op jit(solution)/shard_map/ppermute | solution.py:53
  148.2 1.5 copy-start.2
  153.6 13.6 %copy-start.13 = (s32[3]{0:T(128)S(1)}, s32[3]{0:T(128)}, u32[]{:S(2)}) copy-start(s32[3]{0:T(128)} %param.9) | copy-start | bytes 40
  155.2 40.6 %all-to-all-start = ((bf16[64,61,128]{2,1,0:T(8,128)(2,1)}), bf16[64,61,128]{2,1,0:T(8,128)(2,1)S(1)}, u32[]{:S(2)}, u32[]{:S(2)}) async-start(bf16[64,61,128]{2,1,0:T(8,128)(2,1)} %copy.53), calls=%async_computation | async-start | bytes 2097152 | tf_op jit(solution)/shard_map/all_to_all | solution.py:405
  196.5 13.3 %copy-start.11 = (pred[640,640]{0,1:T(8,128)(4,1)S(1)}, pred[640,640]{0,1:T(8,128)(4,1)}, u32[]{:S(2)}) copy-start(pred[640,640]{0,1:T(8,128)(4,1)} %get-tuple-element.53) | copy-start | bytes 1228804
  200.8 24.3 %all-to-all-start.1 = ((bf16[64,20,128]{2,1,0:T(8,128)(2,1)}), bf16[64,20,128]{2,1,0:T(8,128)(2,1)S(1)}, u32[]{:S(2)}, u32[]{:S(2)}) async-start(bf16[64,20,128]{2,1,0:T(8,128)(2,1)} %copy.55), calls=%async_computation.1 | async-start | bytes 786432 | tf_op jit(solution)/shard_map/all_to_all | solution.py:420
  209.8 2.5 %copy-start.10 = (bf16[1,640,384]{1,2,0:T(8,128)(2,1)S(1)}, bf16[1,640,384]{1,2,0:T(8,128)(2,1)}, u32[]{:S(2)}) copy-start(bf16[1,640,384]{1,2,0:T(8,128)(2,1)} %copy.46) | copy-start | bytes 1474564

commit v5 on v4

--- a/solution.py
+++ b/solution.py
@@ -170,7 +170,7 @@
 
 def early_kernel(place, *refs):
     tokens, weight = refs[:5], refs[5]
-    acc, spare, held, factor, token_sem, weight_sem = refs[6:]
+    acc, held, factor, token_sem, weight_sem = refs[6:]
     z = place[4]
     depth = held.shape[2]
 
@@ -207,12 +207,20 @@
         return carry
 
     lax.fori_loop(0, NZ, step, 0)
+
+
+def late_kernel(
+    place, far, weight, acc, flags, out, held, factor, token_sem, weight_sem
+):
+    z = place[4]
+    depth = held.shape[1]
     start = pl.multiple_of(jnp.where(z == 0, (NZ - 1) * depth, 0), depth)
-    spare[...] = factor[:, pl.ds(start, depth), :]
-
-
-def late_kernel(place, far, factor, acc, flags, out, held, token_sem):
-    z = place[4]
+
+    def load(j):
+        return pltpu.make_async_copy(
+            weight.at[j, pl.ds(start, depth), :], factor.at[j], weight_sem.at[j]
+        )
+
     last = (z == 0) | (z == NZ - 1)
     peers = out.shape[1]
     count = held.shape[0] // peers
@@ -232,9 +240,12 @@
     def _():
         copy = pltpu.make_async_copy(far, held, token_sem)
         copy.start()
+        for j in range(3):
+            load(j).start()
         copy.wait()
 
         def step(j, carry):
+            load(j).wait()
             term = jnp.dot(held[...], factor[j], preferred_element_type=jnp.float32)
             store(j, acc[j] + term)
             return carry
@@ -255,12 +266,9 @@
     _, total, cols = weight.shape
     return pl.pallas_call(
         early_kernel,
-        out_shape=[
-            jax.ShapeDtypeStruct((3, rows, cols), jnp.float32),
-            jax.ShapeDtypeStruct((3, depth, cols), jnp.bfloat16),
-        ],
+        out_shape=jax.ShapeDtypeStruct((3, rows, cols), jnp.float32),
         in_specs=[SMEM] + [HBM] * 6,
-        out_specs=[VMEM, VMEM],
+        out_specs=VMEM,
         scratch_shapes=[
             pltpu.VMEM((NZ, rows, depth), jnp.bfloat16),
             pltpu.VMEM((3, total, cols), jnp.bfloat16),
@@ -276,9 +284,9 @@
     )(place, *in_hbm(gathered[:5] + (weight,)))
 
 
-def project_late(place, far, factor, acc, marks):
+def project_late(place, far, weight, acc, marks):
     rows, depth = far.shape
-    cols = factor.shape[2]
+    cols = weight.shape[2]
     peers = NY * NX * NH * NC
     count = rows // peers
     flags = jnp.transpose(marks.astype(jnp.bfloat16).reshape(count, peers))
@@ -286,16 +294,21 @@
     return pl.pallas_call(
         late_kernel,
         out_shape=jax.ShapeDtypeStruct((3 * cols // HD * count + 1, peers, HD), jnp.bfloat16),
-        in_specs=[SMEM, HBM, VMEM, VMEM, VMEM],
+        in_specs=[SMEM, HBM, HBM, VMEM, VMEM],
         out_specs=VMEM,
-        scratch_shapes=[pltpu.VMEM((rows, depth), jnp.bfloat16), pltpu.SemaphoreType.DMA],
+        scratch_shapes=[
+            pltpu.VMEM((rows, depth), jnp.bfloat16),
+            pltpu.VMEM((3, depth, cols), jnp.bfloat16),
+            pltpu.SemaphoreType.DMA,
+            pltpu.SemaphoreType.DMA((3,)),
+        ],
         compiler_params=pltpu.CompilerParams(vmem_limit_bytes=16 * 1024 * 1024),
         cost_estimate=pl.CostEstimate(
             flops=6 * rows * depth * cols,
             bytes_accessed=2 * (rows * depth + 3 * depth * cols) + 18 * rows * cols,
             transcendentals=0,
         ),
-    )(place, *in_hbm((far,)), factor, acc, flags)
+    )(place, *in_hbm((far, weight)), acc, flags)
 
 
 def project_kernel(place, *refs):
@@ -437,10 +450,10 @@
     own_local = jnp.transpose(w_local, (1, 0, 2))
     gathered, strided, local = gather_all(tokens, own_strided, own_local)
     weight_strided = place_weights(place, *strided, 0)
-    acc, factor = project_early(place, gathered, weight_strided)
+    acc = project_early(place, gathered, weight_strided)
     acc, received = lax.optimization_barrier((acc, local[1]))
     weight_local = place_weights(place, local[0], received, 1)
-    packed = project_late(place, gathered[5], factor, acc, valid[0])
+    packed = project_late(place, gathered[5], weight_strided, acc, valid[0])
     out_strided = strided_attend(packed, w_strided.shape[2] // HD)
     qkv_local = project_local(place, gathered, weight_local)
     out_local = local_attend(qkv_local, valid[0], band_reach)

time: 227 us -> 226 us (level)
  local copies, waits for them, and re-layouts: 14.4 us -> 11.6 us
    unnamed x38 -> x34, local copies, waits for them, and re-layouts: 8.62 us -> 5.78 us
  transfers between devices with their start and end apart: 28 -> 28, of which waited for: 14 -> 14; matrix products, arithmetic and copies ran while one was open for 6% -> 6% of each run, Pallas kernels for 15% -> 16%
where the time goes in v5:
time: 226 us; the launch traced here: 225 us
  waiting for transfers between devices  95.3 us (42%)
  starting transfers between devices  67.9 us (30%)
  Pallas kernels  38.6 us (17%)
  local copies, waits for them, and re-layouts  11.6 us (5%)
  matrix products  6.44 us (3%)
  other arithmetic  4.19 us (2%)
    ppermute x21, waiting for transfers between devices, swap(): return lax.ppermute(value, 'seq', seq_pairs(MOVES[kind]))  63.7 us
    ppermute x21, starting transfers between devices, swap(): return lax.ppermute(value, 'seq', seq_pairs(MOVES[kind]))  35.3 us
    ppermute x5, waiting for transfers between devices, send_z(): return lax.ppermute(value, 'fsdp', pairs)  17.4 us
    pallas_call x1, Pallas kernels, project_local(): pl.pallas_call(project_kernel, out_shape=jax.ShapeDtypeStruct((3, rows, c...  14.1 us
    all_to_all x1, starting transfers between devices, strided_attend(): lax.all_to_all(packed, 'seq', split_axis=0, concat_axis=0, tiled=True)  12 us
    ppermute x5, starting transfers between devices, send_z(): return lax.ppermute(value, 'fsdp', pairs)  11.3 us
    all_to_all x1, starting transfers between devices, strided_attend(): lax.all_to_all(result, 'seq', split_axis=0, concat_axis=0, tiled=True)  9.28 us
    pallas_call x2, Pallas kernels, place_weights(): pl.pallas_call(functools.partial(place_kernel, (OWN_ORDERS[which], OTHER_...  8.93 us
  transfers between devices with their start and end apart: 28, of which 14 were waited for; matrix products, arithmetic and copies ran while one was open for 6% of the time, Pallas kernels for 16%

profile of v5, /device:TPU:1, one launch (start us, length us, event | category | flops | bytes accessed | tf_op | source)
XLA Modules:
  0.0 225.1 jit_solution(3555266273723622688)
XLA Ops:
  0.6 1.0 maximum_bitcast_fusion
  1.7 7.8 %collective-permute-start = (bf16[1,3,80,640]{3,2,1,0:T(8,128)(2,1)S(1)}, bf16[1,3,80,640]{3,2,1,0:T(8,128)(2,1)S(1)}, u32[]{:S(2)}, u32[]{:S(2)}) collective-permute-start(bf16[1,3,80,640]{3,2,1,0:T(8,128)(2,1)S(1)} %maximum_bitcast_fusion), channel_id=1, source_target_pairs={{0,8},{4,12},{8,0},{12,4},{16,24},{20,28},{24,16},{28,20},{32,40},... | collective-permute-start | bytes 921608 | tf_op jit(solution)/shard_map/ppermute | solution.py:53
  9.5 1.2 collective-permute-start.3
  10.7 6.2 %collective-permute-done = bf16[1,3,80,640]{3,2,1,0:T(8,128)(2,1)S(1)} collective-permute-done((bf16[1,3,80,640]{3,2,1,0:T(8,128)(2,1)S(1)}, bf16[1,3,80,640]{3,2,1,0:T(8,128)(2,1)S(1)}, u32[]{:S(2)}, u32[]{:S(2)}) %collective-permute-start) | collective-permute-done | bytes 307232 | tf_op jit(solution)/shard_map/ppermute | solution.py:53
  16.9 1.8 collective-permute-start.6
  18.8 6.1 %collective-permute-start.1 = (bf16[640,1280]{1,0:T(8,128)(2,1)}, bf16[640,1280]{1,0:T(8,128)(2,1)S(1)}, u32[]{:S(2)}, u32[]{:S(2)}) collective-permute-start(bf16[640,1280]{1,0:T(8,128)(2,1)} %refs_0_.1), channel_id=1, source_target_pairs={{0,1},{1,0},{2,3},{3,2},{4,5},{5,4},{6,7},{7,6},{8,9},{9,8},{10,11... | collective-permute-start | bytes 4915208 | tf_op jit(solution)/shard_map/ppermute | solution.py:106
  24.9 0.8 collective-permute-start.2
  25.7 2.6 %collective-permute-start.4 = (bf16[2,3,80,640]{3,2,1,0:T(8,128)(2,1)S(1)}, bf16[2,3,80,640]{3,2,1,0:T(8,128)(2,1)S(1)}, u32[]{:S(2)}, u32[]{:S(2)}) collective-permute-start(bf16[2,3,80,640]{3,2,1,0:T(8,128)(2,1)S(1)} %pad_maximum_fusion.6), channel_id=1, source_target_pairs={{0,48},{4,52},{8,56},{12,60},{16,32},{20,36},{24,40},{28,44},{32,1... | collective-permute-start | bytes 1843208 | tf_op jit(solution)/shard_map/ppermute | solution.py:53
  28.3 2.0 collective-permute-start.7
  30.4 9.9 %collective-permute-done.4 = bf16[2,3,80,640]{3,2,1,0:T(8,128)(2,1)S(1)} collective-permute-done((bf16[2,3,80,640]{3,2,1,0:T(8,128)(2,1)S(1)}, bf16[2,3,80,640]{3,2,1,0:T(8,128)(2,1)S(1)}, u32[]{:S(2)}, u32[]{:S(2)}) %collective-permute-start.4) | collective-permute-done | bytes 614432 | tf_op jit(solution)/shard_map/ppermute | solution.py:53
  40.3 0.3 collective-permute-start.5
  40.6 2.0 collective-permute-done.7
  42.8 0.1 collective-permute-start.8
  43.0 7.1 %collective-permute-done.5 = bf16[4,3,80,256]{3,2,1,0:T(8,128)(2,1)S(1)} collective-permute-done((bf16[4,3,80,256]{3,2,1,0:T(8,128)(2,1)S(1)}, bf16[4,3,80,256]{3,2,1,0:T(8,128)(2,1)S(1)}, u32[]{:S(2)}, u32[]{:S(2)}) %collective-permute-start.5) | collective-permute-done | bytes 491552 | tf_op jit(solution)/shard_map/ppermute | solution.py:53
  50.2 2.1 collective-permute-done.8
  52.4 7.0 %collective-permute-done.1.refs_1_ = bf16[640,1280]{1,0:T(8,128)(2,1)S(1)} collective-permute-done((bf16[640,1280]{1,0:T(8,128)(2,1)}, bf16[640,1280]{1,0:T(8,128)(2,1)S(1)}, u32[]{:S(2)}, u32[]{:S(2)}) %collective-permute-start.1) | collective-permute-done | bytes 1638432 | tf_op jit(solution)/shard_map/ppermute | solution.py:106
  59.4 2.0 collective-permute-start.11
  61.4 2.5 %collective-permute-start.14 = (bf16[4,3,80,384]{3,2,1,0:T(8,128)(2,1)S(1)}, bf16[4,3,80,384]{3,2,1,0:T(8,128)(2,1)S(1)}, u32[]{:S(2)}, u32[]{:S(2)}) collective-permute-start(bf16[4,3,80,384]{3,2,1,0:T(8,128)(2,1)S(1)} %slice.29), channel_id=1, source_target_pairs={{0,48},{4,52},{8,56},{12,60},{16,32},{20,36},{24,40},{28,44},{32,1... | collective-permute-start | bytes 2211848 | tf_op jit(solution)/shard_map/ppermute | solution.py:53
  63.8 0.8 collective-permute-start.13
  64.6 1.3 collective-permute-start.10
  65.9 1.9 collective-permute-start.9
  67.8 10.0 %collective-permute-done.14 = bf16[4,3,80,384]{3,2,1,0:T(8,128)(2,1)S(1)} collective-permute-done((bf16[4,3,80,384]{3,2,1,0:T(8,128)(2,1)S(1)}, bf16[4,3,80,384]{3,2,1,0:T(8,128)(2,1)S(1)}, u32[]{:S(2)}, u32[]{:S(2)}) %collective-permute-start.14) | collective-permute-done | bytes 737312 | tf_op jit(solution)/shard_map/ppermute | solution.py:53
  77.8 2.5 %collective-permute-start.12 = (bf16[8,3,80,256]{3,2,1,0:T(8,128)(2,1)S(1)}, bf16[8,3,80,256]{3,2,1,0:T(8,128)(2,1)S(1)}, u32[]{:S(2)}, u32[]{:S(2)}) collective-permute-start(bf16[8,3,80,256]{3,2,1,0:T(8,128)(2,1)S(1)} %pad_maximum_fusion.3.refs_4_), channel_id=1, source_target_pairs={{0,48},{4,52},{8,56},{12,60},{16,32},{20,36},{24,40},{28,44},{32,1... | collective-permute-start | bytes 2949128 | tf_op jit(solution)/shard_map/ppermute | solution.py:53
  80.3 17.0 %collective-permute-done.13 = bf16[4,3,80,384]{3,2,1,0:T(8,128)(2,1)S(1)} collective-permute-done((bf16[4,3,80,384]{3,2,1,0:T(8,128)(2,1)S(1)}, bf16[4,3,80,384]{3,2,1,0:T(8,128)(2,1)S(1)}, u32[]{:S(2)}, u32[]{:S(2)}) %collective-permute-start.13) | collective-permute-done | bytes 737312 | tf_op jit(solution)/shard_map/ppermute | solution.py:53
  97.3 3.4 %collective-permute-start.17 = (bf16[8,3,80,256]{3,2,1,0:T(8,128)(2,1)S(1)}, bf16[8,3,80,256]{3,2,1,0:T(8,128)(2,1)S(1)}, u32[]{:S(2)}, u32[]{:S(2)}) collective-permute-start(bf16[8,3,80,256]{3,2,1,0:T(8,128)(2,1)S(1)} %pad_maximum_fusion.2.refs_0_), channel_id=1, source_target_pairs={{0,4},{4,0},{8,12},{12,8},{16,20},{20,16},{24,28},{28,24},{32,36},... | collective-permute-start | bytes 2949128 | tf_op jit(solution)/shard_map/ppermute | solution.py:53
  100.7 0.2 pad_maximum_fusion.1.refs_4_
  100.9 1.5 pad_maximum_fusion.refs_0_
  102.4 0.1 collective-permute-start.21
  102.5 1.3 collective-permute-start.22
  103.8 2.1 collective-permute-start.18
  105.9 0.1 collective-permute-start.20
  106.0 0.8 copy-done.6
  106.9 1.3 collective-permute-start.15
  108.4 0.4 collective-permute-start.16
  108.8 0.9 collective-permute-done.20.refs_7_
  109.7 0.4 collective-permute-start.24
  110.0 3.9 %shard_map.68.refs_5_.weight = bf16[3,5120,256]{2,1,0:T(8,128)(2,1)S(1)} custom-call(s32[5]{0:T(128)S(1)} %stack.23.place, bf16[8,3,80,256]{3,2,1,0:T(8,128)(2,1)} %copy-done.2, bf16[8,3,80,256]{3,2,1,0:T(8,128)(2,1)} %copy-done.6, bf16[8,3,80,256]{3,2,1,0:T(8,128)(2,1)} %copy-done.4, bf16[8,3,80,256]{3,2,1,0:T(8,128)(2,1)} %collective-permute-done.18.refs_3_, ...), custom_call_target="tpu_custom_call" | custom-call | bytes 15728640 | tf_op jit(solution)/shard_map/pallas_call | solution.py:91
  114.0 3.1 %copy-done = bf16[3,5120,256]{2,1,0:T(8,128)(2,1)} copy-done((bf16[3,5120,256]{2,1,0:T(8,128)(2,1)}, bf16[3,5120,256]{2,1,0:T(8,128)(2,1)S(1)}, u32[]{:S(2)}) %copy-start) | copy-done | bytes 7864344
  117.0 8.0 %shard_map.69.acc = f32[3,640,256]{2,1,0:T(8,128)S(1)} custom-call(s32[5]{0:T(128)S(1)} %stack.23.place, bf16[640,1280]{1,0:T(8,128)(2,1)} %refs_0_.1, bf16[640,1280]{1,0:T(8,128)(2,1)} %copy-done.12, bf16[640,1280]{1,0:T(8,128)(2,1)} %copy-done.13, bf16[640,1280]{1,0:T(8,128)(2,1)} %collective-permute-done.9.refs_3_, bf16[640,1280]{1,0:T(8,128)(2,1)} %copy-done.14, ...), custom_call_target="tpu_custom_call" | custom-call | flops 5033164800 | bytes 16384000 | tf_op jit(solution)/shard_map/pallas_call | solution.py:267
  125.1 8.5 %collective-permute-done.21.refs_2_ = bf16[8,3,80,384]{3,2,1,0:T(8,128)(2,1)} collective-permute-done((bf16[8,3,80,384]{3,2,1,0:T(8,128)(2,1)}, bf16[8,3,80,384]{3,2,1,0:T(8,128)(2,1)}, u32[]{:S(2)}, u32[]{:S(2)}) %collective-permute-start.21) | collective-permute-done | bytes 1474592 | tf_op jit(solution)/shard_map/ppermute | solution.py:53
  133.6 3.9 %collective-permute-start.23 = (bf16[8,3,80,384]{3,2,1,0:T(8,128)(2,1)}, bf16[8,3,80,384]{3,2,1,0:T(8,128)(2,1)}, u32[]{:S(2)}, u32[]{:S(2)}) collective-permute-start(bf16[8,3,80,384]{3,2,1,0:T(8,128)(2,1)} %collective-permute-done.21.refs_2_), channel_id=1, source_target_pairs={{0,4},{4,0},{8,12},{12,8},{16,20},{20,16},{24,28},{28,24},{32,36},... | collective-permute-start | bytes 4423688 | tf_op jit(solution)/shard_map/ppermute | solution.py:53
  137.7 0.1 copy.52
  137.8 10.4 %collective-permute-done.15.refs_5_.far = bf16[640,1280]{1,0:T(8,128)(2,1)} collective-permute-done((bf16[640,1280]{1,0:T(8,128)(2,1)}, bf16[640,1280]{1,0:T(8,128)(2,1)}, u32[]{:S(2)}, u32[]{:S(2)}) %collective-permute-start.15) | collective-permute-done | bytes 1638432 | tf_op jit(solution)/shard_map/ppermute | solution.py:106
  148.2 4.2 %shard_map.72 = bf16[61,64,128]{2,1,0:T(8,128)(2,1)S(1)} custom-call(s32[5]{0:T(128)S(1)} %stack.23.place, bf16[640,1280]{1,0:T(8,128)(2,1)} %collective-permute-done.15.refs_5_.far, bf16[3,5120,256]{2,1,0:T(8,128)(2,1)} %copy-done, f32[3,640,256]{2,1,0:T(8,128)S(1)} %shard_map.69.acc, bf16[64,128]{1,0:T(8,128)(2,1)S(1)} %pad.4.flags), custom_call_target="tpu_custom_call" | custom-call | flops 1258291200 | bytes 6553600 | tf_op jit(solution)/shard_map/pallas_call | solution.py:294
  152.4 1.6 copy.53
  154.1 12.0 %all-to-all-start = ((bf16[64,61,128]{2,1,0:T(8,128)(2,1)}), bf16[64,61,128]{2,1,0:T(8,128)(2,1)S(1)}, u32[]{:S(2)}, u32[]{:S(2)}) async-start(bf16[64,61,128]{2,1,0:T(8,128)(2,1)} %copy.53), calls=%async_computation | async-start | bytes 2097152 | tf_op jit(solution)/shard_map/all_to_all | solution.py:418
  166.2 1.0 iota_compare_fusion.1
  167.2 5.0 %shard_map.70.refs_6_ = bf16[3,5120,384]{2,1,0:T(8,128)(2,1)S(1)} custom-call(s32[5]{0:T(128)S(1)} %stack.23.place, bf16[8,3,80,384]{3,2,1,0:T(8,128)(2,1)} %pad_maximum_fusion.refs_0_, bf16[8,3,80,384]{3,2,1,0:T(8,128)(2,1)} %collective-permute-done.16.refs_1_, bf16[8,3,80,384]{3,2,1,0:T(8,128)(2,1)} %collective-permute-done.21.refs_2_, ...), custom_call_target="tpu_custom_call" | custom-call | bytes 23592960 | tf_op jit(solution)/shard_map/pallas_call | solution.py:91
  172.3 14.1 %shard_map.71 = bf16[3,640,384]{2,1,0:T(8,128)(2,1)S(1)} custom-call(s32[5]{0:T(128)S(1)} %stack.23.place, bf16[640,1280]{1,0:T(8,128)(2,1)} %refs_0_.1, bf16[640,1280]{1,0:T(8,128)(2,1)} %copy-done.12, bf16[640,1280]{1,0:T(8,128)(2,1)} %copy-done.13, bf16[640,1280]{1,0:T(8,128)(2,1)} %collective-permute-done.9.refs_3_, bf16[640,1280]{1,0:T(8,128)(2,1)} %copy-done.14, ...), custom_call_target="tpu_custom_call" | custom-call | flops 7549747200 | bytes 19824640 | tf_op jit(solution)/shard_map/pallas_call | solution.py:344
  186.4 0.1 fusion.22
  186.5 0.3 copy.48
  186.8 0.3 copy.47
  187.1 1.0 copy.46
  188.1 6.3 %all-to-all-done = bf16[64,61,128]{2,1,0:T(8,128)(2,1)S(1)} async-done(((bf16[64,61,128]{2,1,0:T(8,128)(2,1)}), bf16[64,61,128]{2,1,0:T(8,128)(2,1)S(1)}, u32[]{:S(2)}, u32[]{:S(2)}) %all-to-all-start) | async-done | bytes 999456 | tf_op jit(solution)/shard_map/all_to_all | solution.py:418
  194.4 0.7 copy.65
  195.0 3.3 %shard_map.73 = bf16[20,64,128]{2,1,0:T(8,128)(2,1)S(1)} custom-call(bf16[61,64,128]{2,1,0:T(8,128)(2,1)S(1)} %bitcast.35), custom_call_target="tpu_custom_call" | custom-call | flops 83886080 | bytes 1310720 | tf_op jit(solution)/shard_map/pallas_call | solution.py:420
  198.4 1.0 copy.55
  199.3 9.3 %all-to-all-start.1 = ((bf16[64,20,128]{2,1,0:T(8,128)(2,1)}), bf16[64,20,128]{2,1,0:T(8,128)(2,1)S(1)}, u32[]{:S(2)}, u32[]{:S(2)}) async-start(bf16[64,20,128]{2,1,0:T(8,128)(2,1)} %copy.55), calls=%async_computation.1 | async-start | bytes 786432 | tf_op jit(solution)/shard_map/all_to_all | solution.py:433
  208.6 2.5 %fusion.23 = f32[3,640]{1,0:T(4,128)S(1)} fusion(s32[3,640]{1,0:T(4,128)S(1)} %broadcast_subtract_fusion, s32[640]{0:T(1024)S(1)} %add_select_fusion, pred[640,640]{0,1:T(8,128)(4,1)S(1)} %get-tuple-element.50, pred[640,640]{0,1:T(8,128)(4,1)S(1)} %copy-done.9, bf16[640,3,128]{0,2,1:T(8,128)(2,1)S(1)} %bitcast.41, bf16[640,3,128]{0,2,1:T(8,128)(2,1)S(1)} %bitcast.39), kind=kOutput, calls=%fused_computation.47 | convolution fusion | flops 323175040 | bytes 1820160 | tf_op jit(solution)/shard_map/sub | solution.py:379
  211.2 3.9 %fusion.10 = bf16[3,128,640]{2,1,0:T(8,128)(2,1)S(1)} fusion(bf16[640,3,128]{0,2,1:T(8,128)(2,1)S(1)} %bitcast.43, f32[3,640]{1,0:T(4,128)S(1)} %fusion.23, s32[3,640]{1,0:T(4,128)S(1)} %broadcast_subtract_fusion, s32[640]{0:T(1024)S(1)} %add_select_fusion, pred[640,640]{0,1:T(8,128)(4,1)S(1)} %get-tuple-element.50, ...), kind=kOutput, calls=%fused_computation.17 | convolution fusion | flops 639224320 | bytes 2803200 | tf_op jit(solution)/shard_map/hqk,khc->qhc/dot_general | solution.py:381
  215.1 1.0 copy.58
  216.1 7.8 %all-to-all-done.1 = bf16[64,20,128]{2,1,0:T(8,128)(2,1)S(1)} async-done(((bf16[64,20,128]{2,1,0:T(8,128)(2,1)}), bf16[64,20,128]{2,1,0:T(8,128)(2,1)S(1)}, u32[]{:S(2)}, u32[]{:S(2)}) %all-to-all-start.1) | async-done | bytes 327712 | tf_op jit(solution)/shard_map/all_to_all | solution.py:433
  224.0 0.3 copy.57
  224.3 0.8 copy.66
  (64 shorter events, 1.3 us)
Async XLA Ops:
  1.7 15.3 %collective-permute-start = (bf16[1,3,80,640]{3,2,1,0:T(8,128)(2,1)S(1)}, bf16[1,3,80,640]{3,2,1,0:T(8,128)(2,1)S(1)}, u32[]{:S(2)}, u32[]{:S(2)}) collective-permute-start(bf16[1,3,80,640]{3,2,1,0:T(8,128)(2,1)S(1)} %maximum_bitcast_fusion), channel_id=1, source_target_pairs={{0,8},{4,12},{8,0},{12,4},{16,24},{20,28},{24,16},{28,20},{32,40},... | collective-permute-start | bytes 921608 | tf_op jit(solution)/shard_map/ppermute | solution.py:53
  9.5 16.1 %collective-permute-start.3 = (bf16[1,3,80,640]{3,2,1,0:T(8,128)(2,1)S(1)}, bf16[1,3,80,640]{3,2,1,0:T(8,128)(2,1)S(1)}, u32[]{:S(2)}, u32[]{:S(2)}) collective-permute-start(bf16[1,3,80,640]{3,2,1,0:T(8,128)(2,1)S(1)} %maximum_bitcast_fusion), channel_id=1, source_target_pairs={{0,16},{4,20},{8,24},{12,28},{16,0},{20,4},{24,8},{28,12},{32,48},... | collective-permute-start | bytes 921608 | tf_op jit(solution)/shard_map/ppermute | solution.py:53
  16.9 11.3 %collective-permute-start.6 = (bf16[1,3,80,640]{3,2,1,0:T(8,128)(2,1)S(1)}, bf16[1,3,80,640]{3,2,1,0:T(8,128)(2,1)S(1)}, u32[]{:S(2)}, u32[]{:S(2)}) collective-permute-start(bf16[1,3,80,640]{3,2,1,0:T(8,128)(2,1)S(1)} %collective-permute-done), channel_id=1, source_target_pairs={{0,64},{4,68},{8,72},{12,76},{16,80},{20,84},{24,88},{28,92},{32,9... | collective-permute-start | bytes 921608 | tf_op jit(solution)/shard_map/ppermute | solution.py:53
  18.8 40.6 %collective-permute-start.1 = (bf16[640,1280]{1,0:T(8,128)(2,1)}, bf16[640,1280]{1,0:T(8,128)(2,1)S(1)}, u32[]{:S(2)}, u32[]{:S(2)}) collective-permute-start(bf16[640,1280]{1,0:T(8,128)(2,1)} %refs_0_.1), channel_id=1, source_target_pairs={{0,1},{1,0},{2,3},{3,2},{4,5},{5,4},{6,7},{7,6},{8,9},{9,8},{10,11... | collective-permute-start | bytes 4915208 | tf_op jit(solution)/shard_map/ppermute | solution.py:106
  24.9 34.5 %collective-permute-start.2 = (bf16[640,1280]{1,0:T(8,128)(2,1)}, bf16[640,1280]{1,0:T(8,128)(2,1)S(1)}, u32[]{:S(2)}, u32[]{:S(2)}) collective-permute-start(bf16[640,1280]{1,0:T(8,128)(2,1)} %refs_0_.1), channel_id=1, source_target_pairs={{1,2},{2,1},{5,6},{6,5},{9,10},{10,9},{13,14},{14,13},{17,18},{18,... | collective-permute-start | bytes 4915208 | tf_op jit(solution)/shard_map/ppermute | solution.py:106
  25.7 14.6 %collective-permute-start.4 = (bf16[2,3,80,640]{3,2,1,0:T(8,128)(2,1)S(1)}, bf16[2,3,80,640]{3,2,1,0:T(8,128)(2,1)S(1)}, u32[]{:S(2)}, u32[]{:S(2)}) collective-permute-start(bf16[2,3,80,640]{3,2,1,0:T(8,128)(2,1)S(1)} %pad_maximum_fusion.6), channel_id=1, source_target_pairs={{0,48},{4,52},{8,56},{12,60},{16,32},{20,36},{24,40},{28,44},{32,1... | collective-permute-start | bytes 1843208 | tf_op jit(solution)/shard_map/ppermute | solution.py:53
  28.3 14.3 %collective-permute-start.7 = (bf16[2,3,80,640]{3,2,1,0:T(8,128)(2,1)S(1)}, bf16[2,3,80,640]{3,2,1,0:T(8,128)(2,1)S(1)}, u32[]{:S(2)}, u32[]{:S(2)}) collective-permute-start(bf16[2,3,80,640]{3,2,1,0:T(8,128)(2,1)S(1)} %pad_maximum_fusion.7), channel_id=1, source_target_pairs={{0,192},{4,196},{8,200},{12,204},{16,208},{20,212},{24,216},{28,22... | collective-permute-start | bytes 1843208 | tf_op jit(solution)/shard_map/ppermute | solution.py:53
  40.3 9.8 %collective-permute-start.5 = (bf16[4,3,80,256]{3,2,1,0:T(8,128)(2,1)S(1)}, bf16[4,3,80,256]{3,2,1,0:T(8,128)(2,1)S(1)}, u32[]{:S(2)}, u32[]{:S(2)}) collective-permute-start(bf16[4,3,80,256]{3,2,1,0:T(8,128)(2,1)S(1)} %pad_maximum_fusion.8), channel_id=1, source_target_pairs={{0,64},{4,68},{8,72},{12,76},{16,80},{20,84},{24,88},{28,92},{32,9... | collective-permute-start | bytes 1474568 | tf_op jit(solution)/shard_map/ppermute | solution.py:53
  42.8 9.5 %collective-permute-start.8 = (bf16[4,3,80,256]{3,2,1,0:T(8,128)(2,1)S(1)}, bf16[4,3,80,256]{3,2,1,0:T(8,128)(2,1)S(1)}, u32[]{:S(2)}, u32[]{:S(2)}) collective-permute-start(bf16[4,3,80,256]{3,2,1,0:T(8,128)(2,1)S(1)} %slice.28), channel_id=1, source_target_pairs={{0,16},{4,20},{8,24},{12,28},{16,0},{20,4},{24,8},{28,12},{32,48},... | collective-permute-start | bytes 1474568 | tf_op jit(solution)/shard_map/ppermute | solution.py:53
  50.2 50.7 %copy-start.2 = (bf16[8,3,80,256]{3,2,1,0:T(8,128)(2,1)}, bf16[8,3,80,256]{3,2,1,0:T(8,128)(2,1)S(1)}, u32[]{:S(2)}) copy-start(bf16[8,3,80,256]{3,2,1,0:T(8,128)(2,1)S(1)} %pad_maximum_fusion.2.refs_0_) | copy-start | bytes 2949124
  52.4 50.0 %copy-start.3 = (bf16[8,3,80,256]{3,2,1,0:T(8,128)(2,1)}, bf16[8,3,80,256]{3,2,1,0:T(8,128)(2,1)S(1)}, u32[]{:S(2)}) copy-start(bf16[8,3,80,256]{3,2,1,0:T(8,128)(2,1)S(1)} %pad_maximum_fusion.3.refs_4_) | copy-start | bytes 2949124
  59.4 43.0 %copy-start.12 = (bf16[640,1280]{1,0:T(8,128)(2,1)}, bf16[640,1280]{1,0:T(8,128)(2,1)S(1)}, u32[]{:S(2)}) copy-start(bf16[640,1280]{1,0:T(8,128)(2,1)S(1)} %collective-permute-done.1.refs_1_) | copy-start | bytes 4915204
  59.4 48.8 %copy-start.13 = (bf16[640,1280]{1,0:T(8,128)(2,1)}, bf16[640,1280]{1,0:T(8,128)(2,1)S(1)}, u32[]{:S(2)}) copy-start(bf16[640,1280]{1,0:T(8,128)(2,1)S(1)} %collective-permute-done.2.refs_2_) | copy-start | bytes 4915204
  59.4 41.3 %collective-permute-start.11 = (bf16[8,3,80,256]{3,2,1,0:T(8,128)(2,1)S(1)}, bf16[8,3,80,256]{3,2,1,0:T(8,128)(2,1)S(1)}, u32[]{:S(2)}, u32[]{:S(2)}) collective-permute-start(bf16[8,3,80,256]{3,2,1,0:T(8,128)(2,1)S(1)} %pad_maximum_fusion.2.refs_0_), channel_id=1, source_target_pairs={{0,192},{4,196},{8,200},{12,204},{16,208},{20,212},{24,216},{28,22... | collective-permute-start | bytes 2949128 | tf_op jit(solution)/shard_map/ppermute | solution.py:53
  61.4 16.5 %collective-permute-start.14 = (bf16[4,3,80,384]{3,2,1,0:T(8,128)(2,1)S(1)}, bf16[4,3,80,384]{3,2,1,0:T(8,128)(2,1)S(1)}, u32[]{:S(2)}, u32[]{:S(2)}) collective-permute-start(bf16[4,3,80,384]{3,2,1,0:T(8,128)(2,1)S(1)} %slice.29), channel_id=1, source_target_pairs={{0,48},{4,52},{8,56},{12,60},{16,32},{20,36},{24,40},{28,44},{32,1... | collective-permute-start | bytes 2211848 | tf_op jit(solution)/shard_map/ppermute | solution.py:53
  63.8 33.4 %collective-permute-start.13 = (bf16[4,3,80,384]{3,2,1,0:T(8,128)(2,1)S(1)}, bf16[4,3,80,384]{3,2,1,0:T(8,128)(2,1)S(1)}, u32[]{:S(2)}, u32[]{:S(2)}) collective-permute-start(bf16[4,3,80,384]{3,2,1,0:T(8,128)(2,1)S(1)} %pad_maximum_fusion.4), channel_id=1, source_target_pairs={{0,192},{4,196},{8,200},{12,204},{16,208},{20,212},{24,216},{28,22... | collective-permute-start | bytes 2211848 | tf_op jit(solution)/shard_map/ppermute | solution.py:53
  64.6 37.8 %collective-permute-start.10 = (bf16[640,1280]{1,0:T(8,128)(2,1)S(1)}, bf16[640,1280]{1,0:T(8,128)(2,1)S(1)}, u32[]{:S(2)}, u32[]{:S(2)}) collective-permute-start(bf16[640,1280]{1,0:T(8,128)(2,1)S(1)} %collective-permute-done.2.refs_2_), channel_id=1, source_target_pairs={{2,3},{1,0},{6,7},{5,4},{10,11},{9,8},{14,15},{13,12},{18,19},{17,... | collective-permute-start | bytes 4915208 | tf_op jit(solution)/shard_map/ppermute | solution.py:106
  65.9 36.5 %collective-permute-start.9 = (bf16[640,1280]{1,0:T(8,128)(2,1)S(1)}, bf16[640,1280]{1,0:T(8,128)(2,1)}, u32[]{:S(2)}, u32[]{:S(2)}) collective-permute-start(bf16[640,1280]{1,0:T(8,128)(2,1)S(1)} %collective-permute-done.1.refs_1_), channel_id=1, source_target_pairs={{1,2},{2,1},{5,6},{6,5},{9,10},{10,9},{13,14},{14,13},{17,18},{18,... | collective-permute-start | bytes 4915208 | tf_op jit(solution)/shard_map/ppermute | solution.py:106
  77.8 24.6 %collective-permute-start.12 = (bf16[8,3,80,256]{3,2,1,0:T(8,128)(2,1)S(1)}, bf16[8,3,80,256]{3,2,1,0:T(8,128)(2,1)S(1)}, u32[]{:S(2)}, u32[]{:S(2)}) collective-permute-start(bf16[8,3,80,256]{3,2,1,0:T(8,128)(2,1)S(1)} %pad_maximum_fusion.3.refs_4_), channel_id=1, source_target_pairs={{0,48},{4,52},{8,56},{12,60},{16,32},{20,36},{24,40},{28,44},{32,1... | collective-permute-start | bytes 2949128 | tf_op jit(solution)/shard_map/ppermute | solution.py:53
  97.3 8.7 %collective-permute-start.17 = (bf16[8,3,80,256]{3,2,1,0:T(8,128)(2,1)S(1)}, bf16[8,3,80,256]{3,2,1,0:T(8,128)(2,1)S(1)}, u32[]{:S(2)}, u32[]{:S(2)}) collective-permute-start(bf16[8,3,80,256]{3,2,1,0:T(8,128)(2,1)S(1)} %pad_maximum_fusion.2.refs_0_), channel_id=1, source_target_pairs={{0,4},{4,0},{8,12},{12,8},{16,20},{20,16},{24,28},{28,24},{32,36},... | collective-permute-start | bytes 2949128 | tf_op jit(solution)/shard_map/ppermute | solution.py:53
  100.6 3.2 %copy-start.4 = (bf16[8,3,80,256]{3,2,1,0:T(8,128)(2,1)}, bf16[8,3,80,256]{3,2,1,0:T(8,128)(2,1)S(1)}, u32[]{:S(2)}) copy-start(bf16[8,3,80,256]{3,2,1,0:T(8,128)(2,1)S(1)} %collective-permute-done.11.refs_2_) | copy-start | bytes 2949124
  100.6 5.4 %collective-permute-start.19 = (bf16[8,3,80,256]{3,2,1,0:T(8,128)(2,1)S(1)}, bf16[8,3,80,256]{3,2,1,0:T(8,128)(2,1)S(1)}, u32[]{:S(2)}, u32[]{:S(2)}) collective-permute-start(bf16[8,3,80,256]{3,2,1,0:T(8,128)(2,1)S(1)} %pad_maximum_fusion.3.refs_4_), channel_id=1, source_target_pairs={{0,4},{4,0},{8,12},{12,8},{16,20},{20,16},{24,28},{28,24},{32,36},... | collective-permute-start | bytes 2949128 | tf_op jit(solution)/shard_map/ppermute | solution.py:53
  100.9 8.8 %copy-start.1 = (bf16[8,3,80,384]{3,2,1,0:T(8,128)(2,1)}, bf16[8,3,80,384]{3,2,1,0:T(8,128)(2,1)S(1)}, u32[]{:S(2)}) copy-start(bf16[8,3,80,384]{3,2,1,0:T(8,128)(2,1)S(1)} %pad_maximum_fusion.1.refs_4_) | copy-start | bytes 4423684
  102.4 7.6 %copy-start.5 = (bf16[8,3,80,256]{3,2,1,0:T(8,128)(2,1)}, bf16[8,3,80,256]{3,2,1,0:T(8,128)(2,1)S(1)}, u32[]{:S(2)}) copy-start(bf16[8,3,80,256]{3,2,1,0:T(8,128)(2,1)S(1)} %collective-permute-done.12.refs_6_) | copy-start | bytes 2949124
  102.4 5.8 %copy-start.14 = (bf16[640,1280]{1,0:T(8,128)(2,1)}, bf16[640,1280]{1,0:T(8,128)(2,1)S(1)}, u32[]{:S(2)}) copy-start(bf16[640,1280]{1,0:T(8,128)(2,1)S(1)} %collective-permute-done.10.refs_4_) | copy-start | bytes 4915204
  102.4 31.1 %collective-permute-start.21 = (bf16[8,3,80,384]{3,2,1,0:T(8,128)(2,1)}, bf16[8,3,80,384]{3,2,1,0:T(8,128)(2,1)}, u32[]{:S(2)}, u32[]{:S(2)}) collective-permute-start(bf16[8,3,80,384]{3,2,1,0:T(8,128)(2,1)} %pad_maximum_fusion.refs_0_), channel_id=1, source_target_pairs={{0,64},{4,68},{8,72},{12,76},{16,80},{20,84},{24,88},{28,92},{32,9... | collective-permute-start | bytes 4423688 | tf_op jit(solution)/shard_map/ppermute | solution.py:53
  102.5 31.1 %collective-permute-start.22 = (bf16[8,3,80,384]{3,2,1,0:T(8,128)(2,1)S(1)}, bf16[8,3,80,384]{3,2,1,0:T(8,128)(2,1)}, u32[]{:S(2)}, u32[]{:S(2)}) collective-permute-start(bf16[8,3,80,384]{3,2,1,0:T(8,128)(2,1)S(1)} %pad_maximum_fusion.1.refs_4_), channel_id=1, source_target_pairs={{0,16},{4,20},{8,24},{12,28},{16,0},{20,4},{24,8},{28,12},{32,48},... | collective-permute-start | bytes 4423688 | tf_op jit(solution)/shard_map/ppermute | solution.py:53
  103.8 4.5 %collective-permute-start.18 = (bf16[8,3,80,256]{3,2,1,0:T(8,128)(2,1)S(1)}, bf16[8,3,80,256]{3,2,1,0:T(8,128)(2,1)}, u32[]{:S(2)}, u32[]{:S(2)}) collective-permute-start(bf16[8,3,80,256]{3,2,1,0:T(8,128)(2,1)S(1)} %collective-permute-done.11.refs_2_), channel_id=1, source_target_pairs={{0,4},{4,0},{8,12},{12,8},{16,20},{20,16},{24,28},{28,24},{32,36},... | collective-permute-start | bytes 2949128 | tf_op jit(solution)/shard_map/ppermute | solution.py:53
  105.9 0.9 copy-start.6
  105.9 3.7 %collective-permute-start.20 = (bf16[8,3,80,256]{3,2,1,0:T(8,128)(2,1)S(1)}, bf16[8,3,80,256]{3,2,1,0:T(8,128)(2,1)}, u32[]{:S(2)}, u32[]{:S(2)}) collective-permute-start(bf16[8,3,80,256]{3,2,1,0:T(8,128)(2,1)S(1)} %collective-permute-done.12.refs_6_), channel_id=1, source_target_pairs={{0,4},{4,0},{8,12},{12,8},{16,20},{20,16},{24,28},{28,24},{32,36},... | collective-permute-start | bytes 2949128 | tf_op jit(solution)/shard_map/ppermute | solution.py:53
  106.9 1.3 copy-start.7
  106.9 41.3 %collective-permute-start.15 = (bf16[640,1280]{1,0:T(8,128)(2,1)}, bf16[640,1280]{1,0:T(8,128)(2,1)}, u32[]{:S(2)}, u32[]{:S(2)}) collective-permute-start(bf16[640,1280]{1,0:T(8,128)(2,1)} %collective-permute-done.9.refs_3_), channel_id=1, source_target_pairs={{2,3},{1,0},{6,7},{5,4},{10,11},{9,8},{14,15},{13,12},{18,19},{17,... | collective-permute-start | bytes 4915208 | tf_op jit(solution)/shard_map/ppermute | solution.py:106
  108.4 58.9 %collective-permute-start.16 = (bf16[8,3,80,384]{3,2,1,0:T(8,128)(2,1)}, bf16[8,3,80,384]{3,2,1,0:T(8,128)(2,1)}, u32[]{:S(2)}, u32[]{:S(2)}) collective-permute-start(bf16[8,3,80,384]{3,2,1,0:T(8,128)(2,1)} %pad_maximum_fusion.refs_0_), channel_id=1, source_target_pairs={{0,4},{4,0},{8,12},{12,8},{16,20},{20,16},{24,28},{28,24},{32,36},... | collective-permute-start | bytes 4423688 | tf_op jit(solution)/shard_map/ppermute | solution.py:53
  109.7 57.5 %collective-permute-start.24 = (bf16[8,3,80,384]{3,2,1,0:T(8,128)(2,1)S(1)}, bf16[8,3,80,384]{3,2,1,0:T(8,128)(2,1)}, u32[]{:S(2)}, u32[]{:S(2)}) collective-permute-start(bf16[8,3,80,384]{3,2,1,0:T(8,128)(2,1)S(1)} %pad_maximum_fusion.1.refs_4_), channel_id=1, source_target_pairs={{0,4},{4,0},{8,12},{12,8},{16,20},{20,16},{24,28},{28,24},{32,36},... | collective-permute-start | bytes 4423688 | tf_op jit(solution)/shard_map/ppermute | solution.py:53
  114.0 3.1 %copy-start = (bf16[3,5120,256]{2,1,0:T(8,128)(2,1)}, bf16[3,5120,256]{2,1,0:T(8,128)(2,1)S(1)}, u32[]{:S(2)}) copy-start(bf16[3,5120,256]{2,1,0:T(8,128)(2,1)S(1)} %shard_map.68.refs_5_.weight) | copy-start | bytes 23592964
  117.0 20.5 %copy-start.10 = (s32[1,640]{1,0:T(1,128)S(1)}, s32[1,640]{1,0:T(1,128)}, u32[]{:S(2)}) copy-start(s32[1,640]{1,0:T(1,128)} %param.8) | copy-start | bytes 7684
  133.6 33.6 %collective-permute-start.23 = (bf16[8,3,80,384]{3,2,1,0:T(8,128)(2,1)}, bf16[8,3,80,384]{3,2,1,0:T(8,128)(2,1)}, u32[]{:S(2)}, u32[]{:S(2)}) collective-permute-start(bf16[8,3,80,384]{3,2,1,0:T(8,128)(2,1)} %collective-permute-done.21.refs_2_), channel_id=1, source_target_pairs={{0,4},{4,0},{8,12},{12,8},{16,20},{20,16},{24,28},{28,24},{32,36},... | collective-permute-start | bytes 4423688 | tf_op jit(solution)/shard_map/ppermute | solution.py:53
  137.6 29.7 %collective-permute-start.25 = (bf16[8,3,80,384]{3,2,1,0:T(8,128)(2,1)}, bf16[8,3,80,384]{3,2,1,0:T(8,128)(2,1)}, u32[]{:S(2)}, u32[]{:S(2)}) collective-permute-start(bf16[8,3,80,384]{3,2,1,0:T(8,128)(2,1)} %collective-permute-done.22.refs_6_), channel_id=1, source_target_pairs={{0,4},{4,0},{8,12},{12,8},{16,20},{20,16},{24,28},{28,24},{32,36},... | collective-permute-start | bytes 4423688 | tf_op jit(solution)/shard_map/ppermute | solution.py:53
  154.1 12.1 %copy-start.11 = (s32[3]{0:T(128)S(1)}, s32[3]{0:T(128)}, u32[]{:S(2)}) copy-start(s32[3]{0:T(128)} %param.9) | copy-start | bytes 40
  154.1 40.3 %all-to-all-start = ((bf16[64,61,128]{2,1,0:T(8,128)(2,1)}), bf16[64,61,128]{2,1,0:T(8,128)(2,1)S(1)}, u32[]{:S(2)}, u32[]{:S(2)}) async-start(bf16[64,61,128]{2,1,0:T(8,128)(2,1)} %copy.53), calls=%async_computation | async-start | bytes 2097152 | tf_op jit(solution)/shard_map/all_to_all | solution.py:418
  195.0 13.6 %copy-start.9 = (pred[640,640]{0,1:T(8,128)(4,1)S(1)}, pred[640,640]{0,1:T(8,128)(4,1)}, u32[]{:S(2)}) copy-start(pred[640,640]{0,1:T(8,128)(4,1)} %get-tuple-element.49) | copy-start | bytes 1228804
  199.3 24.6 %all-to-all-start.1 = ((bf16[64,20,128]{2,1,0:T(8,128)(2,1)}), bf16[64,20,128]{2,1,0:T(8,128)(2,1)S(1)}, u32[]{:S(2)}, u32[]{:S(2)}) async-start(bf16[64,20,128]{2,1,0:T(8,128)(2,1)} %copy.55), calls=%async_computation.1 | async-start | bytes 786432 | tf_op jit(solution)/shard_map/all_to_all | solution.py:433
  208.6 2.5 %copy-start.8 = (bf16[1,640,384]{1,2,0:T(8,128)(2,1)S(1)}, bf16[1,640,384]{1,2,0:T(8,128)(2,1)}, u32[]{:S(2)}) copy-start(bf16[1,640,384]{1,2,0:T(8,128)(2,1)} %copy.46) | copy-start | bytes 1474564

commit v6 on v5

--- a/solution.py
+++ b/solution.py
@@ -97,7 +97,7 @@
         scratch_shapes=[pltpu.SemaphoreType.DMA],
         compiler_params=pltpu.CompilerParams(vmem_limit_bytes=16 * 1024 * 1024),
         cost_estimate=pl.CostEstimate(
-            flops=0, bytes_accessed=4 * 3 * total * cols, transcendentals=0
+            flops=0, bytes_accessed=total * cols // 16, transcendentals=0
         ),
     )(place, *[pltpu.with_memory_space_constraint(piece, pltpu.HBM) for piece in pieces])
 
@@ -277,8 +277,8 @@
         ],
         compiler_params=pltpu.CompilerParams(vmem_limit_bytes=24 * 1024 * 1024),
         cost_estimate=pl.CostEstimate(
-            flops=6 * rows * total * cols,
-            bytes_accessed=2 * (rows * total + 3 * total * cols) + 12 * rows * cols,
+            flops=rows * total * cols // 16,
+            bytes_accessed=(rows * total + 3 * total * cols) // 16,
             transcendentals=0,
         ),
     )(place, *in_hbm(gathered[:5] + (weight,)))

time: 226 us -> 226 us (level)
  waiting for transfers between devices: 95.3 us -> 101 us
  starting transfers between devices: 67.9 us -> 62.8 us
    ppermute x21, waiting for transfers between devices: 63.7 us -> 74.6 us  [swap(): return lax.ppermute(value, 'seq', seq_pairs(MOVES[kind]))]
    ppermute x21, starting transfers between devices: 35.3 us -> 30.1 us  [swap(): return lax.ppermute(value, 'seq', seq_pairs(MOVES[kind]))]
    ppermute x5, waiting for transfers between devices: 17.4 us -> 13.8 us  [send_z(): return lax.ppermute(value, 'fsdp', pairs)]
where the time goes in v6:
time: 226 us
  waiting for transfers between devices  101 us (45%)
  starting transfers between devices  62.8 us (28%)
  Pallas kernels  38.6 us (17%)
  local copies, waits for them, and re-layouts  11.6 us (5%)
  matrix products  6.45 us (3%)
  other arithmetic  4.19 us (2%)
    ppermute x21, waiting for transfers between devices, swap(): return lax.ppermute(value, 'seq', seq_pairs(MOVES[kind]))  74.6 us
    ppermute x21, starting transfers between devices, swap(): return lax.ppermute(value, 'seq', seq_pairs(MOVES[kind]))  30.1 us
    pallas_call x1, Pallas kernels, project_local(): pl.pallas_call(project_kernel, out_shape=jax.ShapeDtypeStruct((3, rows, c...  14.1 us
    ppermute x5, waiting for transfers between devices, send_z(): return lax.ppermute(value, 'fsdp', pairs)  13.8 us
    all_to_all x1, starting transfers between devices, strided_attend(): lax.all_to_all(packed, 'seq', split_axis=0, concat_axis=0, tiled=True)  12.1 us
    ppermute x5, starting transfers between devices, send_z(): return lax.ppermute(value, 'fsdp', pairs)  11.3 us
    all_to_all x1, starting transfers between devices, strided_attend(): lax.all_to_all(result, 'seq', split_axis=0, concat_axis=0, tiled=True)  9.28 us
    pallas_call x2, Pallas kernels, place_weights(): pl.pallas_call(functools.partial(place_kernel, (OWN_ORDERS[which], OTHER_...  8.93 us
  transfers between devices with their start and end apart: 28, of which 14 were waited for; matrix products, arithmetic and copies ran while one was open for 6% of the time, Pallas kernels for 16%

profile of v6, /device:TPU:1, one launch (start us, length us, event | category | flops | bytes accessed | tf_op | source)
XLA Modules:
  0.0 225.8 jit_solution(14356439045608640989)
XLA Ops:
  0.6 1.0 maximum_bitcast_fusion
  1.7 7.8 %collective-permute-start = (bf16[1,3,80,640]{3,2,1,0:T(8,128)(2,1)S(1)}, bf16[1,3,80,640]{3,2,1,0:T(8,128)(2,1)S(1)}, u32[]{:S(2)}, u32[]{:S(2)}) collective-permute-start(bf16[1,3,80,640]{3,2,1,0:T(8,128)(2,1)S(1)} %maximum_bitcast_fusion), channel_id=1, source_target_pairs={{0,8},{4,12},{8,0},{12,4},{16,24},{20,28},{24,16},{28,20},{32,40},... | collective-permute-start | bytes 921608 | tf_op jit(solution)/shard_map/ppermute | solution.py:53
  9.5 1.2 collective-permute-start.3
  10.7 6.2 %collective-permute-done = bf16[1,3,80,640]{3,2,1,0:T(8,128)(2,1)S(1)} collective-permute-done((bf16[1,3,80,640]{3,2,1,0:T(8,128)(2,1)S(1)}, bf16[1,3,80,640]{3,2,1,0:T(8,128)(2,1)S(1)}, u32[]{:S(2)}, u32[]{:S(2)}) %collective-permute-start) | collective-permute-done | bytes 307232 | tf_op jit(solution)/shard_map/ppermute | solution.py:53
  16.9 1.8 collective-permute-start.6
  18.8 6.1 %collective-permute-start.1 = (bf16[640,1280]{1,0:T(8,128)(2,1)}, bf16[640,1280]{1,0:T(8,128)(2,1)S(1)}, u32[]{:S(2)}, u32[]{:S(2)}) collective-permute-start(bf16[640,1280]{1,0:T(8,128)(2,1)} %refs_0_.1), channel_id=1, source_target_pairs={{0,1},{1,0},{2,3},{3,2},{4,5},{5,4},{6,7},{7,6},{8,9},{9,8},{10,11... | collective-permute-start | bytes 4915208 | tf_op jit(solution)/shard_map/ppermute | solution.py:106
  24.9 0.8 collective-permute-start.2
  25.7 2.6 %collective-permute-start.4 = (bf16[2,3,80,640]{3,2,1,0:T(8,128)(2,1)S(1)}, bf16[2,3,80,640]{3,2,1,0:T(8,128)(2,1)S(1)}, u32[]{:S(2)}, u32[]{:S(2)}) collective-permute-start(bf16[2,3,80,640]{3,2,1,0:T(8,128)(2,1)S(1)} %pad_maximum_fusion.6), channel_id=1, source_target_pairs={{0,48},{4,52},{8,56},{12,60},{16,32},{20,36},{24,40},{28,44},{32,1... | collective-permute-start | bytes 1843208 | tf_op jit(solution)/shard_map/ppermute | solution.py:53
  28.3 2.0 collective-permute-start.7
  30.4 9.9 %collective-permute-done.4 = bf16[2,3,80,640]{3,2,1,0:T(8,128)(2,1)S(1)} collective-permute-done((bf16[2,3,80,640]{3,2,1,0:T(8,128)(2,1)S(1)}, bf16[2,3,80,640]{3,2,1,0:T(8,128)(2,1)S(1)}, u32[]{:S(2)}, u32[]{:S(2)}) %collective-permute-start.4) | collective-permute-done | bytes 614432 | tf_op jit(solution)/shard_map/ppermute | solution.py:53
  40.3 0.3 collective-permute-start.5
  40.6 2.0 collective-permute-done.7
  43.0 7.1 %collective-permute-done.5 = bf16[4,3,80,256]{3,2,1,0:T(8,128)(2,1)S(1)} collective-permute-done((bf16[4,3,80,256]{3,2,1,0:T(8,128)(2,1)S(1)}, bf16[4,3,80,256]{3,2,1,0:T(8,128)(2,1)S(1)}, u32[]{:S(2)}, u32[]{:S(2)}) %collective-permute-start.5) | collective-permute-done | bytes 491552 | tf_op jit(solution)/shard_map/ppermute | solution.py:53
  50.2 2.1 collective-permute-done.8
  52.4 7.0 %collective-permute-done.1.refs_1_ = bf16[640,1280]{1,0:T(8,128)(2,1)S(1)} collective-permute-done((bf16[640,1280]{1,0:T(8,128)(2,1)}, bf16[640,1280]{1,0:T(8,128)(2,1)S(1)}, u32[]{:S(2)}, u32[]{:S(2)}) %collective-permute-start.1) | collective-permute-done | bytes 1638432 | tf_op jit(solution)/shard_map/ppermute | solution.py:106
  59.4 2.6 %collective-permute-start.14 = (bf16[4,3,80,384]{3,2,1,0:T(8,128)(2,1)S(1)}, bf16[4,3,80,384]{3,2,1,0:T(8,128)(2,1)S(1)}, u32[]{:S(2)}, u32[]{:S(2)}) collective-permute-start(bf16[4,3,80,384]{3,2,1,0:T(8,128)(2,1)S(1)} %slice.29), channel_id=1, source_target_pairs={{0,48},{4,52},{8,56},{12,60},{16,32},{20,36},{24,40},{28,44},{32,1... | collective-permute-start | bytes 2211848 | tf_op jit(solution)/shard_map/ppermute | solution.py:53
  61.9 1.3 collective-permute-start.10
  63.2 1.9 collective-permute-start.9
  65.1 1.9 collective-permute-start.11
  67.0 0.8 collective-permute-start.13
  67.8 8.4 %collective-permute-done.14 = bf16[4,3,80,384]{3,2,1,0:T(8,128)(2,1)S(1)} collective-permute-done((bf16[4,3,80,384]{3,2,1,0:T(8,128)(2,1)S(1)}, bf16[4,3,80,384]{3,2,1,0:T(8,128)(2,1)S(1)}, u32[]{:S(2)}, u32[]{:S(2)}) %collective-permute-start.14) | collective-permute-done | bytes 737312 | tf_op jit(solution)/shard_map/ppermute | solution.py:53
  76.2 2.5 %collective-permute-start.12 = (bf16[8,3,80,256]{3,2,1,0:T(8,128)(2,1)S(1)}, bf16[8,3,80,256]{3,2,1,0:T(8,128)(2,1)S(1)}, u32[]{:S(2)}, u32[]{:S(2)}) collective-permute-start(bf16[8,3,80,256]{3,2,1,0:T(8,128)(2,1)S(1)} %pad_maximum_fusion.3.refs_4_), channel_id=1, source_target_pairs={{0,48},{4,52},{8,56},{12,60},{16,32},{20,36},{24,40},{28,44},{32,1... | collective-permute-start | bytes 2949128 | tf_op jit(solution)/shard_map/ppermute | solution.py:53
  78.7 24.0 %collective-permute-done.13 = bf16[4,3,80,384]{3,2,1,0:T(8,128)(2,1)S(1)} collective-permute-done((bf16[4,3,80,384]{3,2,1,0:T(8,128)(2,1)S(1)}, bf16[4,3,80,384]{3,2,1,0:T(8,128)(2,1)S(1)}, u32[]{:S(2)}, u32[]{:S(2)}) %collective-permute-start.13) | collective-permute-done | bytes 737312 | tf_op jit(solution)/shard_map/ppermute | solution.py:53
  102.6 3.7 %collective-permute-start.17 = (bf16[8,3,80,256]{3,2,1,0:T(8,128)(2,1)S(1)}, bf16[8,3,80,256]{3,2,1,0:T(8,128)(2,1)S(1)}, u32[]{:S(2)}, u32[]{:S(2)}) collective-permute-start(bf16[8,3,80,256]{3,2,1,0:T(8,128)(2,1)S(1)} %pad_maximum_fusion.2.refs_0_), channel_id=1, source_target_pairs={{0,4},{4,0},{8,12},{12,8},{16,20},{20,16},{24,28},{28,24},{32,36},... | collective-permute-start | bytes 2949128 | tf_op jit(solution)/shard_map/ppermute | solution.py:53
  106.4 0.2 pad_maximum_fusion.1.refs_4_
  106.6 1.5 pad_maximum_fusion.refs_0_
  108.1 0.1 collective-permute-start.21
  108.3 1.3 collective-permute-start.15
  109.6 0.7 collective-permute-start.18
  110.3 0.1 collective-permute-start.20
  110.4 0.2 copy-done.9
  110.6 0.7 copy-done.10
  111.4 1.3 collective-permute-done.18.refs_3_
  112.6 0.4 collective-permute-start.16
  113.0 1.0 collective-permute-done.20.refs_7_
  114.0 0.4 collective-permute-start.24
  114.4 3.9 %shard_map.68.refs_5_.weight = bf16[3,5120,256]{2,1,0:T(8,128)(2,1)S(1)} custom-call(s32[5]{0:T(128)S(1)} %stack.23.place, bf16[8,3,80,256]{3,2,1,0:T(8,128)(2,1)} %copy-done.2, bf16[8,3,80,256]{3,2,1,0:T(8,128)(2,1)} %copy-done.9, bf16[8,3,80,256]{3,2,1,0:T(8,128)(2,1)} %copy-done.7, bf16[8,3,80,256]{3,2,1,0:T(8,128)(2,1)} %collective-permute-done.18.refs_3_, ...), custom_call_target="tpu_custom_call" | custom-call | bytes 81920 | tf_op jit(solution)/shard_map/pallas_call | solution.py:91
  118.3 3.1 %copy-done = bf16[3,5120,256]{2,1,0:T(8,128)(2,1)} copy-done((bf16[3,5120,256]{2,1,0:T(8,128)(2,1)}, bf16[3,5120,256]{2,1,0:T(8,128)(2,1)S(1)}, u32[]{:S(2)}) %copy-start) | copy-done | bytes 7864344
  121.4 8.0 %shard_map.69.acc = f32[3,640,256]{2,1,0:T(8,128)S(1)} custom-call(s32[5]{0:T(128)S(1)} %stack.23.place, bf16[640,1280]{1,0:T(8,128)(2,1)} %refs_0_.1, bf16[640,1280]{1,0:T(8,128)(2,1)} %copy-done.4, bf16[640,1280]{1,0:T(8,128)(2,1)} %copy-done.5, bf16[640,1280]{1,0:T(8,128)(2,1)} %collective-permute-done.9.refs_3_, bf16[640,1280]{1,0:T(8,128)(2,1)} %copy-done.6, ...), custom_call_target="tpu_custom_call" | custom-call | flops 52428800 | bytes 450560 | tf_op jit(solution)/shard_map/pallas_call | solution.py:267
  129.4 12.6 %collective-permute-done.21.refs_2_ = bf16[8,3,80,384]{3,2,1,0:T(8,128)(2,1)} collective-permute-done((bf16[8,3,80,384]{3,2,1,0:T(8,128)(2,1)}, bf16[8,3,80,384]{3,2,1,0:T(8,128)(2,1)}, u32[]{:S(2)}, u32[]{:S(2)}) %collective-permute-start.21) | collective-permute-done | bytes 1474592 | tf_op jit(solution)/shard_map/ppermute | solution.py:53
  142.0 1.2 collective-permute-start.23
  143.3 0.1 copy.52
  143.5 6.8 %collective-permute-done.15.refs_5_.far = bf16[640,1280]{1,0:T(8,128)(2,1)} collective-permute-done((bf16[640,1280]{1,0:T(8,128)(2,1)}, bf16[640,1280]{1,0:T(8,128)(2,1)}, u32[]{:S(2)}, u32[]{:S(2)}) %collective-permute-start.15) | collective-permute-done | bytes 1638432 | tf_op jit(solution)/shard_map/ppermute | solution.py:106
  150.3 4.2 %shard_map.72 = bf16[61,64,128]{2,1,0:T(8,128)(2,1)S(1)} custom-call(s32[5]{0:T(128)S(1)} %stack.23.place, bf16[640,1280]{1,0:T(8,128)(2,1)} %collective-permute-done.15.refs_5_.far, bf16[3,5120,256]{2,1,0:T(8,128)(2,1)} %copy-done, f32[3,640,256]{2,1,0:T(8,128)S(1)} %shard_map.69.acc, bf16[64,128]{1,0:T(8,128)(2,1)S(1)} %pad.4.flags), custom_call_target="tpu_custom_call" | custom-call | flops 1258291200 | bytes 6553600 | tf_op jit(solution)/shard_map/pallas_call | solution.py:294
  154.5 1.6 copy.53
  156.1 12.1 %all-to-all-start = ((bf16[64,61,128]{2,1,0:T(8,128)(2,1)}), bf16[64,61,128]{2,1,0:T(8,128)(2,1)S(1)}, u32[]{:S(2)}, u32[]{:S(2)}) async-start(bf16[64,61,128]{2,1,0:T(8,128)(2,1)} %copy.53), calls=%async_computation | async-start | bytes 2097152 | tf_op jit(solution)/shard_map/all_to_all | solution.py:418
  168.4 1.0 iota_compare_fusion.1
  169.4 5.0 %shard_map.70.refs_6_ = bf16[3,5120,384]{2,1,0:T(8,128)(2,1)S(1)} custom-call(s32[5]{0:T(128)S(1)} %stack.23.place, bf16[8,3,80,384]{3,2,1,0:T(8,128)(2,1)} %pad_maximum_fusion.refs_0_, bf16[8,3,80,384]{3,2,1,0:T(8,128)(2,1)} %collective-permute-done.16.refs_1_, bf16[8,3,80,384]{3,2,1,0:T(8,128)(2,1)} %collective-permute-done.21.refs_2_, ...), custom_call_target="tpu_custom_call" | custom-call | bytes 122880 | tf_op jit(solution)/shard_map/pallas_call | solution.py:91
  174.4 14.1 %shard_map.71 = bf16[3,640,384]{2,1,0:T(8,128)(2,1)S(1)} custom-call(s32[5]{0:T(128)S(1)} %stack.23.place, bf16[640,1280]{1,0:T(8,128)(2,1)} %refs_0_.1, bf16[640,1280]{1,0:T(8,128)(2,1)} %copy-done.4, bf16[640,1280]{1,0:T(8,128)(2,1)} %copy-done.5, bf16[640,1280]{1,0:T(8,128)(2,1)} %collective-permute-done.9.refs_3_, bf16[640,1280]{1,0:T(8,128)(2,1)} %copy-done.6, ...), custom_call_target="tpu_custom_call" | custom-call | flops 7549747200 | bytes 19824640 | tf_op jit(solution)/shard_map/pallas_call | solution.py:344
  188.5 0.1 fusion.22
  188.7 0.3 copy.48
  188.9 0.3 copy.47
  189.2 1.0 copy.46
  190.2 4.9 %all-to-all-done = bf16[64,61,128]{2,1,0:T(8,128)(2,1)S(1)} async-done(((bf16[64,61,128]{2,1,0:T(8,128)(2,1)}), bf16[64,61,128]{2,1,0:T(8,128)(2,1)S(1)}, u32[]{:S(2)}, u32[]{:S(2)}) %all-to-all-start) | async-done | bytes 999456 | tf_op jit(solution)/shard_map/all_to_all | solution.py:418
  195.0 0.7 copy.65
  195.7 3.3 %shard_map.73 = bf16[20,64,128]{2,1,0:T(8,128)(2,1)S(1)} custom-call(bf16[61,64,128]{2,1,0:T(8,128)(2,1)S(1)} %bitcast.35), custom_call_target="tpu_custom_call" | custom-call | flops 83886080 | bytes 1310720 | tf_op jit(solution)/shard_map/pallas_call | solution.py:420
  199.0 1.0 copy.55
  200.0 9.3 %all-to-all-start.1 = ((bf16[64,20,128]{2,1,0:T(8,128)(2,1)}), bf16[64,20,128]{2,1,0:T(8,128)(2,1)S(1)}, u32[]{:S(2)}, u32[]{:S(2)}) async-start(bf16[64,20,128]{2,1,0:T(8,128)(2,1)} %copy.55), calls=%async_computation.1 | async-start | bytes 786432 | tf_op jit(solution)/shard_map/all_to_all | solution.py:433
  209.3 2.5 %fusion.23 = f32[3,640]{1,0:T(4,128)S(1)} fusion(s32[3,640]{1,0:T(4,128)S(1)} %broadcast_subtract_fusion, s32[640]{0:T(1024)S(1)} %add_select_fusion, pred[640,640]{0,1:T(8,128)(4,1)S(1)} %get-tuple-element.50, pred[640,640]{0,1:T(8,128)(4,1)S(1)} %copy-done.12, bf16[640,3,128]{0,2,1:T(8,128)(2,1)S(1)} %bitcast.41, bf16[640,3,128]{0,2,1:T(8,128)(2,1)S(1)} %bitcast.39), kind=kOutput, calls=%fused_computation.47 | convolution fusion | flops 323175040 | bytes 1820160 | tf_op jit(solution)/shard_map/sub | solution.py:379
  211.8 3.9 %fusion.10 = bf16[3,128,640]{2,1,0:T(8,128)(2,1)S(1)} fusion(bf16[640,3,128]{0,2,1:T(8,128)(2,1)S(1)} %bitcast.43, f32[3,640]{1,0:T(4,128)S(1)} %fusion.23, s32[3,640]{1,0:T(4,128)S(1)} %broadcast_subtract_fusion, s32[640]{0:T(1024)S(1)} %add_select_fusion, pred[640,640]{0,1:T(8,128)(4,1)S(1)} %get-tuple-element.50, ...), kind=kOutput, calls=%fused_computation.17 | convolution fusion | flops 639224320 | bytes 2803200 | tf_op jit(solution)/shard_map/hqk,khc->qhc/dot_general | solution.py:381
  215.8 1.0 copy.58
  216.8 7.8 %all-to-all-done.1 = bf16[64,20,128]{2,1,0:T(8,128)(2,1)S(1)} async-done(((bf16[64,20,128]{2,1,0:T(8,128)(2,1)}), bf16[64,20,128]{2,1,0:T(8,128)(2,1)S(1)}, u32[]{:S(2)}, u32[]{:S(2)}) %all-to-all-start.1) | async-done | bytes 327712 | tf_op jit(solution)/shard_map/all_to_all | solution.py:433
  224.7 0.3 copy.57
  225.0 0.8 copy.66
  (64 shorter events, 1.4 us)
Async XLA Ops:
  1.7 15.3 %collective-permute-start = (bf16[1,3,80,640]{3,2,1,0:T(8,128)(2,1)S(1)}, bf16[1,3,80,640]{3,2,1,0:T(8,128)(2,1)S(1)}, u32[]{:S(2)}, u32[]{:S(2)}) collective-permute-start(bf16[1,3,80,640]{3,2,1,0:T(8,128)(2,1)S(1)} %maximum_bitcast_fusion), channel_id=1, source_target_pairs={{0,8},{4,12},{8,0},{12,4},{16,24},{20,28},{24,16},{28,20},{32,40},... | collective-permute-start | bytes 921608 | tf_op jit(solution)/shard_map/ppermute | solution.py:53
  9.5 16.1 %collective-permute-start.3 = (bf16[1,3,80,640]{3,2,1,0:T(8,128)(2,1)S(1)}, bf16[1,3,80,640]{3,2,1,0:T(8,128)(2,1)S(1)}, u32[]{:S(2)}, u32[]{:S(2)}) collective-permute-start(bf16[1,3,80,640]{3,2,1,0:T(8,128)(2,1)S(1)} %maximum_bitcast_fusion), channel_id=1, source_target_pairs={{0,16},{4,20},{8,24},{12,28},{16,0},{20,4},{24,8},{28,12},{32,48},... | collective-permute-start | bytes 921608 | tf_op jit(solution)/shard_map/ppermute | solution.py:53
  16.9 11.3 %collective-permute-start.6 = (bf16[1,3,80,640]{3,2,1,0:T(8,128)(2,1)S(1)}, bf16[1,3,80,640]{3,2,1,0:T(8,128)(2,1)S(1)}, u32[]{:S(2)}, u32[]{:S(2)}) collective-permute-start(bf16[1,3,80,640]{3,2,1,0:T(8,128)(2,1)S(1)} %collective-permute-done), channel_id=1, source_target_pairs={{0,64},{4,68},{8,72},{12,76},{16,80},{20,84},{24,88},{28,92},{32,9... | collective-permute-start | bytes 921608 | tf_op jit(solution)/shard_map/ppermute | solution.py:53
  18.8 40.6 %collective-permute-start.1 = (bf16[640,1280]{1,0:T(8,128)(2,1)}, bf16[640,1280]{1,0:T(8,128)(2,1)S(1)}, u32[]{:S(2)}, u32[]{:S(2)}) collective-permute-start(bf16[640,1280]{1,0:T(8,128)(2,1)} %refs_0_.1), channel_id=1, source_target_pairs={{0,1},{1,0},{2,3},{3,2},{4,5},{5,4},{6,7},{7,6},{8,9},{9,8},{10,11... | collective-permute-start | bytes 4915208 | tf_op jit(solution)/shard_map/ppermute | solution.py:106
  24.9 34.5 %collective-permute-start.2 = (bf16[640,1280]{1,0:T(8,128)(2,1)}, bf16[640,1280]{1,0:T(8,128)(2,1)S(1)}, u32[]{:S(2)}, u32[]{:S(2)}) collective-permute-start(bf16[640,1280]{1,0:T(8,128)(2,1)} %refs_0_.1), channel_id=1, source_target_pairs={{1,2},{2,1},{5,6},{6,5},{9,10},{10,9},{13,14},{14,13},{17,18},{18,... | collective-permute-start | bytes 4915208 | tf_op jit(solution)/shard_map/ppermute | solution.py:106
  25.7 14.6 %collective-permute-start.4 = (bf16[2,3,80,640]{3,2,1,0:T(8,128)(2,1)S(1)}, bf16[2,3,80,640]{3,2,1,0:T(8,128)(2,1)S(1)}, u32[]{:S(2)}, u32[]{:S(2)}) collective-permute-start(bf16[2,3,80,640]{3,2,1,0:T(8,128)(2,1)S(1)} %pad_maximum_fusion.6), channel_id=1, source_target_pairs={{0,48},{4,52},{8,56},{12,60},{16,32},{20,36},{24,40},{28,44},{32,1... | collective-permute-start | bytes 1843208 | tf_op jit(solution)/shard_map/ppermute | solution.py:53
  28.3 14.3 %collective-permute-start.7 = (bf16[2,3,80,640]{3,2,1,0:T(8,128)(2,1)S(1)}, bf16[2,3,80,640]{3,2,1,0:T(8,128)(2,1)S(1)}, u32[]{:S(2)}, u32[]{:S(2)}) collective-permute-start(bf16[2,3,80,640]{3,2,1,0:T(8,128)(2,1)S(1)} %pad_maximum_fusion.7), channel_id=1, source_target_pairs={{0,192},{4,196},{8,200},{12,204},{16,208},{20,212},{24,216},{28,22... | collective-permute-start | bytes 1843208 | tf_op jit(solution)/shard_map/ppermute | solution.py:53
  40.3 9.8 %collective-permute-start.5 = (bf16[4,3,80,256]{3,2,1,0:T(8,128)(2,1)S(1)}, bf16[4,3,80,256]{3,2,1,0:T(8,128)(2,1)S(1)}, u32[]{:S(2)}, u32[]{:S(2)}) collective-permute-start(bf16[4,3,80,256]{3,2,1,0:T(8,128)(2,1)S(1)} %pad_maximum_fusion.8), channel_id=1, source_target_pairs={{0,64},{4,68},{8,72},{12,76},{16,80},{20,84},{24,88},{28,92},{32,9... | collective-permute-start | bytes 1474568 | tf_op jit(solution)/shard_map/ppermute | solution.py:53
  42.8 9.5 %collective-permute-start.8 = (bf16[4,3,80,256]{3,2,1,0:T(8,128)(2,1)S(1)}, bf16[4,3,80,256]{3,2,1,0:T(8,128)(2,1)S(1)}, u32[]{:S(2)}, u32[]{:S(2)}) collective-permute-start(bf16[4,3,80,256]{3,2,1,0:T(8,128)(2,1)S(1)} %slice.28), channel_id=1, source_target_pairs={{0,16},{4,20},{8,24},{12,28},{16,0},{20,4},{24,8},{28,12},{32,48},... | collective-permute-start | bytes 1474568 | tf_op jit(solution)/shard_map/ppermute | solution.py:53
  50.2 56.4 %copy-start.2 = (bf16[8,3,80,256]{3,2,1,0:T(8,128)(2,1)}, bf16[8,3,80,256]{3,2,1,0:T(8,128)(2,1)S(1)}, u32[]{:S(2)}) copy-start(bf16[8,3,80,256]{3,2,1,0:T(8,128)(2,1)S(1)} %pad_maximum_fusion.2.refs_0_) | copy-start | bytes 2949124
  52.4 55.7 %copy-start.3 = (bf16[8,3,80,256]{3,2,1,0:T(8,128)(2,1)}, bf16[8,3,80,256]{3,2,1,0:T(8,128)(2,1)S(1)}, u32[]{:S(2)}) copy-start(bf16[8,3,80,256]{3,2,1,0:T(8,128)(2,1)S(1)} %pad_maximum_fusion.3.refs_4_) | copy-start | bytes 2949124
  59.4 48.7 %copy-start.4 = (bf16[640,1280]{1,0:T(8,128)(2,1)}, bf16[640,1280]{1,0:T(8,128)(2,1)S(1)}, u32[]{:S(2)}) copy-start(bf16[640,1280]{1,0:T(8,128)(2,1)S(1)} %collective-permute-done.1.refs_1_) | copy-start | bytes 4915204
  59.4 48.7 %copy-start.5 = (bf16[640,1280]{1,0:T(8,128)(2,1)}, bf16[640,1280]{1,0:T(8,128)(2,1)S(1)}, u32[]{:S(2)}) copy-start(bf16[640,1280]{1,0:T(8,128)(2,1)S(1)} %collective-permute-done.2.refs_2_) | copy-start | bytes 4915204
  59.4 16.8 %collective-permute-start.14 = (bf16[4,3,80,384]{3,2,1,0:T(8,128)(2,1)S(1)}, bf16[4,3,80,384]{3,2,1,0:T(8,128)(2,1)S(1)}, u32[]{:S(2)}, u32[]{:S(2)}) collective-permute-start(bf16[4,3,80,384]{3,2,1,0:T(8,128)(2,1)S(1)} %slice.29), channel_id=1, source_target_pairs={{0,48},{4,52},{8,56},{12,60},{16,32},{20,36},{24,40},{28,44},{32,1... | collective-permute-start | bytes 2211848 | tf_op jit(solution)/shard_map/ppermute | solution.py:53
  61.9 46.1 %collective-permute-start.10 = (bf16[640,1280]{1,0:T(8,128)(2,1)S(1)}, bf16[640,1280]{1,0:T(8,128)(2,1)S(1)}, u32[]{:S(2)}, u32[]{:S(2)}) collective-permute-start(bf16[640,1280]{1,0:T(8,128)(2,1)S(1)} %collective-permute-done.2.refs_2_), channel_id=1, source_target_pairs={{2,3},{1,0},{6,7},{5,4},{10,11},{9,8},{14,15},{13,12},{18,19},{17,... | collective-permute-start | bytes 4915208 | tf_op jit(solution)/shard_map/ppermute | solution.py:106
  63.2 44.9 %collective-permute-start.9 = (bf16[640,1280]{1,0:T(8,128)(2,1)S(1)}, bf16[640,1280]{1,0:T(8,128)(2,1)}, u32[]{:S(2)}, u32[]{:S(2)}) collective-permute-start(bf16[640,1280]{1,0:T(8,128)(2,1)S(1)} %collective-permute-done.1.refs_1_), channel_id=1, source_target_pairs={{1,2},{2,1},{5,6},{6,5},{9,10},{10,9},{13,14},{14,13},{17,18},{18,... | collective-permute-start | bytes 4915208 | tf_op jit(solution)/shard_map/ppermute | solution.py:106
  65.1 41.2 %collective-permute-start.11 = (bf16[8,3,80,256]{3,2,1,0:T(8,128)(2,1)S(1)}, bf16[8,3,80,256]{3,2,1,0:T(8,128)(2,1)S(1)}, u32[]{:S(2)}, u32[]{:S(2)}) collective-permute-start(bf16[8,3,80,256]{3,2,1,0:T(8,128)(2,1)S(1)} %pad_maximum_fusion.2.refs_0_), channel_id=1, source_target_pairs={{0,192},{4,196},{8,200},{12,204},{16,208},{20,212},{24,216},{28,22... | collective-permute-start | bytes 2949128 | tf_op jit(solution)/shard_map/ppermute | solution.py:53
  67.0 35.6 %collective-permute-start.13 = (bf16[4,3,80,384]{3,2,1,0:T(8,128)(2,1)S(1)}, bf16[4,3,80,384]{3,2,1,0:T(8,128)(2,1)S(1)}, u32[]{:S(2)}, u32[]{:S(2)}) collective-permute-start(bf16[4,3,80,384]{3,2,1,0:T(8,128)(2,1)S(1)} %pad_maximum_fusion.4), channel_id=1, source_target_pairs={{0,192},{4,196},{8,200},{12,204},{16,208},{20,212},{24,216},{28,22... | collective-permute-start | bytes 2211848 | tf_op jit(solution)/shard_map/ppermute | solution.py:53
  76.2 31.9 %collective-permute-start.12 = (bf16[8,3,80,256]{3,2,1,0:T(8,128)(2,1)S(1)}, bf16[8,3,80,256]{3,2,1,0:T(8,128)(2,1)S(1)}, u32[]{:S(2)}, u32[]{:S(2)}) collective-permute-start(bf16[8,3,80,256]{3,2,1,0:T(8,128)(2,1)S(1)} %pad_maximum_fusion.3.refs_4_), channel_id=1, source_target_pairs={{0,48},{4,52},{8,56},{12,60},{16,32},{20,36},{24,40},{28,44},{32,1... | collective-permute-start | bytes 2949128 | tf_op jit(solution)/shard_map/ppermute | solution.py:53
  102.6 7.0 %collective-permute-start.17 = (bf16[8,3,80,256]{3,2,1,0:T(8,128)(2,1)S(1)}, bf16[8,3,80,256]{3,2,1,0:T(8,128)(2,1)S(1)}, u32[]{:S(2)}, u32[]{:S(2)}) collective-permute-start(bf16[8,3,80,256]{3,2,1,0:T(8,128)(2,1)S(1)} %pad_maximum_fusion.2.refs_0_), channel_id=1, source_target_pairs={{0,4},{4,0},{8,12},{12,8},{16,20},{20,16},{24,28},{28,24},{32,36},... | collective-permute-start | bytes 2949128 | tf_op jit(solution)/shard_map/ppermute | solution.py:53
  106.3 8.1 %copy-start.7 = (bf16[8,3,80,256]{3,2,1,0:T(8,128)(2,1)}, bf16[8,3,80,256]{3,2,1,0:T(8,128)(2,1)S(1)}, u32[]{:S(2)}) copy-start(bf16[8,3,80,256]{3,2,1,0:T(8,128)(2,1)S(1)} %collective-permute-done.11.refs_2_) | copy-start | bytes 2949124
  106.3 4.0 %collective-permute-start.19 = (bf16[8,3,80,256]{3,2,1,0:T(8,128)(2,1)S(1)}, bf16[8,3,80,256]{3,2,1,0:T(8,128)(2,1)S(1)}, u32[]{:S(2)}, u32[]{:S(2)}) collective-permute-start(bf16[8,3,80,256]{3,2,1,0:T(8,128)(2,1)S(1)} %pad_maximum_fusion.3.refs_4_), channel_id=1, source_target_pairs={{0,4},{4,0},{8,12},{12,8},{16,20},{20,16},{24,28},{28,24},{32,36},... | collective-permute-start | bytes 2949128 | tf_op jit(solution)/shard_map/ppermute | solution.py:53
  106.6 7.4 %copy-start.1 = (bf16[8,3,80,384]{3,2,1,0:T(8,128)(2,1)}, bf16[8,3,80,384]{3,2,1,0:T(8,128)(2,1)S(1)}, u32[]{:S(2)}) copy-start(bf16[8,3,80,384]{3,2,1,0:T(8,128)(2,1)S(1)} %pad_maximum_fusion.1.refs_4_) | copy-start | bytes 4423684
  108.1 6.3 %copy-start.8 = (bf16[8,3,80,256]{3,2,1,0:T(8,128)(2,1)}, bf16[8,3,80,256]{3,2,1,0:T(8,128)(2,1)S(1)}, u32[]{:S(2)}) copy-start(bf16[8,3,80,256]{3,2,1,0:T(8,128)(2,1)S(1)} %collective-permute-done.12.refs_6_) | copy-start | bytes 2949124
  108.1 2.2 copy-start.6
  108.1 33.9 %collective-permute-start.21 = (bf16[8,3,80,384]{3,2,1,0:T(8,128)(2,1)}, bf16[8,3,80,384]{3,2,1,0:T(8,128)(2,1)}, u32[]{:S(2)}, u32[]{:S(2)}) collective-permute-start(bf16[8,3,80,384]{3,2,1,0:T(8,128)(2,1)} %pad_maximum_fusion.refs_0_), channel_id=1, source_target_pairs={{0,64},{4,68},{8,72},{12,76},{16,80},{20,84},{24,88},{28,92},{32,9... | collective-permute-start | bytes 4423688 | tf_op jit(solution)/shard_map/ppermute | solution.py:53
  108.2 33.8 %collective-permute-start.22 = (bf16[8,3,80,384]{3,2,1,0:T(8,128)(2,1)S(1)}, bf16[8,3,80,384]{3,2,1,0:T(8,128)(2,1)}, u32[]{:S(2)}, u32[]{:S(2)}) collective-permute-start(bf16[8,3,80,384]{3,2,1,0:T(8,128)(2,1)S(1)} %pad_maximum_fusion.1.refs_4_), channel_id=1, source_target_pairs={{0,16},{4,20},{8,24},{12,28},{16,0},{20,4},{24,8},{28,12},{32,48},... | collective-permute-start | bytes 4423688 | tf_op jit(solution)/shard_map/ppermute | solution.py:53
  108.3 42.0 %collective-permute-start.15 = (bf16[640,1280]{1,0:T(8,128)(2,1)}, bf16[640,1280]{1,0:T(8,128)(2,1)}, u32[]{:S(2)}, u32[]{:S(2)}) collective-permute-start(bf16[640,1280]{1,0:T(8,128)(2,1)} %collective-permute-done.9.refs_3_), channel_id=1, source_target_pairs={{2,3},{1,0},{6,7},{5,4},{10,11},{9,8},{14,15},{13,12},{18,19},{17,... | collective-permute-start | bytes 4915208 | tf_op jit(solution)/shard_map/ppermute | solution.py:106
  109.6 0.9 copy-start.9
  109.6 3.0 %collective-permute-start.18 = (bf16[8,3,80,256]{3,2,1,0:T(8,128)(2,1)S(1)}, bf16[8,3,80,256]{3,2,1,0:T(8,128)(2,1)}, u32[]{:S(2)}, u32[]{:S(2)}) collective-permute-start(bf16[8,3,80,256]{3,2,1,0:T(8,128)(2,1)S(1)} %collective-permute-done.11.refs_2_), channel_id=1, source_target_pairs={{0,4},{4,0},{8,12},{12,8},{16,20},{20,16},{24,28},{28,24},{32,36},... | collective-permute-start | bytes 2949128 | tf_op jit(solution)/shard_map/ppermute | solution.py:53
  110.3 1.0 copy-start.10
  110.3 3.7 %collective-permute-start.20 = (bf16[8,3,80,256]{3,2,1,0:T(8,128)(2,1)S(1)}, bf16[8,3,80,256]{3,2,1,0:T(8,128)(2,1)}, u32[]{:S(2)}, u32[]{:S(2)}) collective-permute-start(bf16[8,3,80,256]{3,2,1,0:T(8,128)(2,1)S(1)} %collective-permute-done.12.refs_6_), channel_id=1, source_target_pairs={{0,4},{4,0},{8,12},{12,8},{16,20},{20,16},{24,28},{28,24},{32,36},... | collective-permute-start | bytes 2949128 | tf_op jit(solution)/shard_map/ppermute | solution.py:53
  112.6 56.7 %collective-permute-start.16 = (bf16[8,3,80,384]{3,2,1,0:T(8,128)(2,1)}, bf16[8,3,80,384]{3,2,1,0:T(8,128)(2,1)}, u32[]{:S(2)}, u32[]{:S(2)}) collective-permute-start(bf16[8,3,80,384]{3,2,1,0:T(8,128)(2,1)} %pad_maximum_fusion.refs_0_), channel_id=1, source_target_pairs={{0,4},{4,0},{8,12},{12,8},{16,20},{20,16},{24,28},{28,24},{32,36},... | collective-permute-start | bytes 4423688 | tf_op jit(solution)/shard_map/ppermute | solution.py:53
  114.0 55.3 %collective-permute-start.24 = (bf16[8,3,80,384]{3,2,1,0:T(8,128)(2,1)S(1)}, bf16[8,3,80,384]{3,2,1,0:T(8,128)(2,1)}, u32[]{:S(2)}, u32[]{:S(2)}) collective-permute-start(bf16[8,3,80,384]{3,2,1,0:T(8,128)(2,1)S(1)} %pad_maximum_fusion.1.refs_4_), channel_id=1, source_target_pairs={{0,4},{4,0},{8,12},{12,8},{16,20},{20,16},{24,28},{28,24},{32,36},... | collective-permute-start | bytes 4423688 | tf_op jit(solution)/shard_map/ppermute | solution.py:53
  118.3 3.1 %copy-start = (bf16[3,5120,256]{2,1,0:T(8,128)(2,1)}, bf16[3,5120,256]{2,1,0:T(8,128)(2,1)S(1)}, u32[]{:S(2)}) copy-start(bf16[3,5120,256]{2,1,0:T(8,128)(2,1)S(1)} %shard_map.68.refs_5_.weight) | copy-start | bytes 23592964
  121.4 21.9 %copy-start.13 = (s32[1,640]{1,0:T(1,128)S(1)}, s32[1,640]{1,0:T(1,128)}, u32[]{:S(2)}) copy-start(s32[1,640]{1,0:T(1,128)} %param.8) | copy-start | bytes 7684
  142.0 27.3 %collective-permute-start.23 = (bf16[8,3,80,384]{3,2,1,0:T(8,128)(2,1)}, bf16[8,3,80,384]{3,2,1,0:T(8,128)(2,1)}, u32[]{:S(2)}, u32[]{:S(2)}) collective-permute-start(bf16[8,3,80,384]{3,2,1,0:T(8,128)(2,1)} %collective-permute-done.21.refs_2_), channel_id=1, source_target_pairs={{0,4},{4,0},{8,12},{12,8},{16,20},{20,16},{24,28},{28,24},{32,36},... | collective-permute-start | bytes 4423688 | tf_op jit(solution)/shard_map/ppermute | solution.py:53
  143.2 26.1 %collective-permute-start.25 = (bf16[8,3,80,384]{3,2,1,0:T(8,128)(2,1)}, bf16[8,3,80,384]{3,2,1,0:T(8,128)(2,1)}, u32[]{:S(2)}, u32[]{:S(2)}) collective-permute-start(bf16[8,3,80,384]{3,2,1,0:T(8,128)(2,1)} %collective-permute-done.22.refs_6_), channel_id=1, source_target_pairs={{0,4},{4,0},{8,12},{12,8},{16,20},{20,16},{24,28},{28,24},{32,36},... | collective-permute-start | bytes 4423688 | tf_op jit(solution)/shard_map/ppermute | solution.py:53
  156.1 12.1 %copy-start.14 = (s32[3]{0:T(128)S(1)}, s32[3]{0:T(128)}, u32[]{:S(2)}) copy-start(s32[3]{0:T(128)} %param.9) | copy-start | bytes 40
  156.1 38.9 %all-to-all-start = ((bf16[64,61,128]{2,1,0:T(8,128)(2,1)}), bf16[64,61,128]{2,1,0:T(8,128)(2,1)S(1)}, u32[]{:S(2)}, u32[]{:S(2)}) async-start(bf16[64,61,128]{2,1,0:T(8,128)(2,1)} %copy.53), calls=%async_computation | async-start | bytes 2097152 | tf_op jit(solution)/shard_map/all_to_all | solution.py:418
  195.7 13.6 %copy-start.12 = (pred[640,640]{0,1:T(8,128)(4,1)S(1)}, pred[640,640]{0,1:T(8,128)(4,1)}, u32[]{:S(2)}) copy-start(pred[640,640]{0,1:T(8,128)(4,1)} %get-tuple-element.49) | copy-start | bytes 1228804
  200.0 24.6 %all-to-all-start.1 = ((bf16[64,20,128]{2,1,0:T(8,128)(2,1)}), bf16[64,20,128]{2,1,0:T(8,128)(2,1)S(1)}, u32[]{:S(2)}, u32[]{:S(2)}) async-start(bf16[64,20,128]{2,1,0:T(8,128)(2,1)} %copy.55), calls=%async_computation.1 | async-start | bytes 786432 | tf_op jit(solution)/shard_map/all_to_all | solution.py:433
  209.3 2.5 %copy-start.11 = (bf16[1,640,384]{1,2,0:T(8,128)(2,1)S(1)}, bf16[1,640,384]{1,2,0:T(8,128)(2,1)}, u32[]{:S(2)}) copy-start(bf16[1,640,384]{1,2,0:T(8,128)(2,1)} %copy.46) | copy-start | bytes 1474564
